TPU v7x, 128 devices: a whole 4x4x4 slice. The times are simulated.
128 devices in a mesh: dev: 16 (over y, x_hi, core), ta: 8 (over x_lo, z).
Axes of the slice: x: 4 (x_hi: 2, x_lo: 2; x = x_hi * 2 + x_lo), y: 4, z: 4, core: 2. Of those that a mesh axis runs over, the one named last changes fastest.
Arguments:
- tokens: bfloat16 [8, 32, 144, 384], P('ta', 'dev'), may hold values from -36 to 36
- out_grad: bfloat16 [8, 32, 144, 384], P('ta', 'dev'), may hold values from -6 to 6
- first_gain: float32 [384], replicated, may hold values from 0.25 to 1.75
- depth_qkv: bfloat16 [384, 1152], replicated, may hold values from -0.3125 to 0.3125
- depth_out: bfloat16 [384, 384], replicated, may hold values from -0.3125 to 0.3125
- time_qkv: bfloat16 [384, 1152], replicated, may hold values from -0.3125 to 0.3125
- time_out: bfloat16 [384, 384], replicated, may hold values from -0.3125 to 0.3125
- second_gain: float32 [384], replicated, may hold values from 0.25 to 1.75
- up_weight: bfloat16 [384, 1536], replicated, may hold values from -0.3125 to 0.3125
- spatial_kernel: float32 [3, 3, 3, 1536], replicated, may hold values from -1.25 to 1.25
- down_weight: bfloat16 [1536, 384], replicated, may hold values from -0.15625 to 0.15625
- depth_scale: float32 [6], replicated, may hold values from 2 to 10
- time_scale: float32 [6], replicated, may hold values from 2 to 10
Outputs:
- block_out: bfloat16 [8, 32, 144, 384], P('ta', 'dev')
- input_grad: bfloat16 [8, 32, 144, 384], P('ta', 'dev')
- depth_qkv_grad: float32 [384, 1152], replicated
- depth_out_grad: float32 [384, 384], replicated
- time_qkv_grad: float32 [384, 1152], replicated
- time_out_grad: float32 [384, 384], replicated
- up_grad: float32 [384, 1536], replicated
- kernel_grad: float32 [3, 3, 3, 1536], replicated
- down_grad: float32 [1536, 384], replicated
- first_gain_grad: float32 [384], replicated
- second_gain_grad: float32 [384], replicated
- depth_scale_grad: float32 [6], replicated
- time_scale_grad: float32 [6], replicated
All inputs are finite; a program needn't handle non-finite values.
Results may differ from a plain program's by a relative error of at most 0.015.
Values may be sent and summed in bfloat16 or wider, within the bound.
No kernel may reach another device: no remote copies, remote signals or barrier semaphores. Data moves between devices by JAX's collectives and lax.ppermute only.
A program may use at most 128 MiB of HBM per device.

v0:
```python
import functools
import math

import jax
import jax.numpy as jnp
import numpy as np
from jax import lax
from jax.experimental import pallas as pl
from jax.experimental.pallas import tpu as pltpu
from jax.sharding import Mesh
from jax.sharding import PartitionSpec as P

C = 384
HID = 1536
PW = 24
CELLS = 144
ROWS = 288
BLOCK = 256
STEPS = HID // BLOCK
PAD = 192
DEV = ("y", "xh", "core")
TA = ("xl", "z")
CHIPS = ("y", "xh", "xl", "z")
COPIES = 64
CHUNK = 152
F32 = jnp.float32
BF16 = jnp.bfloat16
EPS = 1e-5


def spread_depth():
    table = np.zeros((16, 24, ROWS), np.float32)
    for owner in range(16):
        for k in range(18):
            table[owner, k, (k // 9) * CELLS + 9 * owner + k % 9] = 1
    return table.reshape(384, ROWS)


def spread_time():
    table = np.zeros((8, 40, ROWS), np.float32)
    for owner in range(8):
        for k in range(36):
            table[owner, k, (k // 18) * CELLS + 18 * owner + k % 18] = 1
    return table.reshape(320, ROWS)


def groups_depth():
    k = np.arange(384) % 24
    return np.where(k < 18, k % 9, k - 9).astype(np.int32)


def groups_time():
    return (np.arange(320) % 40).astype(np.int32)


def dot(left, right, dims=((1,), (0,)), precision=None):
    return lax.dot_general(
        left, right, (dims, ((), ())), preferred_element_type=F32, precision=precision
    )


def norm_parts(values):
    centered = values - jnp.mean(values, axis=-1, keepdims=True)
    inverse = lax.rsqrt(jnp.mean(centered * centered, axis=-1, keepdims=True) + EPS)
    return centered * inverse, inverse


def norm_back(scaled, inverse, grads):
    mean = jnp.mean(grads, axis=-1, keepdims=True)
    along = jnp.mean(grads * scaled, axis=-1, keepdims=True)
    return (grads - mean - scaled * along) * inverse


def vmem(count):
    return [pl.BlockSpec(memory_space=pltpu.VMEM)] * count


def shape(dims, kind=BF16):
    return jax.ShapeDtypeStruct(dims, kind)


def first_kernel(tok_ref, gain_ref, pd_ref, pt_ref, dep_ref, tim_ref):
    scaled, _ = norm_parts(tok_ref[...].astype(F32))
    normed = (scaled * gain_ref[...]).astype(BF16)
    dep_ref[...] = dot(pd_ref[...], normed).reshape(16, 24, C).astype(BF16)
    tim_ref[...] = dot(pt_ref[...], normed).reshape(8, 40, C).astype(BF16)


def first_norm(tokens, gain, pd, pt):
    return pl.pallas_call(
        first_kernel,
        out_shape=(shape((16, 24, C)), shape((8, 40, C))),
        in_specs=vmem(4),
        out_specs=tuple(vmem(2)),
        name="first_norm",
    )(tokens, gain, pd, pt)


def lane_is_low():
    return lax.broadcasted_iota(jnp.int32, (1, 128), 1) < 64


def head_ones():
    row = lax.broadcasted_iota(jnp.int32, (128, 128), 0) < 64
    col = lax.broadcasted_iota(jnp.int32, (128, 128), 1) < 64
    return jnp.where(row == col, 1.0, 0.0).astype(BF16)


def head_sum(values, ones):
    high = values.astype(BF16)
    low = (values - high.astype(F32)).astype(BF16)
    return dot(high, ones) + dot(low, ones)


def attend_kernel(in_ref, w_ref, wo_ref, scale_ref, gr_ref, gc_ref, out_ref, fields_ref, mixed_ref, same_ref):
    count, part, _ = in_ref.shape
    rows = count * part
    rowed = in_ref[...].astype(F32).reshape(rows, C).astype(BF16)
    fields_ref[...] = dot(rowed, w_ref[...]).astype(BF16)
    same_ref[...] = jnp.where(gr_ref[...] == gc_ref[...], 1.0, 0.0)
    ones = head_ones()
    low = lane_is_low()
    side = jnp.ones((rows, 128), BF16)
    for pair in range(3):
        at = 128 * pair
        query = fields_ref[:, at : at + 128].astype(F32)
        keyed = fields_ref[:, C + at : C + at + 128].astype(F32)
        valued = fields_ref[:, 2 * C + at : 2 * C + at + 128]
        query = query * lax.rsqrt(head_sum(query * query, ones) + 1e-6)
        keyed = (keyed * lax.rsqrt(head_sum(keyed * keyed, ones) + 1e-6)).astype(BF16)
        query = query * jnp.where(low, scale_ref[2 * pair], scale_ref[2 * pair + 1])
        both = jnp.concatenate([valued, side], axis=1)
        results = []
        for half in range(2):
            mine = low if half == 0 else jnp.logical_not(low)
            scores = dot(jnp.where(mine, query, 0.0).astype(BF16), keyed, ((1,), (1,)))
            weights = (jnp.exp(scores) * same_ref[...]).astype(BF16)
            sums = dot(weights, both)
            results.append(sums[:, :128] / sums[:, 128:])
        mixed_ref[:, at : at + 128] = jnp.where(low, results[0], results[1]).astype(BF16)
    out_ref[...] = dot(mixed_ref[...], wo_ref[...]).reshape(count, part, C).astype(BF16)


def attend(inputs, weight, out_weight, scale, groups, name):
    count, part, _ = inputs.shape
    rows = count * part
    return pl.pallas_call(
        attend_kernel,
        out_shape=(shape((count, part, C)), shape((rows, 3 * C)), shape((rows, C))),
        in_specs=vmem(3) + [pl.BlockSpec(memory_space=pltpu.SMEM)] + vmem(2),
        out_specs=tuple(vmem(3)),
        scratch_shapes=[pltpu.VMEM((rows, rows), F32)],
        name=name,
    )(inputs, weight, out_weight, scale, groups[:, None], groups[None, :])


def attend_back_kernel(
    grad_ref, in_ref, fields_ref, mixed_ref, w_ref, wo_ref, scale_ref, gr_ref, gc_ref, gain_ref,
    out_ref, weights_ref, small_ref, same_ref, fg_ref,
):
    count, part, _ = in_ref.shape
    rows = count * part
    grads = grad_ref[...].astype(F32).reshape(rows, C).astype(BF16)
    same_ref[...] = jnp.where(gr_ref[...] == gc_ref[...], 1.0, 0.0)
    out_grad = dot(mixed_ref[...], grads, ((0,), (0,)))
    for tile in range(3):
        weights_ref[9 + tile] = out_grad[:, 128 * tile : 128 * tile + 128].astype(BF16)
    mixed_grad = dot(grads, wo_ref[...], ((1,), (1,))).astype(BF16)
    ones = head_ones()
    low = lane_is_low()
    side = jnp.ones((rows, 128), BF16)
    small_ref[24:32, :] = jnp.zeros((8, 128), F32)
    for pair in range(3):
        at = 128 * pair
        query = fields_ref[:, at : at + 128].astype(F32)
        keyed = fields_ref[:, C + at : C + at + 128].astype(F32)
        valued = fields_ref[:, 2 * C + at : 2 * C + at + 128]
        query_inv = lax.rsqrt(head_sum(query * query, ones) + 1e-6)
        keyed_inv = lax.rsqrt(head_sum(keyed * keyed, ones) + 1e-6)
        query = query * query_inv
        keyed = keyed * keyed_inv
        scale = jnp.where(low, scale_ref[2 * pair], scale_ref[2 * pair + 1])
        scaled = query * scale
        keyed_short = keyed.astype(BF16)
        cot = mixed_grad[:, at : at + 128]
        delta = head_sum(cot.astype(F32) * mixed_ref[:, at : at + 128].astype(F32), ones)
        query_grad = jnp.zeros((rows, 128), F32)
        keyed_grad = jnp.zeros((rows, 128), F32)
        value_grad = jnp.zeros((rows, 128), F32)
        for half in range(2):
            mine = low if half == 0 else jnp.logical_not(low)
            lane = 64 * half
            mine_query = jnp.where(mine, scaled, 0.0).astype(BF16)
            mine_cot = jnp.where(mine, cot.astype(F32), 0.0).astype(BF16)
            mine_keyed = jnp.where(mine, keyed, 0.0).astype(BF16)
            scores = dot(mine_query, keyed_short, ((1,), (1,)))
            weights = jnp.exp(scores) * same_ref[...]
            total = dot(weights.astype(BF16), side)
            weights = weights * (1.0 / total)[:, :1]
            weights_grad = dot(mine_cot, valued, ((1,), (1,)))
            scores_grad = (weights * (weights_grad - delta[:, lane : lane + 1])).astype(BF16)
            value_grad = value_grad + dot(weights.astype(BF16), mine_cot, ((0,), (0,)))
            query_grad = query_grad + dot(scores_grad, mine_keyed)
            keyed_grad = keyed_grad + dot(scores_grad, mine_query, ((0,), (0,)))
        along = jnp.sum(query_grad * query, axis=0, keepdims=True)
        small_ref[24 + pair : 25 + pair, :] = head_sum(jnp.broadcast_to(along, (8, 128)), ones)[:1]
        query_grad = query_grad * scale
        query_grad = (query_grad - query * head_sum(query * query_grad, ones)) * query_inv
        keyed_grad = (keyed_grad - keyed * head_sum(keyed * keyed_grad, ones)) * keyed_inv
        fg_ref[:, at : at + 128] = query_grad.astype(BF16)
        fg_ref[:, C + at : C + at + 128] = keyed_grad.astype(BF16)
        fg_ref[:, 2 * C + at : 2 * C + at + 128] = value_grad.astype(BF16)
    out_ref[...] = dot(fg_ref[...], w_ref[...], ((1,), (1,))).reshape(count, part, C).astype(BF16)
    rowed = in_ref[...].astype(F32).reshape(rows, C).astype(BF16)
    grad = dot(rowed, fg_ref[...], ((0,), (0,)))
    product = jnp.zeros((C, 128), F32)
    for tile in range(9):
        at = 128 * tile
        weights_ref[tile] = grad[:, at : at + 128].astype(BF16)
        product = product + grad[:, at : at + 128] * w_ref[:, at : at + 128].astype(F32)
    gain_part = dot(jnp.ones((8, 128), F32), product, ((1,), (1,)), lax.Precision.HIGHEST)
    gain_part = gain_part / gain_ref[...]
    for tile in range(3):
        small_ref[8 * tile : 8 * tile + 8, :] = gain_part[:, 128 * tile : 128 * tile + 128]


def attend_back(grads, inputs, fields, mixed, weight, out_weight, scale, groups, gain, name):
    count, part, _ = inputs.shape
    rows = count * part
    return pl.pallas_call(
        attend_back_kernel,
        out_shape=(shape((count, part, C)), shape((12, C, 128)), shape((32, 128), F32)),
        in_specs=vmem(6) + [pl.BlockSpec(memory_space=pltpu.SMEM)] + vmem(3),
        out_specs=tuple(vmem(3)),
        scratch_shapes=[pltpu.VMEM((rows, rows), F32), pltpu.VMEM((rows, 3 * C), BF16)],
        name=name,
    )(grads, inputs, fields, mixed, weight, out_weight, scale, groups[:, None], groups[None, :], gain)


def middle_kernel(tok_ref, dep_ref, tim_ref, pd_ref, pt_ref, out_ref):
    dep = dep_ref[...].astype(F32).reshape(384, C).astype(BF16)
    tim = tim_ref[...].astype(F32).reshape(320, C).astype(BF16)
    total = tok_ref[...].astype(F32) + dot(pd_ref[...], dep, ((0,), (0,)))
    out_ref[...] = (total + dot(pt_ref[...], tim, ((0,), (0,)))).astype(BF16)


def middle_of(tokens, depth, time, pd, pt):
    return pl.pallas_call(
        middle_kernel,
        out_shape=shape((ROWS, C)),
        in_specs=vmem(5),
        out_specs=vmem(1)[0],
        name="middle",
    )(tokens, depth, time, pd, pt)


def down_one(values, first):
    return jnp.where(first, 0.0, pltpu.roll(values, 1, 0))


def up_one(values, last):
    return jnp.where(last, 0.0, pltpu.roll(values, PW - 1, 0))


def act_pair(values):
    square = values * values
    inner = 0.7978845608 * values * (1.0 + 0.044715 * square)
    tanh = jnp.tanh(inner)
    half = 0.5 * (1.0 + tanh)
    slope = 0.7978845608 * (1.0 + 3.0 * 0.044715 * square)
    return values * half, half + 0.5 * values * (1.0 - tanh * tanh) * slope


def feed_kernel(
    low_ref, mid_ref, high_ref, og_low_ref, og_ref, og_high_ref, gain_ref, up_ref, kern_ref, down_ref,
    pd_ref, pt_ref,
    block_ref, mgrad_ref, bdep_ref, btim_ref, weights_ref, kgrad_ref, small_ref,
    norm_ref, og4_ref, hid_ref, fgr_ref, act_ref, hgr_ref, ag_ref, block_acc, back_acc, prod_acc,
):
    step = pl.program_id(0)

    @pl.when(step == 0)
    def _():
        for at, ref in ((0, low_ref), (ROWS, mid_ref), (2 * ROWS, high_ref)):
            scaled, _ = norm_parts(ref[...].astype(F32))
            norm_ref[at : at + ROWS, :] = (scaled * gain_ref[...]).astype(BF16)
        og4_ref[0:CELLS, :] = og_low_ref[...]
        og4_ref[CELLS : CELLS + ROWS, :] = og_ref[...]
        og4_ref[CELLS + ROWS : 2 * ROWS, :] = og_high_ref[...]
        hid_ref[...] = jnp.zeros(hid_ref.shape, F32)
        fgr_ref[...] = jnp.zeros(fgr_ref.shape, F32)
        block_acc[...] = jnp.zeros(block_acc.shape, F32)
        back_acc[...] = jnp.zeros(back_acc.shape, F32)
        prod_acc[...] = jnp.zeros(prod_acc.shape, F32)

    place = lax.broadcasted_iota(jnp.int32, (PW, 128), 0)
    first, last = place == 0, place == PW - 1
    hidden = dot(norm_ref[...], up_ref[...]).astype(BF16).astype(F32)
    ag_ref[...] = dot(og4_ref[...], down_ref[...], ((1,), (1,)))
    for lt in range(2):
        for piece in range(6):
            hid_ref[lt, piece * PAD + PW : piece * PAD + PW + CELLS, :] = hidden[
                piece * CELLS : (piece + 1) * CELLS, 128 * lt : 128 * lt + 128
            ]

    for lt in range(2):
        lanes = slice(128 * lt, 128 * lt + 128)

        def forward(piece, _, lt=lt, lanes=lanes):
            for i in range(6):
                acc = [None] * 3
                for a in range(3):
                    for b in range(3):
                        start = pl.multiple_of((piece + a) * PAD + PW * (i + b), 8)
                        window = hid_ref[lt, pl.ds(start, PW), :]
                        for e in range(3):
                            k = 9 * a + 3 * b + e
                            term = kern_ref[k : k + 1, lanes] * window
                            acc[e] = term if acc[e] is None else acc[e] + term
                filtered = acc[1] + down_one(acc[0], first) + up_one(acc[2], last)
                value, slope = act_pair(filtered)
                at = pl.multiple_of(piece * CELLS + PW * i, 8)
                grad = (ag_ref[pl.ds(at, PW), lanes] * slope).astype(BF16).astype(F32)
                fgr_ref[lt, pl.ds(pl.multiple_of(piece * PAD + PW * (i + 1), 8), PW), :] = grad
                act_ref[pl.ds(at, PW), lanes] = value
            return 0

        lax.fori_loop(0, 4, forward, 0)

        def backward(piece, sums, lt=lt, lanes=lanes):
            sums = list(sums)
            for i in range(6):
                acc = [None] * 3
                for a in range(3):
                    for b in range(3):
                        start = pl.multiple_of((piece + 2 - a) * PAD + PW * (i + 2 - b), 8)
                        window = fgr_ref[lt, pl.ds(start, PW), :]
                        for e in range(3):
                            k = 9 * a + 3 * b + e
                            term = kern_ref[k : k + 1, lanes] * window
                            acc[e] = term if acc[e] is None else acc[e] + term
                total = acc[1] + up_one(acc[0], last) + down_one(acc[2], first)
                hgr_ref[pl.ds(pl.multiple_of(piece * CELLS + PW * i, 8), PW), lanes] = total
            return tuple(sums)

        lax.fori_loop(0, 2, backward, ())

        for a in range(3):

            def products(piece, sums, a=a, lt=lt):
                sums = list(sums)
                for i in range(6):
                    own = pl.multiple_of((piece + 1) * PAD + PW * (i + 1), 8)
                    grad = fgr_ref[lt, pl.ds(own, PW), :]
                    shifted = (up_one(grad, last), grad, down_one(grad, first))
                    for b in range(3):
                        start = pl.multiple_of((piece + 1 + a) * PAD + PW * (i + b), 8)
                        window = hid_ref[lt, pl.ds(start, PW), :]
                        for e in range(3):
                            term = window * shifted[e]
                            k = 3 * b + e
                            sums[k] = sums[k] + (term[0:8] + term[8:16] + term[16:24])
                return tuple(sums)

            sums = lax.fori_loop(0, 2, products, tuple(jnp.zeros((8, 128), F32) for _ in range(9)))
            for k in range(9):
                row = 32 * lt + 9 * a + k
                kgrad_ref[0, row : row + 1, :] = jnp.sum(sums[k], axis=0, keepdims=True)
        kgrad_ref[0, 32 * lt + 27 : 32 * lt + 32, :] = jnp.zeros((5, 128), F32)

    active = act_ref[CELLS : CELLS + ROWS, :].astype(BF16)
    block_acc[...] += dot(active, down_ref[...])
    down_grad = dot(active, og_ref[...], ((0,), (0,)))
    hidden_grad = hgr_ref[...].astype(BF16)
    up_grad = dot(norm_ref[ROWS : 2 * ROWS, :], hidden_grad, ((0,), (0,)))
    back_acc[...] += dot(hidden_grad, up_ref[...], ((1,), (1,)))
    product = up_grad * up_ref[...].astype(F32)
    prod_acc[...] += product[:, :128] + product[:, 128:]
    for tile in range(2):
        weights_ref[0, C * tile : C * tile + C, :] = up_grad[:, 128 * tile : 128 * tile + 128].astype(BF16)
    for tile in range(3):
        at = 2 * C + BLOCK * tile
        weights_ref[0, at : at + BLOCK, :] = down_grad[:, 128 * tile : 128 * tile + 128].astype(BF16)

    @pl.when(step == STEPS - 1)
    def _():
        wide = mid_ref[...].astype(F32)
        block_ref[...] = (wide + block_acc[...]).astype(BF16)
        scaled, inverse = norm_parts(wide)
        back = norm_back(scaled, inverse, back_acc[...] * gain_ref[...])
        middle_grad = og_ref[...].astype(F32) + back
        mgrad_ref[...] = middle_grad
        short = middle_grad.astype(BF16)
        bdep_ref[...] = dot(pd_ref[...], short).reshape(16, 24, C).astype(BF16)
        btim_ref[...] = dot(pt_ref[...], short).reshape(8, 40, C).astype(BF16)
        part = dot(jnp.ones((8, 128), F32), prod_acc[...], ((1,), (1,)), lax.Precision.HIGHEST)
        part = part / gain_ref[...]
        for tile in range(3):
            small_ref[8 * tile : 8 * tile + 8, :] = part[:, 128 * tile : 128 * tile + 128]
        small_ref[24:32, :] = jnp.zeros((8, 128), F32)


def feed_forward(low, mid, high, og_low, og, og_high, gain, up, kern, down, pd, pt):
    def whole(*dims):
        return pl.BlockSpec(dims, lambda s: (0,) * len(dims))

    return pl.pallas_call(
        feed_kernel,
        grid=(STEPS,),
        out_shape=(
            shape((ROWS, C)),
            shape((ROWS, C), F32),
            shape((16, 24, C)),
            shape((8, 40, C)),
            shape((STEPS, 1536, 128)),
            shape((STEPS, 64, 128), F32),
            shape((32, 128), F32),
        ),
        in_specs=[
            whole(ROWS, C),
            whole(ROWS, C),
            whole(ROWS, C),
            whole(CELLS, C),
            whole(ROWS, C),
            whole(CELLS, C),
            whole(1, C),
            pl.BlockSpec((C, BLOCK), lambda s: (0, s)),
            pl.BlockSpec((27, BLOCK), lambda s: (0, s)),
            pl.BlockSpec((BLOCK, C), lambda s: (s, 0)),
            whole(384, ROWS),
            whole(320, ROWS),
        ],
        out_specs=(
            whole(ROWS, C),
            whole(ROWS, C),
            whole(16, 24, C),
            whole(8, 40, C),
            pl.BlockSpec((1, 1536, 128), lambda s: (s, 0, 0)),
            pl.BlockSpec((1, 64, 128), lambda s: (s, 0, 0)),
            whole(32, 128),
        ),
        scratch_shapes=[
            pltpu.VMEM((3 * ROWS, C), BF16),
            pltpu.VMEM((2 * ROWS, C), BF16),
            pltpu.VMEM((2, 6 * PAD, 128), F32),
            pltpu.VMEM((2, 4 * PAD, 128), F32),
            pltpu.VMEM((2 * ROWS, BLOCK), F32),
            pltpu.VMEM((ROWS, BLOCK), F32),
            pltpu.VMEM((2 * ROWS, BLOCK), F32),
            pltpu.VMEM((ROWS, C), F32),
            pltpu.VMEM((ROWS, C), F32),
            pltpu.VMEM((C, 128), F32),
        ],
        name="feed_forward",
    )(low, mid, high, og_low, og, og_high, gain, up, kern, down, pd, pt)


def last_kernel(tok_ref, dep_ref, tim_ref, pd_ref, pt_ref, gain_ref, mgrad_ref, out_ref):
    dep = dep_ref[...].astype(F32).reshape(384, C).astype(BF16)
    tim = tim_ref[...].astype(F32).reshape(320, C).astype(BF16)
    back = dot(pd_ref[...], dep, ((0,), (0,))) + dot(pt_ref[...], tim, ((0,), (0,)))
    scaled, inverse = norm_parts(tok_ref[...].astype(F32))
    out_ref[...] = (mgrad_ref[...] + norm_back(scaled, inverse, back * gain_ref[...])).astype(BF16)


def last_norm(tokens, depth, time, pd, pt, gain, mgrad):
    return pl.pallas_call(
        last_kernel,
        out_shape=shape((ROWS, C)),
        in_specs=vmem(7),
        out_specs=vmem(1)[0],
        name="last_norm",
    )(tokens, depth, time, pd, pt, gain, mgrad)


FFN = 4608
ATT = 2304
TOTAL = COPIES * CHUNK


def pair_kernel(core_ref, f0, f1, d0, d1, t0, t1, k0, k1, s0, s1, out_ref):
    at = 0
    for one, two in ((f0, f1), (d0, d1), (t0, t1), (k0, k1)):
        size = one.shape[1]
        out_ref[at : at + size, :] = (one[0].astype(F32) + two[...].astype(F32)).astype(BF16)
        at += size
    size = s0.shape[0]
    out_ref[at : at + size, :] = (s0[...] + s1[...].astype(F32)).astype(BF16)
    out_ref[at + size :, :] = jnp.zeros((TOTAL - at - size, 128), BF16)


def pair_sum(core, pairs):
    specs, args = [], []
    for mine, theirs in pairs[:-1]:
        rows = mine.shape[1]
        specs.append(pl.BlockSpec((1, rows, 128), lambda i, c: (c[0], 0, 0)))
        specs.append(pl.BlockSpec((rows, 128), lambda i, c: (0, 0)))
        args += [mine, theirs]
    for array in pairs[-1]:
        specs.append(pl.BlockSpec(array.shape, lambda i, c: (0, 0)))
        args.append(array)
    return pl.pallas_call(
        pair_kernel,
        out_shape=shape((TOTAL, 128)),
        grid_spec=pltpu.PrefetchScalarGridSpec(
            num_scalar_prefetch=1,
            grid=(1,),
            in_specs=specs,
            out_specs=pl.BlockSpec((TOTAL, 128), lambda i, c: (0, 0)),
        ),
        name="pair_sum",
    )(core, *args)


def chip_kernel(factor, in_ref, out_ref):
    total = in_ref[0].astype(F32)
    for source in range(1, COPIES):
        total = total + in_ref[source].astype(F32)
    total = (total * factor).astype(BF16)
    for target in range(COPIES):
        out_ref[target] = total


def chip_sum(received, factor):
    return pl.pallas_call(
        functools.partial(chip_kernel, factor),
        out_shape=shape((COPIES, CHUNK, 128)),
        in_specs=vmem(1),
        out_specs=vmem(1)[0],
        name="chip_sum",
    )(received)


def unpack_kernel(core_ref, own_ref, other_ref, dq_ref, do_ref, tq_ref, to_ref, up_ref, kg_ref, dn_ref, small_ref):
    zero = core_ref[0] == 0

    def part(half, at, rows):
        own = own_ref[at : at + rows, :].astype(F32)
        other = other_ref[at : at + rows, :].astype(F32)
        return jnp.where(zero, own, other) if half == 0 else jnp.where(zero, other, own)

    for step in range(STEPS):
        half, at = step // 3, 1536 * (step % 3)
        for tile in range(2):
            lanes = slice(BLOCK * step + 128 * tile, BLOCK * step + 128 * tile + 128)
            up_ref[:, lanes] = part(half, at + C * tile, C)
            kg_ref[:, lanes] = part(half, FFN + 2 * ATT + 64 * (step % 3) + 32 * tile, 32)[:27]
        for tile in range(3):
            lanes = slice(128 * tile, 128 * tile + 128)
            dn_ref[BLOCK * step : BLOCK * step + BLOCK, lanes] = part(half, at + 2 * C + BLOCK * tile, BLOCK)
    for base, q_ref, o_ref in ((FFN, dq_ref, do_ref), (FFN + ATT, tq_ref, to_ref)):
        for tile in range(12):
            half, at = tile // 6, base + C * (tile % 6)
            if tile < 9:
                q_ref[:, 128 * tile : 128 * tile + 128] = part(half, at, C)
            else:
                o_ref[:, 128 * (tile - 9) : 128 * (tile - 9) + 128] = part(half, at, C)
    small_ref[...] = part(0, FFN + 2 * ATT + 192, 96)


def unpack(core, own, other):
    return pl.pallas_call(
        unpack_kernel,
        out_shape=(
            shape((C, 3 * C), F32),
            shape((C, C), F32),
            shape((C, 3 * C), F32),
            shape((C, C), F32),
            shape((C, HID), F32),
            shape((27, HID), F32),
            shape((HID, C), F32),
            shape((96, 128), F32),
        ),
        in_specs=[pl.BlockSpec(memory_space=pltpu.SMEM)] + vmem(2),
        out_specs=tuple(vmem(8)),
        name="unpack",
    )(core, own, other)


def local(
    tokens, out_grad, first_gain, depth_qkv, depth_out, time_qkv, time_out, second_gain, up_weight,
    spatial_kernel, down_weight, depth_scale, time_scale,
):
    pd = jnp.asarray(spread_depth(), BF16)
    pt = jnp.asarray(spread_time(), BF16)
    gd = jnp.asarray(groups_depth())
    gt = jnp.asarray(groups_time())
    core_index = lax.axis_index("core").astype(jnp.int32)
    core = core_index.reshape(1)
    block_shape = tokens.shape
    flat = tokens.reshape(ROWS, C)
    og = out_grad.reshape(ROWS, C)
    gain_one = first_gain.reshape(1, C)
    gain_two = second_gain.reshape(1, C)
    count = lax.axis_size(DEV)
    ahead = [(i, i + 1) for i in range(count - 1)]
    behind = [(i + 1, i) for i in range(count - 1)]
    swap = [(0, 1), (1, 0)]

    def exchange(values, axes):
        return lax.all_to_all(values, axes, split_axis=0, concat_axis=0, tiled=True)

    dep, tim = first_norm(flat, gain_one, pd, pt)
    dep = exchange(dep, DEV)
    tim = exchange(tim, TA)
    og_low = lax.ppermute(og[CELLS:], DEV, ahead)
    og_high = lax.ppermute(og[:CELLS], DEV, behind)
    dep_out, dep_fields, dep_mixed = attend(dep, depth_qkv, depth_out, depth_scale, gd, "depth_attend")
    dep_back = exchange(dep_out, DEV)
    tim_out, tim_fields, tim_mixed = attend(tim, time_qkv, time_out, time_scale, gt, "time_attend")
    tim_back = exchange(tim_out, TA)
    mid = middle_of(flat, dep_back, tim_back, pd, pt)
    low = lax.ppermute(mid, DEV, ahead)
    high = lax.ppermute(mid, DEV, behind)
    block_out, mgrad, bdep, btim, ffn_g, kern_g, small_g = feed_forward(
        low, mid, high, og_low, og, og_high, gain_two, up_weight, spatial_kernel.reshape(27, HID),
        down_weight, pd, pt,
    )
    bdep = exchange(bdep, DEV)
    btim = exchange(btim, TA)
    dep_first, dep_g, dep_small = attend_back(
        bdep, dep, dep_fields, dep_mixed, depth_qkv, depth_out, depth_scale, gd, gain_one, "depth_back"
    )
    dep_first = exchange(dep_first, DEV)
    tim_first, tim_g, tim_small = attend_back(
        btim, tim, tim_fields, tim_mixed, time_qkv, time_out, time_scale, gt, gain_one, "time_back"
    )
    tim_first = exchange(tim_first, TA)
    input_grad = last_norm(flat, dep_first, tim_first, pd, pt, gain_one, mgrad)

    def swapped(halves):
        return lax.ppermute(lax.dynamic_index_in_dim(halves, 1 - core_index, 0, keepdims=False), "core", swap)

    halves = [
        ffn_g.reshape(2, FFN, 128),
        dep_g.reshape(2, ATT, 128),
        tim_g.reshape(2, ATT, 128),
        kern_g.reshape(2, 192, 128),
    ]
    pairs = [(half, swapped(half)) for half in halves]
    small = jnp.concatenate([small_g, dep_small, tim_small], axis=0)
    pairs.append((small, lax.ppermute(small, "core", swap)))
    stack = pair_sum(core, pairs)
    received = exchange(stack.reshape(COPIES, CHUNK, 128), CHIPS)
    factor = 1.0 / math.sqrt(ROWS * count * lax.axis_size(TA))
    own = exchange(chip_sum(received, factor), CHIPS).reshape(TOTAL, 128)
    other = lax.ppermute(own, "core", swap)
    dq, do, tq, to, up_g, kern_sum, down_g, small = unpack(core, own, other)
    small = small.reshape(12, 8, 128)
    second_gain_grad = small[0:3, 0].reshape(C)
    first_gain_grad = (small[4:7, 0] + small[8:11, 0]).reshape(C)
    depth_scale_grad = small[7, 0:3, ::64].reshape(6)
    time_scale_grad = small[11, 0:3, ::64].reshape(6)
    return (
        block_out.reshape(block_shape),
        input_grad.reshape(block_shape),
        dq,
        do,
        tq,
        to,
        up_g,
        kern_sum.reshape(3, 3, 3, HID),
        down_g,
        first_gain_grad,
        second_gain_grad,
        depth_scale_grad,
        time_scale_grad,
    )


def solution(mesh):
    fine = Mesh(mesh.devices.reshape(4, 2, 2, 2, 4), ("y", "xh", "core", "xl", "z"))
    split = P(TA, DEV, None, None)
    return jax.shard_map(
        local,
        mesh=fine,
        in_specs=(split, split) + (P(),) * 11,
        out_specs=(split, split) + (P(),) * 11,
        check_vma=False,
    )
```

profile of v0, /device:TPU:1, one launch (start us, length us, event | category | flops | bytes accessed | tf_op | source)
XLA Modules:
  0.0 284.1 jit_solution(14682502702145871773)
XLA Ops:
  1.9 2.5 first_norm.1
  4.4 12.9 %all_to_all.50.in_ref = bf16[8,40,384]{2,1,0:T(8,128)(2,1)} all-to-all(bf16[8,40,384]{2,1,0:T(8,128)(2,1)} %get-tuple-element.44), channel_id=1, replica_groups=mesh['y'=4,'xh'=2,'core'=2,'xl'=2,'z'=4] {'xl','z'}, dimensions={0} | all-to-all | bytes 491520 | tf_op jit(solution)/shard_map/all_to_all | solution.py:601
  17.3 8.7 %all-to-all-start = ((bf16[16,24,384]{2,1,0:T(8,128)(2,1)}), bf16[16,24,384]{2,1,0:T(8,128)(2,1)S(1)}, u32[]{:S(2)}, u32[]{:S(2)}) async-start(bf16[16,24,384]{2,1,0:T(8,128)(2,1)} %get-tuple-element.42), calls=%async_computation | async-start | bytes 589824 | tf_op jit(solution)/shard_map/all_to_all | solution.py:601
  26.1 4.7 %time_attend.1 = (bf16[8,40,384]{2,1,0:T(8,128)(2,1)}, bf16[320,1152]{1,0:T(8,128)(2,1)}, bf16[320,384]{1,0:T(8,128)(2,1)}) custom-call(bf16[8,40,384]{2,1,0:T(8,128)(2,1)} %all_to_all.50.in_ref, bf16[384,1152]{1,0:T(8,128)(2,1)} %w_ref.7, bf16[384,384]{1,0:T(8,128)(2,1)} %wo_ref.7, f32[6]{0:T(128)} %scale_ref.7, s32[320,1]{1,0:T(8,128)} %constant.41.gr_ref, ...), custom_call_target="tpu_custom_call" | custom-call | tf_op jit(solution)/shard_map/time_attend/pallas_call | solution.py:147
  30.8 4.3 %all-to-all-done.in_ref = bf16[16,24,384]{2,1,0:T(8,128)(2,1)S(1)} async-done(((bf16[16,24,384]{2,1,0:T(8,128)(2,1)}), bf16[16,24,384]{2,1,0:T(8,128)(2,1)S(1)}, u32[]{:S(2)}, u32[]{:S(2)}) %all-to-all-start) | async-done | bytes 294944 | tf_op jit(solution)/shard_map/all_to_all | solution.py:601
  35.0 3.4 %all-to-all-start.3 = ((bf16[8,40,384]{2,1,0:T(8,128)(2,1)}), bf16[8,40,384]{2,1,0:T(8,128)(2,1)S(1)}, u32[]{:S(2)}, u32[]{:S(2)}) async-start(bf16[8,40,384]{2,1,0:T(8,128)(2,1)} %get-tuple-element.45), calls=%async_computation.3 | async-start | bytes 491520 | tf_op jit(solution)/shard_map/all_to_all | solution.py:601
  38.5 5.1 %depth_attend.1 = (bf16[16,24,384]{2,1,0:T(8,128)(2,1)}, bf16[384,1152]{1,0:T(8,128)(2,1)}, bf16[384,384]{1,0:T(8,128)(2,1)}) custom-call(bf16[16,24,384]{2,1,0:T(8,128)(2,1)} %copy-done.1, bf16[384,1152]{1,0:T(8,128)(2,1)} %w_ref.6, bf16[384,384]{1,0:T(8,128)(2,1)} %wo_ref.6, f32[6]{0:T(128)} %scale_ref.6, s32[384,1]{1,0:T(8,128)} %constant.39.gr_ref, ...), custom_call_target="tpu_custom_call" | custom-call | tf_op jit(solution)/shard_map/depth_attend/pallas_call | solution.py:147
  44.4 15.2 %all_to_all.51.dep_ref = bf16[16,24,384]{2,1,0:T(8,128)(2,1)} all-to-all(bf16[16,24,384]{2,1,0:T(8,128)(2,1)} %get-tuple-element.43), channel_id=1, replica_groups=mesh['y'=4,'xh'=2,'core'=2,'xl'=2,'z'=4] {'y','xh','core'}, dimensions={0} | all-to-all | bytes 589824 | tf_op jit(solution)/shard_map/all_to_all | solution.py:601
  59.6 2.4 middle.1.mid_ref
  62.0 2.9 %collective-permute-start.1 = (bf16[288,384]{1,0:T(8,128)(2,1)}, bf16[288,384]{1,0:T(8,128)(2,1)S(1)}, u32[]{:S(2)}, u32[]{:S(2)}) collective-permute-start(bf16[288,384]{1,0:T(8,128)(2,1)} %middle.1.mid_ref), channel_id=1, source_target_pairs={{8,0},{16,8},{24,16},{32,24},{40,32},{48,40},{56,48},{64,56},{72,6... | collective-permute-start | bytes 663560 | tf_op jit(solution)/shard_map/ppermute | solution.py:614
  65.0 4.1 %collective-permute-start = (bf16[288,384]{1,0:T(8,128)(2,1)}, bf16[288,384]{1,0:T(8,128)(2,1)S(1)}, u32[]{:S(2)}, u32[]{:S(2)}) collective-permute-start(bf16[288,384]{1,0:T(8,128)(2,1)} %middle.1.mid_ref), channel_id=1, source_target_pairs={{0,8},{8,16},{16,24},{24,32},{32,40},{40,48},{48,56},{56,64},{64,7... | collective-permute-start | bytes 663560 | tf_op jit(solution)/shard_map/ppermute | solution.py:613
  69.1 1.9 collective-permute-start.3
  71.0 5.1 %collective-permute-start.2 = (bf16[144,384]{1,0:T(8,128)(2,1)S(1)}, bf16[144,384]{1,0:T(8,128)(2,1)S(1)}, u32[]{:S(2)}, u32[]{:S(2)}) collective-permute-start(bf16[144,384]{1,0:T(8,128)(2,1)S(1)} %get-tuple-element.74), channel_id=1, source_target_pairs={{0,8},{8,16},{16,24},{24,32},{32,40},{40,48},{48,56},{56,64},{64,7... | collective-permute-start | bytes 331784 | tf_op jit(solution)/shard_map/ppermute | solution.py:606
  78.7 30.9 %feed_forward.1 = (bf16[288,384]{1,0:T(8,128)(2,1)}, f32[288,384]{1,0:T(8,128)}, bf16[16,24,384]{2,1,0:T(8,128)(2,1)}, bf16[8,40,384]{2,1,0:T(8,128)(2,1)}, bf16...) custom-call(bf16[288,384]{1,0:T(8,128)(2,1)} %copy-done.14, bf16[288,384]{1,0:T(8,128)(2,1)} %middle.1.mid_ref, ...), custom_call_target="tpu_custom_call" | custom-call | tf_op jit(solution)/shard_map/feed_forward/pallas_call | solution.py:407
  109.7 3.4 %all-to-all-start.6 = ((bf16[8,40,384]{2,1,0:T(8,128)(2,1)}), bf16[8,40,384]{2,1,0:T(8,128)(2,1)S(1)}, u32[]{:S(2)}, u32[]{:S(2)}) async-start(bf16[8,40,384]{2,1,0:T(8,128)(2,1)} %get-tuple-element.51), calls=%async_computation.6 | async-start | bytes 491520 | tf_op jit(solution)/shard_map/all_to_all | solution.py:601
  113.1 1.4 dynamic-slice_bitcast_fusion
  114.6 4.6 %all-to-all-done.6.grad_ref = bf16[8,40,384]{2,1,0:T(8,128)(2,1)S(1)} async-done(((bf16[8,40,384]{2,1,0:T(8,128)(2,1)}), bf16[8,40,384]{2,1,0:T(8,128)(2,1)S(1)}, u32[]{:S(2)}, u32[]{:S(2)}) %all-to-all-start.6) | async-done | bytes 245792 | tf_op jit(solution)/shard_map/all_to_all | solution.py:601
  119.1 8.5 %all-to-all-start.4 = ((bf16[16,24,384]{2,1,0:T(8,128)(2,1)}), bf16[16,24,384]{2,1,0:T(8,128)(2,1)S(1)}, u32[]{:S(2)}, u32[]{:S(2)}) async-start(bf16[16,24,384]{2,1,0:T(8,128)(2,1)} %get-tuple-element.47), calls=%async_computation.4 | async-start | bytes 589824 | tf_op jit(solution)/shard_map/all_to_all | solution.py:601
  127.7 9.2 %time_back.1 = (bf16[8,40,384]{2,1,0:T(8,128)(2,1)}, bf16[12,384,128]{2,1,0:T(8,128)(2,1)}, f32[32,128]{1,0:T(8,128)}) custom-call(bf16[8,40,384]{2,1,0:T(8,128)(2,1)} %copy-done.4, bf16[8,40,384]{2,1,0:T(8,128)(2,1)} %all_to_all.50.in_ref, bf16[320,1152]{1,0:T(8,128)(2,1)} %get-tuple-element.52.fields_ref, bf16[320,384]{1,0:T(8,128)(2,1)} %get-tuple-element.53.mixed_ref, ...), custom_call_target="tpu_custom_call" | custom-call | tf_op jit(solution)/shard_map/time_back/pallas_call | solution.py:230
  136.9 1.9 dynamic-slice_bitcast_fusion.1
  139.6 9.6 %depth_back.1 = (bf16[16,24,384]{2,1,0:T(8,128)(2,1)}, bf16[12,384,128]{2,1,0:T(8,128)(2,1)}, f32[32,128]{1,0:T(8,128)}) custom-call(bf16[16,24,384]{2,1,0:T(8,128)(2,1)} %copy-done.3, bf16[16,24,384]{2,1,0:T(8,128)(2,1)} %copy-done.1, bf16[384,1152]{1,0:T(8,128)(2,1)} %get-tuple-element.48.fields_ref, bf16[384,384]{1,0:T(8,128)(2,1)} %get-tuple-element.49.mixed_ref, ...), custom_call_target="tpu_custom_call" | custom-call | tf_op jit(solution)/shard_map/depth_back/pallas_call | solution.py:230
  155.0 4.3 %pair_sum.1 = bf16[9728,128]{1,0:T(8,128)(2,1)} custom-call(s32[1]{0:T(128)} %bitcast.6.core_ref, bf16[2,4608,128]{2,1,0:T(8,128)(2,1)} %bitcast.30, bf16[4608,128]{1,0:T(8,128)(2,1)} %copy-done.2, bf16[2,2304,128]{2,1,0:T(8,128)(2,1)} %bitcast.34, bf16[2304,128]{1,0:T(8,128)(2,1)} %copy-done.8, bf16[2,2304,128]{2,1,0:T(8,128)(2,1)} %bitcast.32, ...), custom_call_target="tpu_custom_call" | custom-call | tf_op jit(solution)/shard_map/pair_sum/pallas_call | solution.py:502
  159.4 42.0 %all_to_all.52.in_ref = bf16[64,152,128]{2,1,0:T(8,128)(2,1)} all-to-all(bf16[64,152,128]{2,1,0:T(8,128)(2,1)} %bitcast.26), channel_id=1, replica_groups=mesh['y'=4,'xh'=2,'core'=2,'xl'=2,'z'=4] {'y','xh','xl','z'}, dimensions={0} | all-to-all | bytes 4980736 | tf_op jit(solution)/shard_map/all_to_all | solution.py:601
  201.4 3.6 %chip_sum.1 = bf16[64,152,128]{2,1,0:T(8,128)(2,1)} custom-call(bf16[64,152,128]{2,1,0:T(8,128)(2,1)} %all_to_all.52.in_ref), custom_call_target="tpu_custom_call" | custom-call | tf_op jit(solution)/shard_map/chip_sum/pallas_call | solution.py:525
  205.0 38.5 %all_to_all.53 = bf16[64,152,128]{2,1,0:T(8,128)(2,1)S(1)} all-to-all(bf16[64,152,128]{2,1,0:T(8,128)(2,1)} %chip_sum.1), channel_id=1, replica_groups=mesh['y'=4,'xh'=2,'core'=2,'xl'=2,'z'=4] {'y','xh','xl','z'}, dimensions={0} | all-to-all | bytes 4980736 | tf_op jit(solution)/shard_map/all_to_all | solution.py:601
  243.5 2.6 collective-permute-start.9
  246.1 9.6 %all_to_all.54.tim_ref = bf16[8,40,384]{2,1,0:T(8,128)(2,1)} all-to-all(bf16[8,40,384]{2,1,0:T(8,128)(2,1)S(1)} %copy-done.11), channel_id=1, replica_groups=mesh['y'=4,'xh'=2,'core'=2,'xl'=2,'z'=4] {'xl','z'}, dimensions={0} | all-to-all | bytes 491520 | tf_op jit(solution)/shard_map/all_to_all | solution.py:601
  255.7 13.3 %all_to_all.55.dep_ref = bf16[16,24,384]{2,1,0:T(8,128)(2,1)} all-to-all(bf16[16,24,384]{2,1,0:T(8,128)(2,1)S(1)} %copy-done.10), channel_id=1, replica_groups=mesh['y'=4,'xh'=2,'core'=2,'xl'=2,'z'=4] {'y','xh','core'}, dimensions={0} | all-to-all | bytes 589824 | tf_op jit(solution)/shard_map/all_to_all | solution.py:601
  269.0 2.7 last_norm.1
  271.7 6.6 %unpack.1 = (f32[384,1152]{1,0:T(8,128)}, f32[384,384]{1,0:T(8,128)}, f32[384,1152]{1,0:T(8,128)}, f32[384,384]{1,0:T(8,128)}, f32[384,1536]{1,0:T(8,128)}, /*in...) custom-call(s32[1]{0:T(128)} %bitcast.6.core_ref, bf16[9728,128]{1,0:T(8,128)(2,1)} %bitcast.28, ...), custom_call_target="tpu_custom_call" | custom-call | tf_op jit(solution)/shard_map/unpack/pallas_call | solution.py:562
  279.9 1.3 slice_reduce_fusion
  282.4 1.7 reshape.94
  (76 shorter events, 14.0 us)
Async XLA Ops:
  17.3 17.7 %all-to-all-start = ((bf16[16,24,384]{2,1,0:T(8,128)(2,1)}), bf16[16,24,384]{2,1,0:T(8,128)(2,1)S(1)}, u32[]{:S(2)}, u32[]{:S(2)}) async-start(bf16[16,24,384]{2,1,0:T(8,128)(2,1)} %get-tuple-element.42), calls=%async_computation | async-start | bytes 589824 | tf_op jit(solution)/shard_map/all_to_all | solution.py:601
  35.0 3.4 %copy-start.1 = (bf16[16,24,384]{2,1,0:T(8,128)(2,1)}, bf16[16,24,384]{2,1,0:T(8,128)(2,1)S(1)}, u32[]{:S(2)}) copy-start(bf16[16,24,384]{2,1,0:T(8,128)(2,1)S(1)} %all-to-all-done.in_ref) | copy-start | bytes 884740
  35.0 9.4 %all-to-all-start.3 = ((bf16[8,40,384]{2,1,0:T(8,128)(2,1)}), bf16[8,40,384]{2,1,0:T(8,128)(2,1)S(1)}, u32[]{:S(2)}, u32[]{:S(2)}) async-start(bf16[8,40,384]{2,1,0:T(8,128)(2,1)} %get-tuple-element.45), calls=%async_computation.3 | async-start | bytes 491520 | tf_op jit(solution)/shard_map/all_to_all | solution.py:601
  38.5 30.6 %copy-start.6 = (bf16[1,2,144,384]{3,2,1,0:T(8,128)(2,1)S(1)}, bf16[1,2,144,384]{3,2,1,0:T(8,128)(2,1)}, u32[]{:S(2)}) copy-start(bf16[1,2,144,384]{3,2,1,0:T(8,128)(2,1)} %param.18) | copy-start | bytes 663556
  38.5 37.7 %copy-start.22 = (f32[384]{0:T(512)S(1)}, f32[384]{0:T(512)}, u32[]{:S(2)}) copy-start(f32[384]{0:T(512)} %param.24) | copy-start | bytes 4612
  38.5 38.3 %copy-start.12 = (f32[3,3,3,1536]{3,2,1,0:T(4,128)S(1)}, f32[3,3,3,1536]{3,2,1,0:T(4,128)}, u32[]{:S(2)}) copy-start(f32[3,3,3,1536]{3,2,1,0:T(4,128)} %param.26) | copy-start | bytes 497668
  44.4 15.2 %copy-start.5 = (bf16[8,40,384]{2,1,0:T(8,128)(2,1)}, bf16[8,40,384]{2,1,0:T(8,128)(2,1)S(1)}, u32[]{:S(2)}) copy-start(bf16[8,40,384]{2,1,0:T(8,128)(2,1)S(1)} %all-to-all-done.3.tim_ref) | copy-start | bytes 737284
  62.0 15.9 %collective-permute-start.1 = (bf16[288,384]{1,0:T(8,128)(2,1)}, bf16[288,384]{1,0:T(8,128)(2,1)S(1)}, u32[]{:S(2)}, u32[]{:S(2)}) collective-permute-start(bf16[288,384]{1,0:T(8,128)(2,1)} %middle.1.mid_ref), channel_id=1, source_target_pairs={{8,0},{16,8},{24,16},{32,24},{40,32},{48,40},{56,48},{64,56},{72,6... | collective-permute-start | bytes 663560 | tf_op jit(solution)/shard_map/ppermute | solution.py:614
  65.0 13.0 %collective-permute-start = (bf16[288,384]{1,0:T(8,128)(2,1)}, bf16[288,384]{1,0:T(8,128)(2,1)S(1)}, u32[]{:S(2)}, u32[]{:S(2)}) collective-permute-start(bf16[288,384]{1,0:T(8,128)(2,1)} %middle.1.mid_ref), channel_id=1, source_target_pairs={{0,8},{8,16},{16,24},{24,32},{32,40},{40,48},{48,56},{56,64},{64,7... | collective-permute-start | bytes 663560 | tf_op jit(solution)/shard_map/ppermute | solution.py:613
  69.1 8.4 %collective-permute-start.3 = (bf16[144,384]{1,0:T(8,128)(2,1)S(1)}, bf16[144,384]{1,0:T(8,128)(2,1)S(1)}, u32[]{:S(2)}, u32[]{:S(2)}) collective-permute-start(bf16[144,384]{1,0:T(8,128)(2,1)S(1)} %get-tuple-element.73), channel_id=1, source_target_pairs={{8,0},{16,8},{24,16},{32,24},{40,32},{48,40},{56,48},{64,56},{72,6... | collective-permute-start | bytes 331784 | tf_op jit(solution)/shard_map/ppermute | solution.py:607
  71.0 6.9 %collective-permute-start.2 = (bf16[144,384]{1,0:T(8,128)(2,1)S(1)}, bf16[144,384]{1,0:T(8,128)(2,1)S(1)}, u32[]{:S(2)}, u32[]{:S(2)}) collective-permute-start(bf16[144,384]{1,0:T(8,128)(2,1)S(1)} %get-tuple-element.74), channel_id=1, source_target_pairs={{0,8},{8,16},{16,24},{24,32},{32,40},{40,48},{48,56},{56,64},{64,7... | collective-permute-start | bytes 331784 | tf_op jit(solution)/shard_map/ppermute | solution.py:606
  109.7 9.4 %all-to-all-start.6 = ((bf16[8,40,384]{2,1,0:T(8,128)(2,1)}), bf16[8,40,384]{2,1,0:T(8,128)(2,1)S(1)}, u32[]{:S(2)}, u32[]{:S(2)}) async-start(bf16[8,40,384]{2,1,0:T(8,128)(2,1)} %get-tuple-element.51), calls=%async_computation.6 | async-start | bytes 491520 | tf_op jit(solution)/shard_map/all_to_all | solution.py:601
  114.5 38.7 %collective-permute-start.4 = (bf16[4608,128]{1,0:T(8,128)(2,1)S(1)}, bf16[4608,128]{1,0:T(8,128)(2,1)S(1)}, u32[]{:S(2)}, u32[]{:S(2)}) collective-permute-start(bf16[4608,128]{1,0:T(8,128)(2,1)S(1)} %dynamic-slice_bitcast_fusion), channel_id=1, source_target_pairs={{0,8},{8,0},{1,9},{9,1},{2,10},{10,2},{3,11},{11,3},{4,12},{12,4},... | collective-permute-start | bytes 3538952 | tf_op jit(solution)/shard_map/ppermute | solution.py:632
  119.1 8.5 %copy-start.4 = (bf16[8,40,384]{2,1,0:T(8,128)(2,1)}, bf16[8,40,384]{2,1,0:T(8,128)(2,1)S(1)}, u32[]{:S(2)}) copy-start(bf16[8,40,384]{2,1,0:T(8,128)(2,1)S(1)} %all-to-all-done.6.grad_ref) | copy-start | bytes 737284
  119.1 19.8 %all-to-all-start.4 = ((bf16[16,24,384]{2,1,0:T(8,128)(2,1)}), bf16[16,24,384]{2,1,0:T(8,128)(2,1)S(1)}, u32[]{:S(2)}, u32[]{:S(2)}) async-start(bf16[16,24,384]{2,1,0:T(8,128)(2,1)} %get-tuple-element.47), calls=%async_computation.4 | async-start | bytes 589824 | tf_op jit(solution)/shard_map/all_to_all | solution.py:601
  138.8 14.3 %collective-permute-start.6 = (bf16[2304,128]{1,0:T(8,128)(2,1)}, bf16[2304,128]{1,0:T(8,128)(2,1)S(1)}, u32[]{:S(2)}, u32[]{:S(2)}) collective-permute-start(bf16[2304,128]{1,0:T(8,128)(2,1)} %dynamic-slice_bitcast_fusion.1), channel_id=1, source_target_pairs={{0,8},{8,0},{1,9},{9,1},{2,10},{10,2},{3,11},{11,3},{4,12},{12,4},... | collective-permute-start | bytes 1769480 | tf_op jit(solution)/shard_map/ppermute | solution.py:632
  139.6 11.2 %copy-start.9 = (f32[6,64,128]{2,1,0:T(8,128)S(1)}, f32[6,64,128]{2,1,0:T(8,128)}, u32[]{:S(2)}) copy-start(f32[6,64,128]{2,1,0:T(8,128)} %get-tuple-element.59) | copy-start | bytes 589828
  139.6 11.4 %copy-start.20 = (f32[32,128]{1,0:T(8,128)S(1)}, f32[32,128]{1,0:T(8,128)}, u32[]{:S(2)}) copy-start(f32[32,128]{1,0:T(8,128)} %get-tuple-element.60) | copy-start | bytes 49156
  139.6 12.1 %copy-start.21 = (f32[32,128]{1,0:T(8,128)S(1)}, f32[32,128]{1,0:T(8,128)}, u32[]{:S(2)}) copy-start(f32[32,128]{1,0:T(8,128)} %get-tuple-element.62) | copy-start | bytes 49156
  150.3 2.8 collective-permute-start.5
  150.8 1.8 collective-permute-start.7
  151.8 2.3 copy-start.18
  151.8 1.4 collective-permute-start.8
  152.6 1.4 copy-start.17
  153.1 0.9 copy-start.19
  153.1 1.0 copy-start.7
  153.1 0.9 copy-start.8
  154.0 1.0 copy-start.2
  205.0 41.2 %copy-start.11 = (bf16[8,40,384]{2,1,0:T(8,128)(2,1)S(1)}, bf16[8,40,384]{2,1,0:T(8,128)(2,1)}, u32[]{:S(2)}) copy-start(bf16[8,40,384]{2,1,0:T(8,128)(2,1)} %get-tuple-element.54) | copy-start | bytes 737284
  205.0 50.7 %copy-start.10 = (bf16[16,24,384]{2,1,0:T(8,128)(2,1)S(1)}, bf16[16,24,384]{2,1,0:T(8,128)(2,1)}, u32[]{:S(2)}) copy-start(bf16[16,24,384]{2,1,0:T(8,128)(2,1)} %get-tuple-element.50) | copy-start | bytes 884740
  243.5 28.2 %copy-start = (bf16[64,152,128]{2,1,0:T(8,128)(2,1)}, bf16[64,152,128]{2,1,0:T(8,128)(2,1)S(1)}, u32[]{:S(2)}) copy-start(bf16[64,152,128]{2,1,0:T(8,128)(2,1)S(1)} %all_to_all.53) | copy-start | bytes 7471108
  243.5 28.2 %collective-permute-start.9 = (bf16[9728,128]{1,0:T(8,128)(2,1)S(1)}, bf16[9728,128]{1,0:T(8,128)(2,1)}, u32[]{:S(2)}, u32[]{:S(2)}) collective-permute-start(bf16[9728,128]{1,0:T(8,128)(2,1)S(1)} %bitcast.27), channel_id=1, source_target_pairs={{0,8},{8,0},{1,9},{9,1},{2,10},{10,2},{3,11},{11,3},{4,12},{12,4},... | collective-permute-start | bytes 7471112 | tf_op jit(solution)/shard_map/ppermute | solution.py:647
  (5 other events, 3.5 us)
where the time goes:
time: 286 us; the launch traced here: 284 us
  blocking collectives  131 us (46%)
  Pallas kernels  81.8 us (29%)
  starting transfers between devices  42.2 us (15%)
  local copies, waits for them, and re-layouts  15.5 us (5%)
  waiting for transfers between devices  10.9 us (4%)
    all_to_all x6, blocking collectives, exchange(): return lax.all_to_all(values, axes, split_axis=0, concat_axis=0, tiled=True)  131 us
    pallas_call x1, Pallas kernels, feed_forward(): pl.pallas_call(feed_kernel, grid=(STEPS,), out_shape=(shape((ROWS, C)), s...  30.9 us
    all_to_all x4, starting transfers between devices, exchange(): return lax.all_to_all(values, axes, split_axis=0, concat_axis=0, tiled=True)  24.1 us
    pallas_call x2, Pallas kernels, attend_back(): pl.pallas_call(attend_back_kernel, out_shape=(shape((count, part, C)), sh...  18.8 us
    pallas_call x2, Pallas kernels, attend(): pl.pallas_call(attend_kernel, out_shape=(shape((count, part, C)), shape((...  9.82 us
    all_to_all x4, waiting for transfers between devices, exchange(): return lax.all_to_all(values, axes, split_axis=0, concat_axis=0, tiled=True)  9.61 us
    pallas_call x1, Pallas kernels, unpack(): pl.pallas_call(unpack_kernel, out_shape=(shape((C, 3 * C), F32), shape((C...  6.61 us
  transfers between devices with their start and end apart: 14, of which 6 were waited for; matrix products, arithmetic and copies ran while one was open for 2% of the time, Pallas kernels for 11%

commit v1 on v0

v1 whole, which is shorter than its diff:
```python
import functools
import math

import jax
import jax.numpy as jnp
import numpy as np
from jax import lax
from jax.experimental import pallas as pl
from jax.experimental.pallas import tpu as pltpu
from jax.sharding import Mesh
from jax.sharding import PartitionSpec as P


C = 384
HID = 1536
PW = 24
CELLS = 144
ROWS = 288
BLOCK = 256
STEPS = HID // BLOCK
PAD = 192
DEV = ("y", "xh", "core")
TA = ("xl", "z")
CHIPS = ("y", "xh", "xl", "z")
COPIES = 64
CHUNK = 80
F32 = jnp.float32
BF16 = jnp.bfloat16
EPS = 1e-5


def spread_depth():
    table = np.zeros((16, 24, ROWS), np.float32)
    for owner in range(16):
        for k in range(18):
            table[owner, k, (k // 9) * CELLS + 9 * owner + k % 9] = 1
    return table.reshape(384, ROWS)


def spread_time():
    table = np.zeros((8, 40, ROWS), np.float32)
    for owner in range(8):
        for k in range(36):
            table[owner, k, (k // 18) * CELLS + 18 * owner + k % 18] = 1
    return table.reshape(320, ROWS)


def groups_depth():
    k = np.arange(384) % 24
    return np.where(k < 18, k % 9, k - 9).astype(np.int32)


def groups_time():
    return (np.arange(320) % 40).astype(np.int32)


def dot(left, right, dims=((1,), (0,)), precision=None):
    return lax.dot_general(
        left, right, (dims, ((), ())), preferred_element_type=F32, precision=precision
    )


def norm_parts(values):
    centered = values - jnp.mean(values, axis=-1, keepdims=True)
    inverse = lax.rsqrt(jnp.mean(centered * centered, axis=-1, keepdims=True) + EPS)
    return centered * inverse, inverse


def norm_back(scaled, inverse, grads):
    mean = jnp.mean(grads, axis=-1, keepdims=True)
    along = jnp.mean(grads * scaled, axis=-1, keepdims=True)
    return (grads - mean - scaled * along) * inverse


def vmem(count):
    return [pl.BlockSpec(memory_space=pltpu.VMEM)] * count


SMEM = [pl.BlockSpec(memory_space=pltpu.SMEM)]


def shape(dims, kind=BF16):
    return jax.ShapeDtypeStruct(dims, kind)


def deal(values, turn, mask, part_refs, hold_ref):
    count = len(part_refs)
    hold_ref[...] = values.reshape(count, values.shape[0] // count, C)
    for step, ref in enumerate(part_refs):
        ref[...] = hold_ref[(turn + step) & mask].astype(BF16)


def row_of(ref):
    return ref[...].reshape(1, ref.shape[0])


def first_kernel(tok_ref, gain_ref, pd_ref, pt_ref, dep_ref, tim_ref):
    scaled, _ = norm_parts(tok_ref[...].astype(F32))
    normed = (scaled * row_of(gain_ref)).astype(BF16)
    dep_ref[...] = dot(pd_ref[...], normed).reshape(16, 24, C).astype(BF16)
    tim_ref[...] = dot(pt_ref[...], normed).reshape(8, 40, C).astype(BF16)


def first_norm(tokens, gain, pd, pt):
    return pl.pallas_call(
        first_kernel,
        out_shape=(shape((16, 24, C)), shape((8, 40, C))),
        in_specs=vmem(4),
        out_specs=tuple(vmem(2)),
        name="first_norm",
    )(tokens, gain, pd, pt)


ATT = 2304


def lane_is_low():
    return lax.broadcasted_iota(jnp.int32, (1, 128), 1) < 64


def head_ones():
    row = lax.broadcasted_iota(jnp.int32, (128, 128), 0) < 64
    col = lax.broadcasted_iota(jnp.int32, (128, 128), 1) < 64
    return jnp.where(row == col, 1.0, 0.0).astype(BF16)


def head_sum(values, ones):
    high = values.astype(BF16)
    low = (values - high.astype(F32)).astype(BF16)
    return dot(high, ones) + dot(low, ones)


def joined(refs):
    if len(refs) == 1:
        count, part, _ = refs[0].shape
        return refs[0][...].astype(F32).reshape(count * part, C).astype(BF16)
    return jnp.concatenate([ref[...].astype(F32) for ref in refs], axis=0).astype(BF16)


def dealt(values, refs):
    if len(refs) == 1:
        refs[0][...] = values.reshape(refs[0].shape).astype(BF16)
        return
    part = values.shape[0] // len(refs)
    for step, ref in enumerate(refs):
        ref[...] = values[part * step : part * step + part].astype(BF16)


def attend_kernel(count, *refs):
    in_refs, refs = refs[:count], refs[count:]
    w_ref, wo_ref, scale_ref, gr_ref, gc_ref = refs[:5]
    out_refs, (fields_ref, mixed_ref, same_ref) = refs[5 : 5 + count], refs[5 + count :]
    rowed = joined(in_refs)
    rows = rowed.shape[0]
    fields_ref[...] = dot(rowed, w_ref[...]).astype(BF16)
    same_ref[...] = jnp.where(gr_ref[...] == gc_ref[...], 1.0, 0.0)
    ones = head_ones()
    low = lane_is_low()
    side = jnp.ones((rows, 128), BF16)

    def one_pair(pair, _):
        at = pl.multiple_of(128 * pair, 128)
        query = fields_ref[:, pl.ds(at, 128)].astype(F32)
        keyed = fields_ref[:, pl.ds(C + at, 128)].astype(F32)
        valued = fields_ref[:, pl.ds(2 * C + at, 128)]
        query = query * lax.rsqrt(head_sum(query * query, ones) + 1e-6)
        keyed = (keyed * lax.rsqrt(head_sum(keyed * keyed, ones) + 1e-6)).astype(BF16)
        query = query * jnp.where(low, scale_ref[2 * pair], scale_ref[2 * pair + 1])
        both = jnp.concatenate([valued, side], axis=1)
        results = []
        for half in range(2):
            mine = low if half == 0 else jnp.logical_not(low)
            scores = dot(jnp.where(mine, query, 0.0).astype(BF16), keyed, ((1,), (1,)))
            weights = (jnp.exp(scores) * same_ref[...]).astype(BF16)
            sums = dot(weights, both)
            results.append(sums[:, :128] / sums[:, 128:])
        mixed_ref[:, pl.ds(at, 128)] = jnp.where(low, results[0], results[1]).astype(BF16)
        return 0

    lax.fori_loop(0, 3, one_pair, 0)
    dealt(dot(mixed_ref[...], wo_ref[...]), out_refs)


def attend(inputs, weight, out_weight, scale, groups):
    count, rows = len(inputs), groups.shape[0]
    outs = pl.pallas_call(
        functools.partial(attend_kernel, count),
        out_shape=tuple(shape(x.shape) for x in inputs) + (shape((rows, 3 * C)), shape((rows, C))),
        in_specs=vmem(count + 2) + SMEM + vmem(2),
        out_specs=tuple(vmem(count + 2)),
        scratch_shapes=[pltpu.VMEM((rows, rows), F32)],
    )(*inputs, weight, out_weight, scale, groups[:, None], groups[None, :])
    return outs[:count], outs[count], outs[count + 1]


def put_tile(ref, tile, values):
    for half in range(2):
        ref[half, 192 * tile : 192 * tile + 192, :] = values[192 * half : 192 * half + 192].astype(BF16)


def attend_back_kernel(count, out_count, *refs):
    grad_refs, in_refs, refs = refs[:count], refs[count : 2 * count], refs[2 * count :]
    me_ref, fields_ref, mixed_ref, w_ref, wo_ref, scale_ref, gr_ref, gc_ref, gain_ref = refs[:9]
    out_refs, refs = refs[9 : 9 + out_count], refs[9 + out_count :]
    weights_ref, small_ref, same_ref, fg_ref, cot_ref = refs[:5]
    grads = joined(grad_refs)
    rows = grads.shape[0]
    same_ref[...] = jnp.where(gr_ref[...] == gc_ref[...], 1.0, 0.0)
    out_grad = dot(mixed_ref[...], grads, ((0,), (0,)))
    for tile in range(3):
        put_tile(weights_ref, 9 + tile, out_grad[:, 128 * tile : 128 * tile + 128])
    cot_ref[...] = dot(grads, wo_ref[...], ((1,), (1,))).astype(BF16)
    ones = head_ones()
    low = lane_is_low()
    side = jnp.ones((rows, 128), BF16)
    small_ref[24:32, :] = jnp.zeros((8, 128), F32)

    def one_pair(pair, _):
        at = pl.multiple_of(128 * pair, 128)
        query = fields_ref[:, pl.ds(at, 128)].astype(F32)
        keyed = fields_ref[:, pl.ds(C + at, 128)].astype(F32)
        valued = fields_ref[:, pl.ds(2 * C + at, 128)]
        query_inv = lax.rsqrt(head_sum(query * query, ones) + 1e-6)
        keyed_inv = lax.rsqrt(head_sum(keyed * keyed, ones) + 1e-6)
        query = query * query_inv
        keyed = keyed * keyed_inv
        scale = jnp.where(low, scale_ref[2 * pair], scale_ref[2 * pair + 1])
        scaled = query * scale
        keyed_short = keyed.astype(BF16)
        cot = cot_ref[:, pl.ds(at, 128)]
        delta = head_sum(cot.astype(F32) * mixed_ref[:, pl.ds(at, 128)].astype(F32), ones)
        query_grad = jnp.zeros((rows, 128), F32)
        keyed_grad = jnp.zeros((rows, 128), F32)
        value_grad = jnp.zeros((rows, 128), F32)
        for half in range(2):
            mine = low if half == 0 else jnp.logical_not(low)
            lane = 64 * half
            mine_query = jnp.where(mine, scaled, 0.0).astype(BF16)
            mine_cot = jnp.where(mine, cot.astype(F32), 0.0).astype(BF16)
            mine_keyed = jnp.where(mine, keyed, 0.0).astype(BF16)
            scores = dot(mine_query, keyed_short, ((1,), (1,)))
            weights = jnp.exp(scores) * same_ref[...]
            total = dot(weights.astype(BF16), side)
            weights = weights * (1.0 / total)[:, :1]
            weights_grad = dot(mine_cot, valued, ((1,), (1,)))
            scores_grad = (weights * (weights_grad - delta[:, lane : lane + 1])).astype(BF16)
            value_grad = value_grad + dot(weights.astype(BF16), mine_cot, ((0,), (0,)))
            query_grad = query_grad + dot(scores_grad, mine_keyed)
            keyed_grad = keyed_grad + dot(scores_grad, mine_query, ((0,), (0,)))
        along = jnp.sum(query_grad * query, axis=0, keepdims=True)
        small_ref[pl.ds(24 + pair, 1), :] = head_sum(jnp.broadcast_to(along, (8, 128)), ones)[:1]
        query_grad = query_grad * scale
        query_grad = (query_grad - query * head_sum(query * query_grad, ones)) * query_inv
        keyed_grad = (keyed_grad - keyed * head_sum(keyed * keyed_grad, ones)) * keyed_inv
        fg_ref[:, pl.ds(at, 128)] = query_grad.astype(BF16)
        fg_ref[:, pl.ds(C + at, 128)] = keyed_grad.astype(BF16)
        fg_ref[:, pl.ds(2 * C + at, 128)] = value_grad.astype(BF16)
        return 0

    lax.fori_loop(0, 3, one_pair, 0)
    back = dot(fg_ref[...], w_ref[...], ((1,), (1,)))
    if out_count == 16:
        deal(back, me_ref[2], 15, out_refs, refs[5])
    else:
        dealt(back, out_refs)
    grad = dot(joined(in_refs), fg_ref[...], ((0,), (0,)))
    product = jnp.zeros((C, 128), F32)
    for tile in range(9):
        at = 128 * tile
        put_tile(weights_ref, tile, grad[:, at : at + 128])
        product = product + grad[:, at : at + 128] * w_ref[:, at : at + 128].astype(F32)
    gain_part = dot(jnp.ones((8, 128), F32), product, ((1,), (1,)), lax.Precision.HIGHEST)
    gain_part = gain_part / row_of(gain_ref)
    for tile in range(3):
        small_ref[8 * tile : 8 * tile + 8, :] = gain_part[:, 128 * tile : 128 * tile + 128]
    for half in range(2):
        weights_ref[half, ATT:, :] = small_ref[...].astype(BF16)


def attend_back(me, grads, inputs, fields, mixed, weight, out_weight, scale, groups, gain, deals):
    count, rows = len(inputs), groups.shape[0]
    part = rows // 16
    scratch = [pltpu.VMEM((32, 128), F32), pltpu.VMEM((rows, rows), F32), pltpu.VMEM((rows, 3 * C), BF16)]
    scratch.append(pltpu.VMEM((rows, C), BF16))
    if deals == 16:
        scratch.append(pltpu.VMEM((16, part, C), F32))
    outs = pl.pallas_call(
        functools.partial(attend_back_kernel, count, deals),
        out_shape=((shape((part, C)),) * 16 if deals == 16 else (shape(inputs[0].shape),))
        + (shape((2, ATT + 32, 128)),),
        in_specs=vmem(2 * count) + SMEM + vmem(4) + SMEM + vmem(3),
        out_specs=tuple(vmem(deals + 1)),
        scratch_shapes=scratch,
    )(*grads, *inputs, me, fields, mixed, weight, out_weight, scale, groups[:, None], groups[None, :], gain)
    return outs[:deals], outs[deals]


def middle_kernel(tok_ref, pd_ref, pt_ref, dep_ref, tim_ref, out_ref):
    total = tok_ref[...].astype(F32) + dot(pd_ref[...], joined([dep_ref]), ((0,), (0,)))
    out_ref[...] = (total + dot(pt_ref[...], joined([tim_ref]), ((0,), (0,)))).astype(BF16)


def middle_of(tokens, depth, time, pd, pt):
    return pl.pallas_call(
        middle_kernel,
        out_shape=shape((ROWS, C)),
        in_specs=vmem(5),
        out_specs=vmem(1)[0],
        name="middle",
    )(tokens, pd, pt, depth, time)


STRIDE = 1600
FFN = 3 * STRIDE


def down_one(values, first):
    return jnp.where(first, 0.0, pltpu.roll(values, 1, 0))


def up_one(values, last):
    return jnp.where(last, 0.0, pltpu.roll(values, PW - 1, 0))


def act_pair(values):
    square = values * values
    inner = 0.7978845608 * values * (1.0 + 0.044715 * square)
    tanh = jnp.tanh(inner)
    half = 0.5 * (1.0 + tanh)
    slope = 0.7978845608 * (1.0 + 3.0 * 0.044715 * square)
    return values * half, half + 0.5 * values * (1.0 - tanh * tanh) * slope


def feed_kernel(
    low_ref, mid_ref, high_ref, og_low_ref, og_ref, og_high_ref, gain_ref, up_ref, kern_ref, down_ref,
    pd_ref, pt_ref, block_ref, mgrad_ref, weights_ref, bdep_ref, btim_ref,
    norm_ref, og4_ref, hid_ref, fgr_ref, act_ref, hgr_ref, ag_ref, block_acc, back_acc, prod_acc, kgrad_ref,
):
    step = pl.program_id(0)

    @pl.when(step == 0)
    def _():
        for at, ref in ((0, low_ref), (ROWS, mid_ref), (2 * ROWS, high_ref)):
            scaled, _ = norm_parts(ref[...].astype(F32))
            norm_ref[at : at + ROWS, :] = (scaled * row_of(gain_ref)).astype(BF16)
        og4_ref[0:CELLS, :] = og_low_ref[...]
        og4_ref[CELLS : CELLS + ROWS, :] = og_ref[...]
        og4_ref[CELLS + ROWS : 2 * ROWS, :] = og_high_ref[...]
        hid_ref[...] = jnp.zeros(hid_ref.shape, F32)
        fgr_ref[...] = jnp.zeros(fgr_ref.shape, F32)
        block_acc[...] = jnp.zeros(block_acc.shape, F32)
        back_acc[...] = jnp.zeros(back_acc.shape, F32)
        prod_acc[...] = jnp.zeros(prod_acc.shape, F32)

    place = lax.broadcasted_iota(jnp.int32, (PW, 128), 0)
    first, last = place == 0, place == PW - 1
    hidden = dot(norm_ref[...], up_ref[...]).astype(BF16).astype(F32)
    ag_ref[...] = dot(og4_ref[...], down_ref[...], ((1,), (1,)))
    for lt in range(2):
        for piece in range(6):
            hid_ref[lt, piece * PAD + PW : piece * PAD + PW + CELLS, :] = hidden[
                piece * CELLS : (piece + 1) * CELLS, 128 * lt : 128 * lt + 128
            ]

    for lt in range(2):
        lanes = slice(128 * lt, 128 * lt + 128)

        def forward(piece, _, lt=lt, lanes=lanes):
            for i in range(6):
                acc = [None] * 3
                for a in range(3):
                    for b in range(3):
                        start = pl.multiple_of((piece + a) * PAD + PW * (i + b), 8)
                        window = hid_ref[lt, pl.ds(start, PW), :]
                        for e in range(3):
                            term = kern_ref[a, b, e : e + 1, lanes] * window
                            acc[e] = term if acc[e] is None else acc[e] + term
                filtered = acc[1] + down_one(acc[0], first) + up_one(acc[2], last)
                value, slope = act_pair(filtered)
                at = pl.multiple_of(piece * CELLS + PW * i, 8)
                grad = (ag_ref[pl.ds(at, PW), lanes] * slope).astype(BF16).astype(F32)
                fgr_ref[lt, pl.ds(pl.multiple_of(piece * PAD + PW * (i + 1), 8), PW), :] = grad
                act_ref[pl.ds(at, PW), lanes] = value
            return 0

        lax.fori_loop(0, 4, forward, 0)

        def backward(piece, sums, lt=lt, lanes=lanes):
            sums = list(sums)
            for i in range(6):
                acc = [None] * 3
                for a in range(3):
                    for b in range(3):
                        start = pl.multiple_of((piece + 2 - a) * PAD + PW * (i + 2 - b), 8)
                        window = fgr_ref[lt, pl.ds(start, PW), :]
                        for e in range(3):
                            term = kern_ref[a, b, e : e + 1, lanes] * window
                            acc[e] = term if acc[e] is None else acc[e] + term
                total = acc[1] + up_one(acc[0], last) + down_one(acc[2], first)
                hgr_ref[pl.ds(pl.multiple_of(piece * CELLS + PW * i, 8), PW), lanes] = total
            return tuple(sums)

        lax.fori_loop(0, 2, backward, ())

        for a in range(3):

            def products(piece, sums, a=a, lt=lt):
                sums = list(sums)
                for i in range(6):
                    own = pl.multiple_of((piece + 1) * PAD + PW * (i + 1), 8)
                    grad = fgr_ref[lt, pl.ds(own, PW), :]
                    shifted = (up_one(grad, last), grad, down_one(grad, first))
                    for b in range(3):
                        start = pl.multiple_of((piece + 1 + a) * PAD + PW * (i + b), 8)
                        window = hid_ref[lt, pl.ds(start, PW), :]
                        for e in range(3):
                            term = window * shifted[e]
                            k = 3 * b + e
                            sums[k] = sums[k] + (term[0:8] + term[8:16] + term[16:24])
                return tuple(sums)

            sums = lax.fori_loop(0, 2, products, tuple(jnp.zeros((8, 128), F32) for _ in range(9)))
            for k in range(9):
                row = 32 * lt + 9 * a + k
                kgrad_ref[row : row + 1, :] = jnp.sum(sums[k], axis=0, keepdims=True)
        kgrad_ref[32 * lt + 27 : 32 * lt + 32, :] = jnp.zeros((5, 128), F32)

    active = act_ref[CELLS : CELLS + ROWS, :].astype(BF16)
    block_acc[...] += dot(active, down_ref[...])
    down_grad = dot(active, og_ref[...], ((0,), (0,)))
    hidden_grad = hgr_ref[...].astype(BF16)
    up_grad = dot(norm_ref[ROWS : 2 * ROWS, :], hidden_grad, ((0,), (0,)))
    back_acc[...] += dot(hidden_grad, up_ref[...], ((1,), (1,)))
    product = up_grad * up_ref[...].astype(F32)
    prod_acc[...] += product[:, :128] + product[:, 128:]
    half = step // 3
    base = pl.multiple_of((step - 3 * half) * STRIDE, 16)
    for tile in range(2):
        weights_ref[half, pl.ds(base + C * tile, C), :] = up_grad[:, 128 * tile : 128 * tile + 128].astype(BF16)
    for tile in range(3):
        at = 2 * C + BLOCK * tile
        weights_ref[half, pl.ds(base + at, BLOCK), :] = down_grad[:, 128 * tile : 128 * tile + 128].astype(BF16)
    weights_ref[half, pl.ds(base + 1536, 64), :] = kgrad_ref[...].astype(BF16)

    @pl.when(step == STEPS - 1)
    def _():
        wide = mid_ref[...].astype(F32)
        block_ref[...] = (wide + block_acc[...]).astype(BF16)
        scaled, inverse = norm_parts(wide)
        back = norm_back(scaled, inverse, back_acc[...] * row_of(gain_ref))
        middle_grad = og_ref[...].astype(F32) + back
        mgrad_ref[...] = middle_grad
        short = middle_grad.astype(BF16)
        bdep_ref[...] = dot(pd_ref[...], short).reshape(16, 24, C).astype(BF16)
        btim_ref[...] = dot(pt_ref[...], short).reshape(8, 40, C).astype(BF16)
        part = dot(jnp.ones((8, 128), F32), prod_acc[...], ((1,), (1,)), lax.Precision.HIGHEST)
        part = part / row_of(gain_ref)
        for tile in range(3):
            kgrad_ref[8 * tile : 8 * tile + 8, :] = part[:, 128 * tile : 128 * tile + 128]
        kgrad_ref[24:32, :] = jnp.zeros((8, 128), F32)
        for side in range(2):
            weights_ref[side, 3 * STRIDE :, :] = kgrad_ref[0:32, :].astype(BF16)


def feed_forward(low, mid, high, og_low, og, og_high, gain, up, kern, down, pd, pt):
    def whole(*dims):
        return pl.BlockSpec(dims, lambda s: (0,) * len(dims))

    return pl.pallas_call(
        feed_kernel,
        grid=(STEPS,),
        out_shape=(
            shape((ROWS, C)),
            shape((ROWS, C), F32),
            shape((2, FFN + 32, 128)),
            shape((16, 24, C)),
            shape((8, 40, C)),
        ),
        in_specs=[
            whole(ROWS, C),
            whole(ROWS, C),
            whole(ROWS, C),
            whole(CELLS, C),
            whole(ROWS, C),
            whole(CELLS, C),
            whole(C),
            pl.BlockSpec((C, BLOCK), lambda s: (0, s)),
            pl.BlockSpec((3, 3, 3, BLOCK), lambda s: (0, 0, 0, s)),
            pl.BlockSpec((BLOCK, C), lambda s: (s, 0)),
            whole(384, ROWS),
            whole(320, ROWS),
        ],
        out_specs=(
            whole(ROWS, C),
            whole(ROWS, C),
            whole(2, FFN + 32, 128),
            whole(16, 24, C),
            whole(8, 40, C),
        ),
        scratch_shapes=[
            pltpu.VMEM((3 * ROWS, C), BF16),
            pltpu.VMEM((2 * ROWS, C), BF16),
            pltpu.VMEM((2, 6 * PAD, 128), F32),
            pltpu.VMEM((2, 4 * PAD, 128), F32),
            pltpu.VMEM((2 * ROWS, BLOCK), F32),
            pltpu.VMEM((ROWS, BLOCK), F32),
            pltpu.VMEM((2 * ROWS, BLOCK), F32),
            pltpu.VMEM((ROWS, C), F32),
            pltpu.VMEM((ROWS, C), F32),
            pltpu.VMEM((C, 128), F32),
            pltpu.VMEM((64, 128), F32),
        ],
        name="feed_forward",
    )(low, mid, high, og_low, og, og_high, gain, up, kern, down, pd, pt)


def last_kernel(me_ref, tok_ref, pd_ref, pt_ref, gain_ref, mgrad_ref, tim_ref, *rest):
    dep_refs, (out_ref, dep_hold) = rest[:16], rest[16:]
    for step, ref in enumerate(dep_refs):
        dep_hold[(me_ref[2] - step) & 15] = ref[...].astype(F32)
    dep = dep_hold[...].reshape(384, C).astype(BF16)
    back = dot(pd_ref[...], dep, ((0,), (0,))) + dot(pt_ref[...], joined([tim_ref]), ((0,), (0,)))
    scaled, inverse = norm_parts(tok_ref[...].astype(F32))
    out_ref[...] = (mgrad_ref[...] + norm_back(scaled, inverse, back * row_of(gain_ref))).astype(BF16)


def last_norm(me, tokens, depth, time, pd, pt, gain, mgrad):
    return pl.pallas_call(
        last_kernel,
        out_shape=shape((ROWS, C)),
        in_specs=SMEM + vmem(22),
        out_specs=vmem(1)[0],
        scratch_shapes=[pltpu.VMEM((16, 24, C), F32)],
        name="last_norm",
    )(me, tokens, pd, pt, gain, mgrad, time, *depth)


STACK = COPIES * CHUNK
DEP = 0
TIM = DEP + ATT + 32


def pair_kernel(me_ref, *refs):
    out_ref, at = refs[-1], 0
    for one, two in zip(refs[0:-1:2], refs[1:-1:2], strict=True):
        size = one.shape[1]
        out_ref[at : at + size, :] = (one[0].astype(F32) + two[0].astype(F32)).astype(BF16)
        at += size
    out_ref[at:, :] = jnp.zeros((STACK - at, 128), BF16)


def swapped(array):
    return lax.ppermute(array, "core", [(0, 1), (1, 0)])


def pair_sum(me, args):
    return pl.pallas_call(
        pair_kernel,
        out_shape=shape((STACK, 128)),
        grid_spec=pltpu.PrefetchScalarGridSpec(
            num_scalar_prefetch=1,
            grid=(1,),
            in_specs=[pl.BlockSpec((1,) + a.shape[1:], lambda i, m: (m[0], 0, 0)) for a in args],
            out_specs=pl.BlockSpec((STACK, 128), lambda i, m: (0, 0)),
        ),
    )(me, *args)


def chip_total(factor, in_ref):
    def add(source, total):
        return total + in_ref[source].astype(F32)

    total = lax.fori_loop(1, COPIES, add, in_ref[0].astype(F32), unroll=3)
    return (total * factor).astype(BF16)


def chip_kernel(factor, in_ref, out_ref):
    out_ref[...] = chip_total(factor, in_ref)


def chip_spread_kernel(factor, in_ref, other_ref, out_ref):
    total = chip_total(factor, in_ref)
    other = other_ref[...]

    def put(target, _):
        out_ref[target, :CHUNK, :] = other
        out_ref[target, CHUNK:, :] = total
        return 0

    lax.fori_loop(0, COPIES, put, 0, unroll=2)


def chip_sum(received, factor):
    return pl.pallas_call(
        functools.partial(chip_kernel, factor),
        out_shape=shape((CHUNK, 128)),
        in_specs=vmem(1),
        out_specs=vmem(1)[0],
        name="chip_sum",
    )(received)


def chip_spread(received, other, factor):
    return pl.pallas_call(
        functools.partial(chip_spread_kernel, factor),
        out_shape=shape((COPIES, 2 * CHUNK, 128)),
        in_specs=vmem(2),
        out_specs=vmem(1)[0],
        name="chip_spread",
    )(received, other)


def unpack_kernel(own, me_ref, in_ref, *refs):
    refs = refs if own else refs[7:]
    dq_ref, do_ref, tq_ref, to_ref, up_ref, kg_ref, dn_ref = refs[:7]
    ffn_ref, att_ref = refs[-2:]

    def split(source, _):
        at = pl.multiple_of(CHUNK * source, 16)
        ffn_ref[pl.ds(at, CHUNK), :] = in_ref[source, :CHUNK, :]
        att_ref[pl.ds(at, CHUNK), :] = in_ref[source, CHUNK:, :]
        return 0

    lax.fori_loop(0, COPIES, split, 0, unroll=2)
    for step in range(3):
        at = STRIDE * step
        for tile in range(2):
            lanes = slice(BLOCK * step + 128 * tile, BLOCK * step + 128 * tile + 128)
            up_ref[:, lanes] = ffn_ref[at + C * tile : at + C * tile + C, :].astype(F32)
            kgrad = ffn_ref[at + 1536 + 32 * tile : at + 1568 + 32 * tile, :].astype(F32)
            for k in range(27):
                kg_ref[k // 9, k // 3 % 3, k % 3 : k % 3 + 1, lanes] = kgrad[k : k + 1]
        for tile in range(3):
            rows = ffn_ref[at + 768 + BLOCK * tile : at + 1024 + BLOCK * tile, :].astype(F32)
            dn_ref[BLOCK * step : BLOCK * step + BLOCK, 128 * tile : 128 * tile + 128] = rows
    for base, q_ref, o_ref in ((DEP, dq_ref, do_ref), (TIM, tq_ref, to_ref)):
        for tile in range(12):
            rows = att_ref[base + 192 * tile : base + 192 * tile + 192, :].astype(F32)
            if tile < 9:
                q_ref[:, 128 * tile : 128 * tile + 128] = rows
            else:
                o_ref[:, 128 * (tile - 9) : 128 * (tile - 9) + 128] = rows
    if own:
        first_ref, second_ref, dscale_ref, tscale_ref = refs[7:11]
        two = ffn_ref[FFN : FFN + 32, :].astype(F32)
        dep = att_ref[DEP + ATT : DEP + ATT + 32, :].astype(F32)
        tim = att_ref[TIM + ATT : TIM + ATT + 32, :].astype(F32)
        one = dep + tim
        for tile in range(3):
            lanes = slice(128 * tile, 128 * tile + 128)
            second_ref[lanes] = two[8 * tile : 8 * tile + 1].reshape(128)
            first_ref[lanes] = one[8 * tile : 8 * tile + 1].reshape(128)
        for head in range(6):
            dscale_ref[head] = dep[24 + head // 2, 64 * (head % 2)]
            tscale_ref[head] = tim[24 + head // 2, 64 * (head % 2)]


def unpack(own, me, gathered, partial=()):
    half = (lambda m: m[0]) if own else (lambda m: 1 - m[0])
    out_shape = [
        shape((C, 3 * C), F32),
        shape((C, C), F32),
        shape((C, 3 * C), F32),
        shape((C, C), F32),
        shape((C, HID), F32),
        shape((3, 3, 3, HID), F32),
        shape((HID, C), F32),
    ]
    out_specs = [
        pl.BlockSpec((192, 3 * C), lambda i, m: (half(m), 0)),
        pl.BlockSpec((192, C), lambda i, m: (half(m), 0)),
        pl.BlockSpec((192, 3 * C), lambda i, m: (half(m), 0)),
        pl.BlockSpec((192, C), lambda i, m: (half(m), 0)),
        pl.BlockSpec((C, HID // 2), lambda i, m: (0, half(m))),
        pl.BlockSpec((3, 3, 3, HID // 2), lambda i, m: (0, 0, 0, half(m))),
        pl.BlockSpec((HID // 2, C), lambda i, m: (half(m), 0)),
    ]
    if own:
        out_shape += [shape((C,), F32), shape((C,), F32), shape((6,), F32), shape((6,), F32)]
        out_specs += [pl.BlockSpec((C,), lambda i, m: (0,))] * 2 + [pl.BlockSpec(memory_space=pltpu.SMEM)] * 2
    return pl.pallas_call(
        functools.partial(unpack_kernel, own),
        out_shape=tuple(out_shape),
        grid_spec=pltpu.PrefetchScalarGridSpec(
            num_scalar_prefetch=1,
            grid=(1,),
            in_specs=[pl.BlockSpec((COPIES, 2 * CHUNK, 128), lambda i, m: (0, 0, 0))]
            + [pl.BlockSpec(memory_space=pl.ANY)] * len(partial),
            out_specs=tuple(out_specs),
            scratch_shapes=[pltpu.VMEM((STACK, 128), BF16), pltpu.VMEM((STACK, 128), BF16)],
        ),
        input_output_aliases={2 + i: i for i in range(len(partial))},
        name="unpack_own" if own else "unpack_other",
    )(me, gathered, *partial)


def local(
    tokens, out_grad, first_gain, depth_qkv, depth_out, time_qkv, time_out, second_gain, up_weight,
    spatial_kernel, down_weight, depth_scale, time_scale,
):
    pd = jnp.asarray(spread_depth(), BF16)
    pt = jnp.asarray(spread_time(), BF16)
    gd = jnp.asarray(groups_depth())
    gt = jnp.asarray(groups_time())
    me = jnp.stack([lax.axis_index("core"), lax.axis_index(TA), lax.axis_index(DEV)]).astype(jnp.int32)
    block_shape = tokens.shape
    flat = tokens.reshape(ROWS, C)
    og = out_grad.reshape(ROWS, C)
    count, frames = lax.axis_size(DEV), lax.axis_size(TA)
    ahead = [(i, i + 1) for i in range(count - 1)]
    behind = [(i + 1, i) for i in range(count - 1)]

    queue = []

    def exchange(values, axes):
        if queue:
            values, _ = lax.optimization_barrier((values, queue[-1]))
        queue.append(lax.all_to_all(values, axes, split_axis=0, concat_axis=0, tiled=True))
        return queue[-1]

    dep, tim = first_norm(flat, first_gain, pd, pt)
    tim = [exchange(tim, TA)]
    dep = [exchange(dep, DEV)]
    tim_out, tim_fields, tim_mixed = attend(tim, time_qkv, time_out, time_scale, gt)
    tim_back = exchange(tim_out[0], TA)
    dep_out, dep_fields, dep_mixed = attend(dep, depth_qkv, depth_out, depth_scale, gd)
    dep_back = exchange(dep_out[0], DEV)
    og_low = lax.ppermute(og[CELLS:], DEV, ahead)
    og_high = lax.ppermute(og[:CELLS], DEV, behind)
    dep_back, og_low, og_high = lax.optimization_barrier((dep_back, og_low, og_high))
    mid = middle_of(flat, dep_back, tim_back, pd, pt)
    low = lax.ppermute(mid, DEV, ahead)
    high = lax.ppermute(mid, DEV, behind)
    block_out, mgrad, ffn_g, bdep, btim = feed_forward(
        low, mid, high, og_low, og, og_high, second_gain, up_weight, spatial_kernel, down_weight, pd, pt
    )
    btim = exchange(btim, TA)
    bdep = exchange(bdep, DEV)
    ffn_other = swapped(ffn_g)
    ffn_stack = pair_sum(me, [ffn_g, ffn_other])
    ffn_stack = exchange(ffn_stack.reshape(COPIES, CHUNK, 128), CHIPS)
    (tim_first,), tim_g = attend_back(
        me, [btim], tim, tim_fields, tim_mixed, time_qkv, time_out, time_scale, gt, first_gain, 1
    )
    tim_other = swapped(tim_g)
    dep_first, dep_g = attend_back(
        me, [bdep], dep, dep_fields, dep_mixed, depth_qkv, depth_out, depth_scale, gd, first_gain, 16
    )
    dep_other = swapped(dep_g)
    tim_first = exchange(tim_first, TA)
    factor = 1.0 / math.sqrt(ROWS * count * frames)
    att_stack = pair_sum(me, [dep_g, dep_other, tim_g, tim_other])
    att_stack = exchange(att_stack.reshape(COPIES, CHUNK, 128), CHIPS)
    ffn_chunk = chip_sum(ffn_stack, factor)
    dep_first = [
        lax.ppermute(part, DEV, [(i, (i + step) % count) for i in range(count)]) if step else part
        for step, part in enumerate(dep_first)
    ]
    spread = chip_spread(att_stack, ffn_chunk, factor)
    own = exchange(spread, CHIPS)
    input_grad = last_norm(me, flat, dep_first, tim_first, pd, pt, first_gain, mgrad)
    other = swapped(own)
    *partial, first_gain_grad, second_gain_grad, depth_scale_grad, time_scale_grad = unpack(True, me, own)
    dq, do, tq, to, up_g, kern_g, down_g = unpack(False, me, other, partial)
    return (
        block_out.reshape(block_shape),
        input_grad.reshape(block_shape),
        dq,
        do,
        tq,
        to,
        up_g,
        kern_g,
        down_g,
        first_gain_grad,
        second_gain_grad,
        depth_scale_grad,
        time_scale_grad,
    )


def solution(mesh):
    fine = Mesh(mesh.devices.reshape(4, 2, 2, 2, 4), ("y", "xh", "core", "xl", "z"))
    split = P(TA, DEV, None, None)
    return jax.shard_map(
        local,
        mesh=fine,
        in_specs=(split, split) + (P(),) * 11,
        out_specs=(split, split) + (P(),) * 11,
        check_vma=False,
    )
```

time: 286 us -> 297 us (1.038)
  blocking collectives: 131 us -> 61.2 us
  starting transfers between devices: 42.2 us -> 95.3 us
  waiting for transfers between devices: 10.9 us -> 38.2 us
  Pallas kernels: 81.8 us -> 93.5 us
  local copies, waits for them, and re-layouts: 15.5 us -> 5.58 us
    all_to_all x6 -> x3, blocking collectives: 131 us -> 61.2 us  [exchange(): lax.all_to_all(values, axes, split_axis=0, concat_axis=0, tiled=True)]
    ppermute x6 -> x19, starting transfers between devices: 3.97 us -> 32.5 us  [the longest x15 28.1 us: local(): lax.ppermute(part, DEV, [(i, (i + step) % count) for i in range(count)])]
    all_to_all x4 -> x7, starting transfers between devices: 24.1 us -> 48.1 us  [exchange(): lax.all_to_all(values, axes, split_axis=0, concat_axis=0, tiled=True)]
    all_to_all x4 -> x7, waiting for transfers between devices: 9.61 us -> 26.8 us  [exchange(): lax.all_to_all(values, axes, split_axis=0, concat_axis=0, tiled=True)]
    pallas_call x7 -> x10, Pallas kernels: 42.3 us -> 54.8 us  [the longest x2 20.8 us: attend_back(): pl.pallas_call(functools.partial(attend_back_kernel, count, deals), out_s...]
    ppermute x6 -> x19, waiting for transfers between devices: 0.89 us -> 6.44 us  [the longest x15 6.43 us: local(): lax.ppermute(part, DEV, [(i, (i + step) % count) for i in range(count)])]
    squeeze x4 -> x0, local copies, waits for them, and re-layouts: 4.38 us -> none  [swapped(): lax.dynamic_index_in_dim(halves, 1 - core_index, 0, keepdims=False)]
    reshape x4 -> x0, local copies, waits for them, and re-layouts: 4.24 us -> none  [the longest x1 1.68 us: local(): kern_sum.reshape(3, 3, 3, HID)]
  transfers between devices with their start and end apart: 14 -> 30, of which waited for: 6 -> 13; matrix products, arithmetic and copies ran while one was open for 2% -> 0% of each run, Pallas kernels for 11% -> 16%
where the time goes in v1:
time: 297 us; the launch traced here: 296 us
  starting transfers between devices  95.3 us (32%)
  Pallas kernels  93.5 us (31%)
  blocking collectives  61.2 us (21%)
  waiting for transfers between devices  38.2 us (13%)
  local copies, waits for them, and re-layouts  5.58 us (2%)
    all_to_all x3, blocking collectives, exchange(): lax.all_to_all(values, axes, split_axis=0, concat_axis=0, tiled=True)  61.2 us
    all_to_all x7, starting transfers between devices, exchange(): lax.all_to_all(values, axes, split_axis=0, concat_axis=0, tiled=True)  48.1 us
    pallas_call x1, Pallas kernels, feed_forward(): pl.pallas_call(feed_kernel, grid=(STEPS,), out_shape=(shape((ROWS, C)), s...  31.6 us
    ppermute x15, starting transfers between devices, local(): lax.ppermute(part, DEV, [(i, (i + step) % count) for i in range(count)])  28.1 us
    all_to_all x7, waiting for transfers between devices, exchange(): lax.all_to_all(values, axes, split_axis=0, concat_axis=0, tiled=True)  26.8 us
    pallas_call x2, Pallas kernels, attend_back(): pl.pallas_call(functools.partial(attend_back_kernel, count, deals), out_s...  20.8 us
    pallas_call x2, Pallas kernels, attend(): pl.pallas_call(functools.partial(attend_kernel, count), out_shape=tuple((...  10.4 us
    pallas_call x2, Pallas kernels, unpack(): pl.pallas_call(functools.partial(unpack_kernel, own), out_shape=tuple(out...  10.1 us
  transfers between devices with their start and end apart: 30, of which 13 were waited for; matrix products, arithmetic and copies ran while one was open for 0% of the time, Pallas kernels for 16%

profile of v1, /device:TPU:1, one launch (start us, length us, event | category | flops | bytes accessed | tf_op | source)
XLA Modules:
  0.0 295.5 jit_solution(17012110260722345624)
XLA Ops:
  3.2 12.9 %all_to_all.50.refs_0_.refs_1_ = bf16[8,40,384]{2,1,0:T(8,128)(2,1)} all-to-all(bf16[8,40,384]{2,1,0:T(8,128)(2,1)} %get-tuple-element.76), channel_id=1, replica_groups=mesh['y'=4,'xh'=2,'core'=2,'xl'=2,'z'=4] {'xl','z'}, dimensions={0} | all-to-all | bytes 491520 | tf_op jit(solution)/shard_map/all_to_all | solution.py:718
  16.1 8.7 %all-to-all-start.1 = ((bf16[16,24,384]{2,1,0:T(8,128)(2,1)}), bf16[16,24,384]{2,1,0:T(8,128)(2,1)S(1)}, u32[]{:S(2)}, u32[]{:S(2)}) async-start(bf16[16,24,384]{2,1,0:T(8,128)(2,1)} %get-tuple-element.77), calls=%async_computation.1 | async-start | bytes 589824 | tf_op jit(solution)/shard_map/all_to_all | solution.py:718
  24.8 5.0 %shard_map.265 = (bf16[8,40,384]{2,1,0:T(8,128)(2,1)}, bf16[320,1152]{1,0:T(8,128)(2,1)}, bf16[320,384]{1,0:T(8,128)(2,1)}) custom-call(bf16[8,40,384]{2,1,0:T(8,128)(2,1)} %all_to_all.50.refs_0_.refs_1_, bf16[384,1152]{1,0:T(8,128)(2,1)} %refs_5_.2, bf16[384,384]{1,0:T(8,128)(2,1)} %refs_6_.2, f32[6]{0:T(128)} %refs_7_.2, ...), custom_call_target="tpu_custom_call" | custom-call | tf_op jit(solution)/shard_map/pallas_call | solution.py:186
  29.9 3.9 %all-to-all-done.1.refs_0_.refs_1_ = bf16[16,24,384]{2,1,0:T(8,128)(2,1)S(1)} async-done(((bf16[16,24,384]{2,1,0:T(8,128)(2,1)}), bf16[16,24,384]{2,1,0:T(8,128)(2,1)S(1)}, u32[]{:S(2)}, u32[]{:S(2)}) %all-to-all-start.1) | async-done | bytes 294944 | tf_op jit(solution)/shard_map/all_to_all | solution.py:718
  33.8 3.4 %all-to-all-start.2 = ((bf16[8,40,384]{2,1,0:T(8,128)(2,1)}), bf16[8,40,384]{2,1,0:T(8,128)(2,1)S(1)}, u32[]{:S(2)}, u32[]{:S(2)}) async-start(bf16[8,40,384]{2,1,0:T(8,128)(2,1)} %get-tuple-element.80), calls=%async_computation.2 | async-start | bytes 491520 | tf_op jit(solution)/shard_map/all_to_all | solution.py:718
  37.2 5.4 %shard_map.264 = (bf16[16,24,384]{2,1,0:T(8,128)(2,1)}, bf16[384,1152]{1,0:T(8,128)(2,1)}, bf16[384,384]{1,0:T(8,128)(2,1)}) custom-call(bf16[16,24,384]{2,1,0:T(8,128)(2,1)} %copy-done.3, bf16[384,1152]{1,0:T(8,128)(2,1)} %refs_5_.3, bf16[384,384]{1,0:T(8,128)(2,1)} %refs_6_.3, f32[6]{0:T(128)} %refs_7_.3, s32[384,1]{1,0:T(8,128)} %constant.38.refs_4_.refs_8_, ...), custom_call_target="tpu_custom_call" | custom-call | tf_op jit(solution)/shard_map/pallas_call | solution.py:186
  43.2 5.5 %all-to-all-start.3 = ((bf16[16,24,384]{2,1,0:T(8,128)(2,1)}), bf16[16,24,384]{2,1,0:T(8,128)(2,1)S(1)}, u32[]{:S(2)}, u32[]{:S(2)}) async-start(bf16[16,24,384]{2,1,0:T(8,128)(2,1)} %get-tuple-element.81), calls=%async_computation.3 | async-start | bytes 589824 | tf_op jit(solution)/shard_map/all_to_all | solution.py:718
  50.8 4.9 %collective-permute-start = (bf16[144,384]{1,0:T(8,128)(2,1)S(1)}, bf16[144,384]{1,0:T(8,128)(2,1)S(1)}, u32[]{:S(2)}, u32[]{:S(2)}) collective-permute-start(bf16[144,384]{1,0:T(8,128)(2,1)S(1)} %get-tuple-element.138), channel_id=1, source_target_pairs={{0,8},{8,16},{16,24},{24,32},{32,40},{40,48},{48,56},{56,64},{64,7... | collective-permute-start | bytes 331784 | tf_op jit(solution)/shard_map/ppermute | solution.py:728
  60.8 2.9 collective-permute-start.3
  63.7 4.7 %collective-permute-start.2 = (bf16[288,384]{1,0:T(8,128)(2,1)}, bf16[288,384]{1,0:T(8,128)(2,1)S(1)}, u32[]{:S(2)}, u32[]{:S(2)}) collective-permute-start(bf16[288,384]{1,0:T(8,128)(2,1)} %middle.1.mid_ref), channel_id=1, source_target_pairs={{0,8},{8,16},{16,24},{24,32},{32,40},{40,48},{48,56},{56,64},{64,7... | collective-permute-start | bytes 663560 | tf_op jit(solution)/shard_map/ppermute | solution.py:732
  72.3 31.6 %feed_forward.1 = (bf16[288,384]{1,0:T(8,128)(2,1)}, f32[288,384]{1,0:T(8,128)}, bf16[2,4832,128]{2,1,0:T(8,128)(2,1)}, bf16[16,24,384]{2,1,0:T(8,128)(2,1)}, bf16[8,40,384]{2,1,0:T(8,128)(2,1)}) custom-call(bf16[288,384]{1,0:T(8,128)(2,1)} %copy-done.12, bf16[288,384]{1,0:T(8,128)(2,1)} %middle.1.mid_ref, bf16[288,384]{1,0:T(8,128)(2,1)} %copy-done.11, ...), custom_call_target="tpu_custom_call" | custom-call | tf_op jit(solution)/shard_map/feed_forward/pallas_call | solution.py:469
  103.9 10.1 %all_to_all.51.refs_0_ = bf16[8,40,384]{2,1,0:T(8,128)(2,1)} all-to-all(bf16[8,40,384]{2,1,0:T(8,128)(2,1)} %get-tuple-element.88), channel_id=1, replica_groups=mesh['y'=4,'xh'=2,'core'=2,'xl'=2,'z'=4] {'xl','z'}, dimensions={0} | all-to-all | bytes 491520 | tf_op jit(solution)/shard_map/all_to_all | solution.py:718
  114.0 11.7 %all-to-all-start.5 = ((bf16[16,24,384]{2,1,0:T(8,128)(2,1)}), bf16[16,24,384]{2,1,0:T(8,128)(2,1)S(1)}, u32[]{:S(2)}, u32[]{:S(2)}) async-start(bf16[16,24,384]{2,1,0:T(8,128)(2,1)} %get-tuple-element.94), calls=%async_computation.5 | async-start | bytes 589824 | tf_op jit(solution)/shard_map/all_to_all | solution.py:718
  127.8 3.7 %shard_map.267 = bf16[5120,128]{1,0:T(8,128)(2,1)} custom-call(s32[3]{0:T(128)} %pad_add_fusion.refs_2_.me_ref, bf16[2,4832,128]{2,1,0:T(8,128)(2,1)} %get-tuple-element.92.refs_0_, bf16[2,4832,128]{2,1,0:T(8,128)(2,1)} %copy-done.4), custom_call_target="tpu_custom_call" | custom-call | tf_op jit(solution)/shard_map/pallas_call | solution.py:557
  131.5 3.2 %all-to-all-done.5.refs_0_ = bf16[16,24,384]{2,1,0:T(8,128)(2,1)S(1)} async-done(((bf16[16,24,384]{2,1,0:T(8,128)(2,1)}), bf16[16,24,384]{2,1,0:T(8,128)(2,1)S(1)}, u32[]{:S(2)}, u32[]{:S(2)}) %all-to-all-start.5) | async-done | bytes 294944 | tf_op jit(solution)/shard_map/all_to_all | solution.py:718
  134.7 5.4 %all-to-all-start.6 = ((bf16[64,80,128]{2,1,0:T(8,128)(2,1)}), bf16[64,80,128]{2,1,0:T(8,128)(2,1)S(1)}, u32[]{:S(2)}, u32[]{:S(2)}) async-start(bf16[64,80,128]{2,1,0:T(8,128)(2,1)} %bitcast.13), calls=%async_computation.6 | async-start | bytes 2621440 | tf_op jit(solution)/shard_map/all_to_all | solution.py:718
  140.1 10.2 %shard_map.266 = (bf16[8,40,384]{2,1,0:T(8,128)(2,1)}, bf16[2,2336,128]{2,1,0:T(8,128)(2,1)}) custom-call(bf16[8,40,384]{2,1,0:T(8,128)(2,1)} %all_to_all.51.refs_0_, bf16[8,40,384]{2,1,0:T(8,128)(2,1)} %all_to_all.50.refs_0_.refs_1_, s32[3]{0:T(128)} %pad_add_fusion.refs_2_.me_ref, bf16[320,1152]{1,0:T(8,128)(2,1)} %get-tuple-element.89.refs_3_, ...), custom_call_target="tpu_custom_call" | custom-call | tf_op jit(solution)/shard_map/pallas_call | solution.py:287
  150.9 10.6 %shard_map.268 = (bf16[24,384]{1,0:T(8,128)(2,1)}, bf16[24,384]{1,0:T(8,128)(2,1)}, bf16[24,384]{1,0:T(8,128)(2,1)}, bf16[24,384]{1,0:T(8,128)(2,1)}, bf16[24,38...) custom-call(bf16[16,24,384]{2,1,0:T(8,128)(2,1)} %copy-done.6, ...), custom_call_target="tpu_custom_call" | custom-call | tf_op jit(solution)/shard_map/pallas_call | solution.py:287
  161.7 4.8 %all-to-all-start.7 = ((bf16[8,40,384]{2,1,0:T(8,128)(2,1)}), bf16[8,40,384]{2,1,0:T(8,128)(2,1)S(1)}, u32[]{:S(2)}, u32[]{:S(2)}) async-start(bf16[8,40,384]{2,1,0:T(8,128)(2,1)} %get-tuple-element.96), calls=%async_computation.7 | async-start | bytes 491520 | tf_op jit(solution)/shard_map/all_to_all | solution.py:718
  167.6 3.6 %shard_map.269 = bf16[5120,128]{1,0:T(8,128)(2,1)} custom-call(s32[3]{0:T(128)} %pad_add_fusion.refs_2_.me_ref, bf16[2,2336,128]{2,1,0:T(8,128)(2,1)} %get-tuple-element.115.refs_0_, bf16[2,2336,128]{2,1,0:T(8,128)(2,1)} %collective-permute-done.20.refs_1_, bf16[2,2336,128]{2,1,0:T(8,128)(2,1)} %get-tuple-element.116.refs_2_, bf16[2,2336,128]{2,1,0:T(8,128)(2,1)} %copy-done.5), custom_call_target="tpu_custom_call" | custom-call | tf_op jit(solution)/shard_map/pallas_call | solution.py:557
  172.6 8.5 %all-to-all-start.8 = ((bf16[64,80,128]{2,1,0:T(8,128)(2,1)}), bf16[64,80,128]{2,1,0:T(8,128)(2,1)S(1)}, u32[]{:S(2)}, u32[]{:S(2)}) async-start(bf16[64,80,128]{2,1,0:T(8,128)(2,1)} %bitcast.14), calls=%async_computation.8 | async-start | bytes 2621440 | tf_op jit(solution)/shard_map/all_to_all | solution.py:718
  183.4 17.6 %all-to-all-done.8.in_ref = bf16[64,80,128]{2,1,0:T(8,128)(2,1)S(1)} async-done(((bf16[64,80,128]{2,1,0:T(8,128)(2,1)}), bf16[64,80,128]{2,1,0:T(8,128)(2,1)S(1)}, u32[]{:S(2)}, u32[]{:S(2)}) %all-to-all-start.8) | async-done | bytes 1310752 | tf_op jit(solution)/shard_map/all_to_all | solution.py:718
  202.0 3.4 %chip_spread.1 = bf16[64,160,128]{2,1,0:T(8,128)(2,1)} custom-call(bf16[64,80,128]{2,1,0:T(8,128)(2,1)} %copy-done.2, bf16[80,128]{1,0:T(8,128)(2,1)} %chip_sum.1.other_ref), custom_call_target="tpu_custom_call" | custom-call | tf_op jit(solution)/shard_map/chip_spread/pallas_call | solution.py:604
  205.5 38.2 %all_to_all.52.in_ref = bf16[64,160,128]{2,1,0:T(8,128)(2,1)S(1)} all-to-all(bf16[64,160,128]{2,1,0:T(8,128)(2,1)} %chip_spread.1), channel_id=1, replica_groups=mesh['y'=4,'xh'=2,'core'=2,'xl'=2,'z'=4] {'y','xh','xl','z'}, dimensions={0} | all-to-all | bytes 5242880 | tf_op jit(solution)/shard_map/all_to_all | solution.py:718
  243.7 3.6 %collective-permute-start.22 = (bf16[64,160,128]{2,1,0:T(8,128)(2,1)S(1)}, bf16[64,160,128]{2,1,0:T(8,128)(2,1)}, u32[]{:S(2)}, u32[]{:S(2)}) collective-permute-start(bf16[64,160,128]{2,1,0:T(8,128)(2,1)S(1)} %all_to_all.52.in_ref), channel_id=1, source_target_pairs={{0,8},{8,0},{1,9},{9,1},{2,10},{10,2},{3,11},{11,3},{4,12},{12,4},... | collective-permute-start | bytes 7864328 | tf_op jit(solution)/shard_map/ppermute | solution.py:553
  251.9 4.7 %collective-permute-start.9 = (bf16[24,384]{1,0:T(8,128)(2,1)S(1)}, bf16[24,384]{1,0:T(8,128)(2,1)S(1)}, u32[]{:S(2)}, u32[]{:S(2)}) collective-permute-start(bf16[24,384]{1,0:T(8,128)(2,1)S(1)} %copy-done.40), channel_id=1, source_target_pairs={{0,40},{8,48},{16,56},{24,64},{32,72},{40,80},{48,88},{56,96},{64,... | collective-permute-start | bytes 55304 | tf_op jit(solution)/shard_map/ppermute | solution.py:756
  260.3 4.9 %collective-permute-start.13 = (bf16[24,384]{1,0:T(8,128)(2,1)S(1)}, bf16[24,384]{1,0:T(8,128)(2,1)S(1)}, u32[]{:S(2)}, u32[]{:S(2)}) collective-permute-start(bf16[24,384]{1,0:T(8,128)(2,1)S(1)} %copy-done.36), channel_id=1, source_target_pairs={{0,72},{8,80},{16,88},{24,96},{32,104},{40,112},{48,120},{56,0},{6... | collective-permute-start | bytes 55304 | tf_op jit(solution)/shard_map/ppermute | solution.py:756
  270.0 3.8 %collective-permute-start.17 = (bf16[24,384]{1,0:T(8,128)(2,1)S(1)}, bf16[24,384]{1,0:T(8,128)(2,1)S(1)}, u32[]{:S(2)}, u32[]{:S(2)}) collective-permute-start(bf16[24,384]{1,0:T(8,128)(2,1)S(1)} %copy-done.32), channel_id=1, source_target_pairs={{0,104},{8,112},{16,120},{24,0},{32,8},{40,16},{48,24},{56,32},{64... | collective-permute-start | bytes 55304 | tf_op jit(solution)/shard_map/ppermute | solution.py:756
  273.8 3.5 %collective-permute-start.18 = (bf16[24,384]{1,0:T(8,128)(2,1)S(1)}, bf16[24,384]{1,0:T(8,128)(2,1)S(1)}, u32[]{:S(2)}, u32[]{:S(2)}) collective-permute-start(bf16[24,384]{1,0:T(8,128)(2,1)S(1)} %copy-done.31), channel_id=1, source_target_pairs={{0,112},{8,120},{16,0},{24,8},{32,16},{40,24},{48,32},{56,40},{64,... | collective-permute-start | bytes 55304 | tf_op jit(solution)/shard_map/ppermute | solution.py:756
  278.2 3.9 %collective-permute-done.19.rest_15_ = bf16[24,384]{1,0:T(8,128)(2,1)S(1)} collective-permute-done((bf16[24,384]{1,0:T(8,128)(2,1)S(1)}, bf16[24,384]{1,0:T(8,128)(2,1)S(1)}, u32[]{:S(2)}, u32[]{:S(2)}) %collective-permute-start.19) | collective-permute-done | bytes 18464 | tf_op jit(solution)/shard_map/ppermute | solution.py:756
  285.5 5.1 %unpack_own.1 = (f32[384,1152]{1,0:T(8,128)}, f32[384,384]{1,0:T(8,128)}, f32[384,1152]{1,0:T(8,128)}, f32[384,384]{1,0:T(8,128)}, f32[384,1536]{1,0:T(8,128)}, ...) custom-call(s32[3]{0:T(128)} %pad_add_fusion.refs_2_.me_ref, ...), custom_call_target="tpu_custom_call" | custom-call | tf_op jit(solution)/shard_map/unpack_own/pallas_call | solution.py:681
  290.6 4.9 %unpack_other.1 = (f32[384,1152]{1,0:T(8,128)}, f32[384,384]{1,0:T(8,128)}, f32[384,1152]{1,0:T(8,128)}, f32[384,384]{1,0:T(8,128)}, f32[384,1536]{1,0:T(8,128)}...) custom-call(s32[3]{0:T(128)} %pad_add_fusion.refs_2_.me_ref, ...), custom_call_target="tpu_custom_call", output_to_operand_aliasing={{0}: (2, {}), {1}: (3, {}), {2}: (4, {}), {3}: (5, {}), {4}... | custom-call | tf_op jit(solution)/shard_map/unpack_other/pallas_call | solution.py:681
  (137 shorter events, 40.0 us)
Async XLA Ops:
  16.1 17.7 %all-to-all-start.1 = ((bf16[16,24,384]{2,1,0:T(8,128)(2,1)}), bf16[16,24,384]{2,1,0:T(8,128)(2,1)S(1)}, u32[]{:S(2)}, u32[]{:S(2)}) async-start(bf16[16,24,384]{2,1,0:T(8,128)(2,1)} %get-tuple-element.77), calls=%async_computation.1 | async-start | bytes 589824 | tf_op jit(solution)/shard_map/all_to_all | solution.py:718
  33.8 9.4 %all-to-all-start.2 = ((bf16[8,40,384]{2,1,0:T(8,128)(2,1)}), bf16[8,40,384]{2,1,0:T(8,128)(2,1)S(1)}, u32[]{:S(2)}, u32[]{:S(2)}) async-start(bf16[8,40,384]{2,1,0:T(8,128)(2,1)} %get-tuple-element.80), calls=%async_computation.2 | async-start | bytes 491520 | tf_op jit(solution)/shard_map/all_to_all | solution.py:718
  43.2 14.5 %all-to-all-start.3 = ((bf16[16,24,384]{2,1,0:T(8,128)(2,1)}), bf16[16,24,384]{2,1,0:T(8,128)(2,1)S(1)}, u32[]{:S(2)}, u32[]{:S(2)}) async-start(bf16[16,24,384]{2,1,0:T(8,128)(2,1)} %get-tuple-element.81), calls=%async_computation.3 | async-start | bytes 589824 | tf_op jit(solution)/shard_map/all_to_all | solution.py:718
  48.7 8.6 %collective-permute-start.1 = (bf16[144,384]{1,0:T(8,128)(2,1)S(1)}, bf16[144,384]{1,0:T(8,128)(2,1)S(1)}, u32[]{:S(2)}, u32[]{:S(2)}) collective-permute-start(bf16[144,384]{1,0:T(8,128)(2,1)S(1)} %get-tuple-element.137), channel_id=1, source_target_pairs={{8,0},{16,8},{24,16},{32,24},{40,32},{48,40},{56,48},{64,56},{72,6... | collective-permute-start | bytes 331784 | tf_op jit(solution)/shard_map/ppermute | solution.py:729
  50.8 6.7 %collective-permute-start = (bf16[144,384]{1,0:T(8,128)(2,1)S(1)}, bf16[144,384]{1,0:T(8,128)(2,1)S(1)}, u32[]{:S(2)}, u32[]{:S(2)}) collective-permute-start(bf16[144,384]{1,0:T(8,128)(2,1)S(1)} %get-tuple-element.138), channel_id=1, source_target_pairs={{0,8},{8,16},{16,24},{24,32},{32,40},{40,48},{48,56},{56,64},{64,7... | collective-permute-start | bytes 331784 | tf_op jit(solution)/shard_map/ppermute | solution.py:728
  60.8 9.5 %collective-permute-start.3 = (bf16[288,384]{1,0:T(8,128)(2,1)}, bf16[288,384]{1,0:T(8,128)(2,1)S(1)}, u32[]{:S(2)}, u32[]{:S(2)}) collective-permute-start(bf16[288,384]{1,0:T(8,128)(2,1)} %middle.1.mid_ref), channel_id=1, source_target_pairs={{8,0},{16,8},{24,16},{32,24},{40,32},{48,40},{56,48},{64,56},{72,6... | collective-permute-start | bytes 663560 | tf_op jit(solution)/shard_map/ppermute | solution.py:733
  63.7 7.8 %collective-permute-start.2 = (bf16[288,384]{1,0:T(8,128)(2,1)}, bf16[288,384]{1,0:T(8,128)(2,1)S(1)}, u32[]{:S(2)}, u32[]{:S(2)}) collective-permute-start(bf16[288,384]{1,0:T(8,128)(2,1)} %middle.1.mid_ref), channel_id=1, source_target_pairs={{0,8},{8,16},{16,24},{24,32},{32,40},{40,48},{48,56},{56,64},{64,7... | collective-permute-start | bytes 663560 | tf_op jit(solution)/shard_map/ppermute | solution.py:732
  103.9 22.5 %collective-permute-start.4 = (bf16[2,4832,128]{2,1,0:T(8,128)(2,1)}, bf16[2,4832,128]{2,1,0:T(8,128)(2,1)S(1)}, u32[]{:S(2)}, u32[]{:S(2)}) collective-permute-start(bf16[2,4832,128]{2,1,0:T(8,128)(2,1)} %get-tuple-element.92.refs_0_), channel_id=1, source_target_pairs={{0,8},{8,0},{1,9},{9,1},{2,10},{10,2},{3,11},{11,3},{4,12},{12,4},... | collective-permute-start | bytes 7421960 | tf_op jit(solution)/shard_map/ppermute | solution.py:553
  114.0 20.7 %all-to-all-start.5 = ((bf16[16,24,384]{2,1,0:T(8,128)(2,1)}), bf16[16,24,384]{2,1,0:T(8,128)(2,1)S(1)}, u32[]{:S(2)}, u32[]{:S(2)}) async-start(bf16[16,24,384]{2,1,0:T(8,128)(2,1)} %get-tuple-element.94), calls=%async_computation.5 | async-start | bytes 589824 | tf_op jit(solution)/shard_map/all_to_all | solution.py:718
  134.7 27.0 %all-to-all-start.6 = ((bf16[64,80,128]{2,1,0:T(8,128)(2,1)}), bf16[64,80,128]{2,1,0:T(8,128)(2,1)S(1)}, u32[]{:S(2)}, u32[]{:S(2)}) async-start(bf16[64,80,128]{2,1,0:T(8,128)(2,1)} %bitcast.13), calls=%async_computation.6 | async-start | bytes 2621440 | tf_op jit(solution)/shard_map/all_to_all | solution.py:718
  150.3 16.2 %collective-permute-start.21 = (bf16[2,2336,128]{2,1,0:T(8,128)(2,1)}, bf16[2,2336,128]{2,1,0:T(8,128)(2,1)S(1)}, u32[]{:S(2)}, u32[]{:S(2)}) collective-permute-start(bf16[2,2336,128]{2,1,0:T(8,128)(2,1)} %get-tuple-element.116.refs_2_), channel_id=1, source_target_pairs={{0,8},{8,0},{1,9},{9,1},{2,10},{10,2},{3,11},{11,3},{4,12},{12,4},... | collective-permute-start | bytes 3588104 | tf_op jit(solution)/shard_map/ppermute | solution.py:553
  161.6 5.0 %collective-permute-start.20 = (bf16[2,2336,128]{2,1,0:T(8,128)(2,1)}, bf16[2,2336,128]{2,1,0:T(8,128)(2,1)}, u32[]{:S(2)}, u32[]{:S(2)}) collective-permute-start(bf16[2,2336,128]{2,1,0:T(8,128)(2,1)} %get-tuple-element.115.refs_0_), channel_id=1, source_target_pairs={{0,8},{8,0},{1,9},{9,1},{2,10},{10,2},{3,11},{11,3},{4,12},{12,4},... | collective-permute-start | bytes 3588104 | tf_op jit(solution)/shard_map/ppermute | solution.py:553
  161.7 10.9 %all-to-all-start.7 = ((bf16[8,40,384]{2,1,0:T(8,128)(2,1)}), bf16[8,40,384]{2,1,0:T(8,128)(2,1)S(1)}, u32[]{:S(2)}, u32[]{:S(2)}) async-start(bf16[8,40,384]{2,1,0:T(8,128)(2,1)} %get-tuple-element.96), calls=%async_computation.7 | async-start | bytes 491520 | tf_op jit(solution)/shard_map/all_to_all | solution.py:718
  172.6 28.3 %all-to-all-start.8 = ((bf16[64,80,128]{2,1,0:T(8,128)(2,1)}), bf16[64,80,128]{2,1,0:T(8,128)(2,1)S(1)}, u32[]{:S(2)}, u32[]{:S(2)}) async-start(bf16[64,80,128]{2,1,0:T(8,128)(2,1)} %bitcast.14), calls=%async_computation.8 | async-start | bytes 2621440 | tf_op jit(solution)/shard_map/all_to_all | solution.py:718
  205.5 68.3 %copy-start.31 = (bf16[24,384]{1,0:T(8,128)(2,1)S(1)}, bf16[24,384]{1,0:T(8,128)(2,1)}, u32[]{:S(2)}) copy-start(bf16[24,384]{1,0:T(8,128)(2,1)} %get-tuple-element.113) | copy-start | bytes 55300
  205.5 71.8 %copy-start.30 = (bf16[24,384]{1,0:T(8,128)(2,1)S(1)}, bf16[24,384]{1,0:T(8,128)(2,1)}, u32[]{:S(2)}) copy-start(bf16[24,384]{1,0:T(8,128)(2,1)} %get-tuple-element.114) | copy-start | bytes 55300
  243.7 46.9 %collective-permute-start.22 = (bf16[64,160,128]{2,1,0:T(8,128)(2,1)S(1)}, bf16[64,160,128]{2,1,0:T(8,128)(2,1)}, u32[]{:S(2)}, u32[]{:S(2)}) collective-permute-start(bf16[64,160,128]{2,1,0:T(8,128)(2,1)S(1)} %all_to_all.52.in_ref), channel_id=1, source_target_pairs={{0,8},{8,0},{1,9},{9,1},{2,10},{10,2},{3,11},{11,3},{4,12},{12,4},... | collective-permute-start | bytes 7864328 | tf_op jit(solution)/shard_map/ppermute | solution.py:553
  247.4 4.5 %collective-permute-start.5 = (bf16[24,384]{1,0:T(8,128)(2,1)S(1)}, bf16[24,384]{1,0:T(8,128)(2,1)S(1)}, u32[]{:S(2)}, u32[]{:S(2)}) collective-permute-start(bf16[24,384]{1,0:T(8,128)(2,1)S(1)} %copy-done.44), channel_id=1, source_target_pairs={{0,8},{8,16},{16,24},{24,32},{32,40},{40,48},{48,56},{56,64},{64,7... | collective-permute-start | bytes 55304 | tf_op jit(solution)/shard_map/ppermute | solution.py:756
  247.5 9.1 %collective-permute-start.6 = (bf16[24,384]{1,0:T(8,128)(2,1)S(1)}, bf16[24,384]{1,0:T(8,128)(2,1)S(1)}, u32[]{:S(2)}, u32[]{:S(2)}) collective-permute-start(bf16[24,384]{1,0:T(8,128)(2,1)S(1)} %copy-done.43), channel_id=1, source_target_pairs={{0,16},{8,24},{16,32},{24,40},{32,48},{40,56},{48,64},{56,72},{64,... | collective-permute-start | bytes 55304 | tf_op jit(solution)/shard_map/ppermute | solution.py:756
  249.8 7.3 %collective-permute-start.7 = (bf16[24,384]{1,0:T(8,128)(2,1)S(1)}, bf16[24,384]{1,0:T(8,128)(2,1)S(1)}, u32[]{:S(2)}, u32[]{:S(2)}) collective-permute-start(bf16[24,384]{1,0:T(8,128)(2,1)S(1)} %copy-done.42), channel_id=1, source_target_pairs={{0,24},{8,32},{16,40},{24,48},{32,56},{40,64},{48,72},{56,80},{64,... | collective-permute-start | bytes 55304 | tf_op jit(solution)/shard_map/ppermute | solution.py:756
  249.8 7.8 %collective-permute-start.8 = (bf16[24,384]{1,0:T(8,128)(2,1)S(1)}, bf16[24,384]{1,0:T(8,128)(2,1)S(1)}, u32[]{:S(2)}, u32[]{:S(2)}) collective-permute-start(bf16[24,384]{1,0:T(8,128)(2,1)S(1)} %copy-done.41), channel_id=1, source_target_pairs={{0,32},{8,40},{16,48},{24,56},{32,64},{40,72},{48,80},{56,88},{64,... | collective-permute-start | bytes 55304 | tf_op jit(solution)/shard_map/ppermute | solution.py:756
  251.9 8.4 %collective-permute-start.9 = (bf16[24,384]{1,0:T(8,128)(2,1)S(1)}, bf16[24,384]{1,0:T(8,128)(2,1)S(1)}, u32[]{:S(2)}, u32[]{:S(2)}) collective-permute-start(bf16[24,384]{1,0:T(8,128)(2,1)S(1)} %copy-done.40), channel_id=1, source_target_pairs={{0,40},{8,48},{16,56},{24,64},{32,72},{40,80},{48,88},{56,96},{64,... | collective-permute-start | bytes 55304 | tf_op jit(solution)/shard_map/ppermute | solution.py:756
  256.6 8.6 %collective-permute-start.10 = (bf16[24,384]{1,0:T(8,128)(2,1)S(1)}, bf16[24,384]{1,0:T(8,128)(2,1)S(1)}, u32[]{:S(2)}, u32[]{:S(2)}) collective-permute-start(bf16[24,384]{1,0:T(8,128)(2,1)S(1)} %copy-done.39), channel_id=1, source_target_pairs={{0,48},{8,56},{16,64},{24,72},{32,80},{40,88},{48,96},{56,104},{64... | collective-permute-start | bytes 55304 | tf_op jit(solution)/shard_map/ppermute | solution.py:756
  257.1 10.8 %collective-permute-start.11 = (bf16[24,384]{1,0:T(8,128)(2,1)S(1)}, bf16[24,384]{1,0:T(8,128)(2,1)S(1)}, u32[]{:S(2)}, u32[]{:S(2)}) collective-permute-start(bf16[24,384]{1,0:T(8,128)(2,1)S(1)} %copy-done.38), channel_id=1, source_target_pairs={{0,56},{8,64},{16,72},{24,80},{32,88},{40,96},{48,104},{56,112},{6... | collective-permute-start | bytes 55304 | tf_op jit(solution)/shard_map/ppermute | solution.py:756
  257.6 10.9 %collective-permute-start.12 = (bf16[24,384]{1,0:T(8,128)(2,1)S(1)}, bf16[24,384]{1,0:T(8,128)(2,1)S(1)}, u32[]{:S(2)}, u32[]{:S(2)}) collective-permute-start(bf16[24,384]{1,0:T(8,128)(2,1)S(1)} %copy-done.37), channel_id=1, source_target_pairs={{0,64},{8,72},{16,80},{24,88},{32,96},{40,104},{48,112},{56,120},{... | collective-permute-start | bytes 55304 | tf_op jit(solution)/shard_map/ppermute | solution.py:756
  260.3 9.7 %collective-permute-start.13 = (bf16[24,384]{1,0:T(8,128)(2,1)S(1)}, bf16[24,384]{1,0:T(8,128)(2,1)S(1)}, u32[]{:S(2)}, u32[]{:S(2)}) collective-permute-start(bf16[24,384]{1,0:T(8,128)(2,1)S(1)} %copy-done.36), channel_id=1, source_target_pairs={{0,72},{8,80},{16,88},{24,96},{32,104},{40,112},{48,120},{56,0},{6... | collective-permute-start | bytes 55304 | tf_op jit(solution)/shard_map/ppermute | solution.py:756
  265.2 8.5 %collective-permute-start.14 = (bf16[24,384]{1,0:T(8,128)(2,1)S(1)}, bf16[24,384]{1,0:T(8,128)(2,1)S(1)}, u32[]{:S(2)}, u32[]{:S(2)}) collective-permute-start(bf16[24,384]{1,0:T(8,128)(2,1)S(1)} %copy-done.35), channel_id=1, source_target_pairs={{0,80},{8,88},{16,96},{24,104},{32,112},{40,120},{48,0},{56,8},{64... | collective-permute-start | bytes 55304 | tf_op jit(solution)/shard_map/ppermute | solution.py:756
  268.0 9.3 %collective-permute-start.15 = (bf16[24,384]{1,0:T(8,128)(2,1)S(1)}, bf16[24,384]{1,0:T(8,128)(2,1)S(1)}, u32[]{:S(2)}, u32[]{:S(2)}) collective-permute-start(bf16[24,384]{1,0:T(8,128)(2,1)S(1)} %copy-done.34), channel_id=1, source_target_pairs={{0,88},{8,96},{16,104},{24,112},{32,120},{40,0},{48,8},{56,16},{64... | collective-permute-start | bytes 55304 | tf_op jit(solution)/shard_map/ppermute | solution.py:756
  268.5 8.9 %collective-permute-start.16 = (bf16[24,384]{1,0:T(8,128)(2,1)S(1)}, bf16[24,384]{1,0:T(8,128)(2,1)S(1)}, u32[]{:S(2)}, u32[]{:S(2)}) collective-permute-start(bf16[24,384]{1,0:T(8,128)(2,1)S(1)} %copy-done.33), channel_id=1, source_target_pairs={{0,96},{8,104},{16,112},{24,120},{32,0},{40,8},{48,16},{56,24},{64... | collective-permute-start | bytes 55304 | tf_op jit(solution)/shard_map/ppermute | solution.py:756
  270.0 7.4 %collective-permute-start.17 = (bf16[24,384]{1,0:T(8,128)(2,1)S(1)}, bf16[24,384]{1,0:T(8,128)(2,1)S(1)}, u32[]{:S(2)}, u32[]{:S(2)}) collective-permute-start(bf16[24,384]{1,0:T(8,128)(2,1)S(1)} %copy-done.32), channel_id=1, source_target_pairs={{0,104},{8,112},{16,120},{24,0},{32,8},{40,16},{48,24},{56,32},{64... | collective-permute-start | bytes 55304 | tf_op jit(solution)/shard_map/ppermute | solution.py:756
  273.8 4.4 %collective-permute-start.18 = (bf16[24,384]{1,0:T(8,128)(2,1)S(1)}, bf16[24,384]{1,0:T(8,128)(2,1)S(1)}, u32[]{:S(2)}, u32[]{:S(2)}) collective-permute-start(bf16[24,384]{1,0:T(8,128)(2,1)S(1)} %copy-done.31), channel_id=1, source_target_pairs={{0,112},{8,120},{16,0},{24,8},{32,16},{40,24},{48,32},{56,40},{64,... | collective-permute-start | bytes 55304 | tf_op jit(solution)/shard_map/ppermute | solution.py:756
  277.3 4.8 %collective-permute-start.19 = (bf16[24,384]{1,0:T(8,128)(2,1)S(1)}, bf16[24,384]{1,0:T(8,128)(2,1)S(1)}, u32[]{:S(2)}, u32[]{:S(2)}) collective-permute-start(bf16[24,384]{1,0:T(8,128)(2,1)S(1)} %copy-done.30), channel_id=1, source_target_pairs={{0,120},{8,0},{16,8},{24,16},{32,24},{40,32},{48,40},{56,48},{64,5... | collective-permute-start | bytes 55304 | tf_op jit(solution)/shard_map/ppermute | solution.py:756
  (43 other events, 1039.4 us)

commit v2 on v1

v2 whole, which is shorter than its diff:
```python
import functools
import math

import jax
import jax.numpy as jnp
from jax import lax
from jax.experimental import pallas as pl
from jax.experimental.pallas import tpu as pltpu
from jax.sharding import Mesh
from jax.sharding import PartitionSpec as P


C = 384
HID = 1536
PW = 24
CELLS = 144
ROWS = 288
BLOCK = 256
STEPS = HID // BLOCK
PAD = 192
DEV = ("y", "xh", "core")
TA = ("xl", "z")
CHIPS = ("y", "xh", "xl", "z")
COPIES = 64
CHUNK = 152
F32 = jnp.float32
BF16 = jnp.bfloat16
EPS = 1e-5


def piece_of(row, size):
    return (row * (65536 // size + 1)) >> 16


def spread(size, cells):
    row = lax.broadcasted_iota(jnp.int32, (size * (CELLS // cells), 1), 0)
    owner = piece_of(row, size)
    k = row - size * owner
    token = k + cells * owner + jnp.where(k >= cells, CELLS - cells, 0)
    token = jnp.where(k < 2 * cells, token, -1)
    lane = lax.broadcasted_iota(jnp.int32, (row.shape[0], ROWS), 1)
    return jnp.where(token == lane, 1.0, 0.0).astype(BF16)


def spread_depth():
    return spread(24, 9)


def spread_time():
    return spread(40, 18)


def same_group(rows):
    def group(index):
        if rows == 320:
            return index - 40 * piece_of(index, 40)
        k = index - 24 * piece_of(index, 24)
        return jnp.where(k >= 9, k - 9, k) + jnp.where(k >= 18, 9, 0)

    left = group(lax.broadcasted_iota(jnp.int32, (rows, 1), 0))
    right = group(lax.broadcasted_iota(jnp.int32, (1, rows), 1))
    return jnp.where(left == right, 1.0, 0.0)


def dot(left, right, dims=((1,), (0,)), precision=None):
    return lax.dot_general(
        left, right, (dims, ((), ())), preferred_element_type=F32, precision=precision
    )


def norm_parts(values):
    centered = values - jnp.mean(values, axis=-1, keepdims=True)
    inverse = lax.rsqrt(jnp.mean(centered * centered, axis=-1, keepdims=True) + EPS)
    return centered * inverse, inverse


def norm_back(scaled, inverse, grads):
    mean = jnp.mean(grads, axis=-1, keepdims=True)
    along = jnp.mean(grads * scaled, axis=-1, keepdims=True)
    return (grads - mean - scaled * along) * inverse


def vmem(count):
    return [pl.BlockSpec(memory_space=pltpu.VMEM)] * count


SMEM = [pl.BlockSpec(memory_space=pltpu.SMEM)]


def shape(dims, kind=BF16):
    return jax.ShapeDtypeStruct(dims, kind)


def deal(values, turn, mask, part_refs, hold_ref):
    count = len(part_refs)
    hold_ref[...] = values.reshape(count, values.shape[0] // count, C)
    for step, ref in enumerate(part_refs):
        ref[...] = hold_ref[(turn + step) & mask].astype(BF16)


def row_of(ref):
    return ref[...].reshape(1, ref.shape[0])


def first_kernel(tok_ref, gain_ref, dep_ref, tim_ref):
    scaled, _ = norm_parts(tok_ref[...].astype(F32))
    normed = (scaled * row_of(gain_ref)).astype(BF16)
    dep_ref[...] = dot(spread_depth(), normed).reshape(16, 24, C).astype(BF16)
    tim_ref[...] = dot(spread_time(), normed).reshape(8, 40, C).astype(BF16)


def first_norm(tokens, gain):
    return pl.pallas_call(
        first_kernel,
        out_shape=(shape((16, 24, C)), shape((8, 40, C))),
        in_specs=vmem(2),
        out_specs=tuple(vmem(2)),
        name="first_norm",
    )(tokens, gain)


ATT = 2304


def lane_is_low():
    return lax.broadcasted_iota(jnp.int32, (1, 128), 1) < 64


def head_ones():
    row = lax.broadcasted_iota(jnp.int32, (128, 128), 0) < 64
    col = lax.broadcasted_iota(jnp.int32, (128, 128), 1) < 64
    return jnp.where(row == col, 1.0, 0.0).astype(BF16)


def head_sum(values, ones):
    high = values.astype(BF16)
    low = (values - high.astype(F32)).astype(BF16)
    return dot(high, ones) + dot(low, ones)


def joined(ref):
    count, part, _ = ref.shape
    return ref[...].astype(F32).reshape(count * part, C).astype(BF16)


def attend_kernel(in_ref, w_ref, wo_ref, scale_ref, out_ref, fields_ref, mixed_ref, same_ref):
    rowed = joined(in_ref)
    rows = rowed.shape[0]
    fields_ref[...] = dot(rowed, w_ref[...]).astype(BF16)
    same_ref[...] = same_group(rows)
    ones = head_ones()
    low = lane_is_low()
    side = jnp.ones((rows, 128), BF16)

    def one_pair(pair, _):
        at = pl.multiple_of(128 * pair, 128)
        query = fields_ref[:, pl.ds(at, 128)].astype(F32)
        keyed = fields_ref[:, pl.ds(C + at, 128)].astype(F32)
        valued = fields_ref[:, pl.ds(2 * C + at, 128)]
        query = query * lax.rsqrt(head_sum(query * query, ones) + 1e-6)
        keyed = (keyed * lax.rsqrt(head_sum(keyed * keyed, ones) + 1e-6)).astype(BF16)
        query = query * jnp.where(low, scale_ref[2 * pair], scale_ref[2 * pair + 1])
        both = jnp.concatenate([valued, side], axis=1)
        results = []
        for half in range(2):
            mine = low if half == 0 else jnp.logical_not(low)
            scores = dot(jnp.where(mine, query, 0.0).astype(BF16), keyed, ((1,), (1,)))
            weights = (jnp.exp(scores) * same_ref[...]).astype(BF16)
            sums = dot(weights, both)
            results.append(sums[:, :128] / sums[:, 128:])
        mixed_ref[:, pl.ds(at, 128)] = jnp.where(low, results[0], results[1]).astype(BF16)
        return 0

    lax.fori_loop(0, 3, one_pair, 0)
    out_ref[...] = dot(mixed_ref[...], wo_ref[...]).reshape(out_ref.shape).astype(BF16)


def attend(inputs, weight, out_weight, scale):
    rows = inputs.shape[0] * inputs.shape[1]
    return pl.pallas_call(
        attend_kernel,
        out_shape=(shape(inputs.shape), shape((rows, 3 * C)), shape((rows, C))),
        in_specs=vmem(3) + SMEM,
        out_specs=tuple(vmem(3)),
        scratch_shapes=[pltpu.VMEM((rows, rows), F32)],
    )(inputs, weight, out_weight, scale)


def put_tile(ref, tile, values):
    for half in range(2):
        ref[half, 192 * tile : 192 * tile + 192, :] = values[192 * half : 192 * half + 192].astype(BF16)


def wide(values, lanes):
    return jnp.concatenate([values] * 3, axis=1)[:, :lanes]


def attend_back_kernel(grad_ref, in_ref, me_ref, fields_ref, mixed_ref, w_ref, wo_ref, scale_ref, gain_ref, *refs):
    count = in_ref.shape[0]
    out_refs, (weights_ref, small_ref, same_ref, fg_ref, cot_ref, hold_ref) = refs[:count], refs[count:]
    grads = joined(grad_ref)
    rows = grads.shape[0]
    same_ref[...] = same_group(rows)
    out_grad = dot(mixed_ref[...], grads, ((0,), (0,)))
    for tile in range(3):
        put_tile(weights_ref, 9 + tile, out_grad[:, 128 * tile : 128 * tile + 128])
    cot_ref[...] = dot(grads, wo_ref[...], ((1,), (1,))).astype(BF16)
    ones = head_ones()
    low = lane_is_low()
    side = jnp.ones((rows, 128), BF16)
    full = jnp.ones((128, 128), BF16)
    small_ref[24:32, :] = jnp.zeros((8, 128), F32)

    def one_pair(pair, _):
        at = pl.multiple_of(128 * pair, 128)
        query = fields_ref[:, pl.ds(at, 128)].astype(F32)
        keyed = fields_ref[:, pl.ds(C + at, 128)].astype(F32)
        valued = fields_ref[:, pl.ds(2 * C + at, 128)]
        query_inv = lax.rsqrt(head_sum(query * query, ones) + 1e-6)
        keyed_inv = lax.rsqrt(head_sum(keyed * keyed, ones) + 1e-6)
        query = query * query_inv
        keyed = keyed * keyed_inv
        scale = jnp.where(low, scale_ref[2 * pair], scale_ref[2 * pair + 1])
        scaled = query * scale
        keyed_short = keyed.astype(BF16)
        cot = cot_ref[:, pl.ds(at, 128)]
        along = cot.astype(F32) * mixed_ref[:, pl.ds(at, 128)].astype(F32)
        query_grad = jnp.zeros((rows, 128), F32)
        keyed_grad = jnp.zeros((rows, 128), F32)
        value_grad = jnp.zeros((rows, 128), F32)
        for half in range(2):
            mine = low if half == 0 else jnp.logical_not(low)
            delta = wide(head_sum(jnp.where(mine, along, 0.0), full), rows)
            mine_query = jnp.where(mine, scaled, 0.0).astype(BF16)
            mine_cot = jnp.where(mine, cot.astype(F32), 0.0).astype(BF16)
            mine_keyed = jnp.where(mine, keyed, 0.0).astype(BF16)
            scores = dot(mine_query, keyed_short, ((1,), (1,)))
            weights = jnp.exp(scores) * same_ref[...]
            total = dot(weights.astype(BF16), side)
            weights = weights * wide(1.0 / total, rows)
            weights_grad = dot(mine_cot, valued, ((1,), (1,)))
            scores_grad = (weights * (weights_grad - delta)).astype(BF16)
            value_grad = value_grad + dot(weights.astype(BF16), mine_cot, ((0,), (0,)))
            query_grad = query_grad + dot(scores_grad, mine_keyed)
            keyed_grad = keyed_grad + dot(scores_grad, mine_query, ((0,), (0,)))
        total = jnp.sum(query_grad * query, axis=0, keepdims=True)
        small_ref[pl.ds(24 + pair, 1), :] = head_sum(jnp.broadcast_to(total, (8, 128)), ones)[:1]
        query_grad = query_grad * scale
        query_grad = (query_grad - query * head_sum(query * query_grad, ones)) * query_inv
        keyed_grad = (keyed_grad - keyed * head_sum(keyed * keyed_grad, ones)) * keyed_inv
        fg_ref[:, pl.ds(at, 128)] = query_grad.astype(BF16)
        fg_ref[:, pl.ds(C + at, 128)] = keyed_grad.astype(BF16)
        fg_ref[:, pl.ds(2 * C + at, 128)] = value_grad.astype(BF16)
        return 0

    lax.fori_loop(0, 3, one_pair, 0)
    back = dot(fg_ref[...], w_ref[...], ((1,), (1,)))
    deal(back, me_ref[count // 8 - 1], count - 1, out_refs, hold_ref)
    rowed = joined(in_ref)
    grad = dot(rowed, fg_ref[...], ((0,), (0,)))
    for tile in range(9):
        put_tile(weights_ref, tile, grad[:, 128 * tile : 128 * tile + 128])
    gain_part = jnp.sum(back * rowed.astype(F32), axis=0, keepdims=True) / row_of(gain_ref)
    small_ref[0:24, :] = jnp.zeros((24, 128), F32)
    for tile in range(3):
        small_ref[8 * tile : 8 * tile + 1, :] = gain_part[:, 128 * tile : 128 * tile + 128]
    for half in range(2):
        weights_ref[half, ATT:, :] = small_ref[...].astype(BF16)


def attend_back(me, grads, inputs, fields, mixed, weight, out_weight, scale, gain):
    count, part, _ = inputs.shape
    rows = count * part
    outs = pl.pallas_call(
        attend_back_kernel,
        out_shape=(shape((part, C)),) * count + (shape((2, ATT + 32, 128)),),
        in_specs=vmem(2) + SMEM + vmem(4) + SMEM + vmem(1),
        out_specs=tuple(vmem(count + 1)),
        scratch_shapes=[
            pltpu.VMEM((32, 128), F32),
            pltpu.VMEM((rows, rows), F32),
            pltpu.VMEM((rows, 3 * C), BF16),
            pltpu.VMEM((rows, C), BF16),
            pltpu.VMEM((count, part, C), F32),
        ],
    )(grads, inputs, me, fields, mixed, weight, out_weight, scale, gain)
    return outs[:count], outs[count]


def middle_kernel(tok_ref, dep_ref, tim_ref, out_ref):
    total = tok_ref[...].astype(F32) + dot(spread_depth(), joined(dep_ref), ((0,), (0,)))
    out_ref[...] = (total + dot(spread_time(), joined(tim_ref), ((0,), (0,)))).astype(BF16)


def middle_of(tokens, depth, time):
    return pl.pallas_call(
        middle_kernel,
        out_shape=shape((ROWS, C)),
        in_specs=vmem(3),
        out_specs=vmem(1)[0],
        name="middle",
    )(tokens, depth, time)


STRIDE = 1600
FFN = 3 * STRIDE


def down_one(values, first):
    return jnp.where(first, 0.0, pltpu.roll(values, 1, 0))


def up_one(values, last):
    return jnp.where(last, 0.0, pltpu.roll(values, PW - 1, 0))


def act_pair(values):
    square = values * values
    inner = 0.7978845608 * values * (1.0 + 0.044715 * square)
    tanh = jnp.tanh(inner)
    half = 0.5 * (1.0 + tanh)
    slope = 0.7978845608 * (1.0 + 3.0 * 0.044715 * square)
    return values * half, half + 0.5 * values * (1.0 - tanh * tanh) * slope


def feed_kernel(
    low_ref, mid_ref, high_ref, og_low_ref, og_ref, og_high_ref, gain_ref, up_ref, kern_ref, down_ref,
    block_ref, mgrad_ref, bdep_ref, btim_ref, own_ref, hid_out, fgr_out, act_out, hgr_out,
    norm_ref, og4_ref, hid_ref, fgr_ref, act_ref, hgr_ref, ag_ref, block_acc, back_acc,
):
    step = pl.program_id(0)

    @pl.when(step == 0)
    def _():
        for at, ref in ((0, low_ref), (ROWS, mid_ref), (2 * ROWS, high_ref)):
            scaled, _ = norm_parts(ref[...].astype(F32))
            norm_ref[at : at + ROWS, :] = (scaled * row_of(gain_ref)).astype(BF16)
        og4_ref[0:CELLS, :] = og_low_ref[...]
        og4_ref[CELLS : CELLS + ROWS, :] = og_ref[...]
        og4_ref[CELLS + ROWS : 2 * ROWS, :] = og_high_ref[...]
        hid_ref[...] = jnp.zeros(hid_ref.shape, F32)
        fgr_ref[...] = jnp.zeros(fgr_ref.shape, F32)
        block_acc[...] = jnp.zeros(block_acc.shape, F32)
        back_acc[...] = jnp.zeros(back_acc.shape, F32)
        own_ref[...] = norm_ref[ROWS : 2 * ROWS, :]

    place = lax.broadcasted_iota(jnp.int32, (PW, 128), 0)
    first, last = place == 0, place == PW - 1
    short = dot(norm_ref[...], up_ref[...]).astype(BF16)
    hid_out[...] = short[CELLS : 5 * CELLS]
    hidden = short.astype(F32)
    ag_ref[...] = dot(og4_ref[...], down_ref[...], ((1,), (1,)))
    for lt in range(2):
        for piece in range(6):
            hid_ref[lt, piece * PAD + PW : piece * PAD + PW + CELLS, :] = hidden[
                piece * CELLS : (piece + 1) * CELLS, 128 * lt : 128 * lt + 128
            ]

    for lt in range(2):
        lanes = slice(128 * lt, 128 * lt + 128)

        def forward(piece, _, lt=lt, lanes=lanes):
            for i in range(6):
                acc = [None] * 3
                for a in range(3):
                    for b in range(3):
                        start = pl.multiple_of((piece + a) * PAD + PW * (i + b), 8)
                        window = hid_ref[lt, pl.ds(start, PW), :]
                        for e in range(3):
                            term = kern_ref[a, b, e : e + 1, lanes] * window
                            acc[e] = term if acc[e] is None else acc[e] + term
                filtered = acc[1] + down_one(acc[0], first) + up_one(acc[2], last)
                value, slope = act_pair(filtered)
                at = pl.multiple_of(piece * CELLS + PW * i, 8)
                grad = (ag_ref[pl.ds(at, PW), lanes] * slope).astype(BF16).astype(F32)
                fgr_ref[lt, pl.ds(pl.multiple_of(piece * PAD + PW * (i + 1), 8), PW), :] = grad
                act_ref[pl.ds(at, PW), lanes] = value
            return 0

        lax.fori_loop(0, 4, forward, 0)

        def backward(piece, sums, lt=lt, lanes=lanes):
            sums = list(sums)
            for i in range(6):
                acc = [None] * 3
                for a in range(3):
                    for b in range(3):
                        start = pl.multiple_of((piece + 2 - a) * PAD + PW * (i + 2 - b), 8)
                        window = fgr_ref[lt, pl.ds(start, PW), :]
                        for e in range(3):
                            term = kern_ref[a, b, e : e + 1, lanes] * window
                            acc[e] = term if acc[e] is None else acc[e] + term
                total = acc[1] + up_one(acc[0], last) + down_one(acc[2], first)
                hgr_ref[pl.ds(pl.multiple_of(piece * CELLS + PW * i, 8), PW), lanes] = total
            return tuple(sums)

        lax.fori_loop(0, 2, backward, ())

    for lt in range(2):
        for piece in range(2):
            at = (piece + 1) * PAD + PW
            fgr_out[piece * CELLS : piece * CELLS + CELLS, 128 * lt : 128 * lt + 128] = fgr_ref[
                lt, at : at + CELLS, :
            ].astype(BF16)
    active = act_ref[CELLS : CELLS + ROWS, :].astype(BF16)
    act_out[...] = active
    block_acc[...] += dot(active, down_ref[...])
    hidden_grad = hgr_ref[...].astype(BF16)
    hgr_out[...] = hidden_grad
    back_acc[...] += dot(hidden_grad, up_ref[...], ((1,), (1,)))

    @pl.when(step == STEPS - 1)
    def _():
        wide = mid_ref[...].astype(F32)
        block_ref[...] = (wide + block_acc[...]).astype(BF16)
        scaled, inverse = norm_parts(wide)
        back = norm_back(scaled, inverse, back_acc[...] * row_of(gain_ref))
        middle_grad = og_ref[...].astype(F32) + back
        mgrad_ref[...] = middle_grad
        short = middle_grad.astype(BF16)
        bdep_ref[...] = dot(spread_depth(), short).reshape(16, 24, C).astype(BF16)
        btim_ref[...] = dot(spread_time(), short).reshape(8, 40, C).astype(BF16)


def grads_kernel(
    og_ref, own_ref, hid_in, fgr_in, act_in, hgr_in, up_ref, gain_ref, weights_ref, hid_ref, fgr_ref, prod_acc, kgrad_ref
):
    step = pl.program_id(0)

    @pl.when(step == 0)
    def _():
        hid_ref[...] = jnp.zeros(hid_ref.shape, F32)
        prod_acc[...] = jnp.zeros(prod_acc.shape, F32)

    place = lax.broadcasted_iota(jnp.int32, (PW, 128), 0)
    first, last = place == 0, place == PW - 1
    for lt in range(2):
        lanes = slice(128 * lt, 128 * lt + 128)
        fgr_ref[lt] = fgr_in[:, lanes].astype(F32)
        for piece in range(4):
            hid_ref[lt, piece * PAD + PW : piece * PAD + PW + CELLS, :] = hid_in[
                piece * CELLS : piece * CELLS + CELLS, lanes
            ].astype(F32)

    for lt in range(2):
        for a in range(3):

            def products(piece, sums, a=a, lt=lt):
                sums = list(sums)
                for i in range(6):
                    own = pl.multiple_of(piece * CELLS + PW * i, 8)
                    grad = fgr_ref[lt, pl.ds(own, PW), :]
                    shifted = (up_one(grad, last), grad, down_one(grad, first))
                    for b in range(3):
                        start = pl.multiple_of((piece + a) * PAD + PW * (i + b), 8)
                        window = hid_ref[lt, pl.ds(start, PW), :]
                        for e in range(3):
                            term = window * shifted[e]
                            k = 3 * b + e
                            sums[k] = sums[k] + (term[0:8] + term[8:16] + term[16:24])
                return tuple(sums)

            sums = lax.fori_loop(0, 2, products, tuple(jnp.zeros((8, 128), F32) for _ in range(9)))
            for k in range(9):
                row = 32 * lt + 9 * a + k
                kgrad_ref[row : row + 1, :] = jnp.sum(sums[k], axis=0, keepdims=True)
        kgrad_ref[32 * lt + 27 : 32 * lt + 32, :] = jnp.zeros((5, 128), F32)

    down_grad = dot(act_in[...], og_ref[...], ((0,), (0,)))
    up_grad = dot(own_ref[...], hgr_in[...], ((0,), (0,)))
    product = up_grad * up_ref[...].astype(F32)
    prod_acc[...] += product[:, :128] + product[:, 128:]
    half = step // 3
    base = pl.multiple_of((step - 3 * half) * STRIDE, 16)
    for tile in range(2):
        weights_ref[half, pl.ds(base + C * tile, C), :] = up_grad[:, 128 * tile : 128 * tile + 128].astype(BF16)
    for tile in range(3):
        at = 2 * C + BLOCK * tile
        weights_ref[half, pl.ds(base + at, BLOCK), :] = down_grad[:, 128 * tile : 128 * tile + 128].astype(BF16)
    weights_ref[half, pl.ds(base + 1536, 64), :] = kgrad_ref[...].astype(BF16)

    @pl.when(step == STEPS - 1)
    def _():
        part = dot(jnp.ones((8, 128), F32), prod_acc[...], ((1,), (1,)), lax.Precision.HIGHEST)
        part = part / row_of(gain_ref)
        for tile in range(3):
            kgrad_ref[8 * tile : 8 * tile + 8, :] = part[:, 128 * tile : 128 * tile + 128]
        kgrad_ref[24:32, :] = jnp.zeros((8, 128), F32)
        for side in range(2):
            weights_ref[side, 3 * STRIDE :, :] = kgrad_ref[0:32, :].astype(BF16)


def feed_grads(og, own, hid, fgr, act, hgr, up, gain):
    def column(rows):
        return pl.BlockSpec((rows, BLOCK), lambda s: (0, s))

    return pl.pallas_call(
        grads_kernel,
        grid=(STEPS,),
        out_shape=shape((2, FFN + 32, 128)),
        in_specs=[
            pl.BlockSpec((ROWS, C), lambda s: (0, 0)),
            pl.BlockSpec((ROWS, C), lambda s: (0, 0)),
            column(2 * ROWS),
            column(ROWS),
            column(ROWS),
            column(ROWS),
            column(C),
            pl.BlockSpec((C,), lambda s: (0,)),
        ],
        out_specs=pl.BlockSpec((2, FFN + 32, 128), lambda s: (0, 0, 0)),
        scratch_shapes=[
            pltpu.VMEM((2, 4 * PAD, 128), F32),
            pltpu.VMEM((2, ROWS, 128), F32),
            pltpu.VMEM((C, 128), F32),
            pltpu.VMEM((64, 128), F32),
        ],
        name="feed_grads",
    )(og, own, hid, fgr, act, hgr, up, gain)


def feed_forward(low, mid, high, og_low, og, og_high, gain, up, kern, down):
    def whole(*dims):
        return pl.BlockSpec(dims, lambda s: (0,) * len(dims))

    return pl.pallas_call(
        feed_kernel,
        grid=(STEPS,),
        out_shape=(
            shape((ROWS, C)),
            shape((ROWS, C), F32),
            shape((16, 24, C)),
            shape((8, 40, C)),
            shape((ROWS, C)),
            shape((2 * ROWS, HID)),
            shape((ROWS, HID)),
            shape((ROWS, HID)),
            shape((ROWS, HID)),
        ),
        in_specs=[
            whole(ROWS, C),
            whole(ROWS, C),
            whole(ROWS, C),
            whole(CELLS, C),
            whole(ROWS, C),
            whole(CELLS, C),
            whole(C),
            pl.BlockSpec((C, BLOCK), lambda s: (0, s)),
            pl.BlockSpec((3, 3, 3, BLOCK), lambda s: (0, 0, 0, s)),
            pl.BlockSpec((BLOCK, C), lambda s: (s, 0)),
        ],
        out_specs=(
            whole(ROWS, C),
            whole(ROWS, C),
            whole(16, 24, C),
            whole(8, 40, C),
            whole(ROWS, C),
            pl.BlockSpec((2 * ROWS, BLOCK), lambda s: (0, s)),
            pl.BlockSpec((ROWS, BLOCK), lambda s: (0, s)),
            pl.BlockSpec((ROWS, BLOCK), lambda s: (0, s)),
            pl.BlockSpec((ROWS, BLOCK), lambda s: (0, s)),
        ),
        scratch_shapes=[
            pltpu.VMEM((3 * ROWS, C), BF16),
            pltpu.VMEM((2 * ROWS, C), BF16),
            pltpu.VMEM((2, 6 * PAD, 128), F32),
            pltpu.VMEM((2, 4 * PAD, 128), F32),
            pltpu.VMEM((2 * ROWS, BLOCK), F32),
            pltpu.VMEM((ROWS, BLOCK), F32),
            pltpu.VMEM((2 * ROWS, BLOCK), F32),
            pltpu.VMEM((ROWS, C), F32),
            pltpu.VMEM((ROWS, C), F32),
        ],
        name="feed_forward",
    )(low, mid, high, og_low, og, og_high, gain, up, kern, down)


def last_kernel(me_ref, tok_ref, gain_ref, mgrad_ref, *rest):
    dep_refs, tim_refs, (out_ref, dep_hold, tim_hold) = rest[:16], rest[16:24], rest[24:]
    for step, ref in enumerate(dep_refs):
        dep_hold[(me_ref[1] - step) & 15] = ref[...].astype(F32)
    for step, ref in enumerate(tim_refs):
        tim_hold[(me_ref[0] - step) & 7] = ref[...].astype(F32)
    dep = dep_hold[...].reshape(384, C).astype(BF16)
    tim = tim_hold[...].reshape(320, C).astype(BF16)
    back = dot(spread_depth(), dep, ((0,), (0,))) + dot(spread_time(), tim, ((0,), (0,)))
    scaled, inverse = norm_parts(tok_ref[...].astype(F32))
    out_ref[...] = (mgrad_ref[...] + norm_back(scaled, inverse, back * row_of(gain_ref))).astype(BF16)


def last_norm(me, tokens, depth, time, gain, mgrad):
    return pl.pallas_call(
        last_kernel,
        out_shape=shape((ROWS, C)),
        in_specs=SMEM + vmem(27),
        out_specs=vmem(1)[0],
        scratch_shapes=[pltpu.VMEM((16, 24, C), F32), pltpu.VMEM((8, 40, C), F32)],
        name="last_norm",
    )(me, tokens, gain, mgrad, *depth, *time)


STACK = COPIES * CHUNK
DEP = FFN + 32
TIM = DEP + ATT + 32


def pair_kernel(me_ref, *refs):
    out_ref, at = refs[-1], 0
    for one, two in zip(refs[0:-1:2], refs[1:-1:2], strict=True):
        size = one.shape[1]
        out_ref[at : at + size, :] = (one[0].astype(F32) + two[0].astype(F32)).astype(BF16)
        at += size
    out_ref[at:, :] = jnp.zeros((STACK - at, 128), BF16)


def swapped(array):
    return lax.ppermute(array, "core", [(0, 1), (1, 0)])


def pair_sum(me, args):
    return pl.pallas_call(
        pair_kernel,
        out_shape=shape((STACK, 128)),
        grid_spec=pltpu.PrefetchScalarGridSpec(
            num_scalar_prefetch=1,
            grid=(1,),
            in_specs=[pl.BlockSpec((1,) + a.shape[1:], lambda i, m: (m[2], 0, 0)) for a in args],
            out_specs=pl.BlockSpec((STACK, 128), lambda i, m: (0, 0)),
        ),
    )(me, *args)


def chip_kernel(factor, in_ref, out_ref):
    def add(source, total):
        return total + in_ref[source].astype(F32)

    total = lax.fori_loop(1, COPIES, add, in_ref[0].astype(F32), unroll=3)
    total = (total * factor).astype(BF16)

    def put(target, _):
        out_ref[target] = total
        return 0

    lax.fori_loop(0, COPIES, put, 0, unroll=2)


def chip_sum(received, factor):
    return pl.pallas_call(
        functools.partial(chip_kernel, factor),
        out_shape=shape(received.shape),
        in_specs=vmem(1),
        out_specs=vmem(1)[0],
        name="chip_sum",
    )(received)


def unpack_kernel(own, me_ref, in_ref, *refs):
    refs = refs if own else refs[7:]
    dq_ref, do_ref, tq_ref, to_ref, up_ref, kg_ref, dn_ref = refs[:7]
    for step in range(3):
        at = STRIDE * step
        for tile in range(2):
            lanes = slice(BLOCK * step + 128 * tile, BLOCK * step + 128 * tile + 128)
            up_ref[:, lanes] = in_ref[at + C * tile : at + C * tile + C, :].astype(F32)
            kgrad = in_ref[at + 1536 + 32 * tile : at + 1568 + 32 * tile, :].astype(F32)
            for k in range(27):
                kg_ref[k // 9, k // 3 % 3, k % 3 : k % 3 + 1, lanes] = kgrad[k : k + 1]
        for tile in range(3):
            rows = in_ref[at + 768 + BLOCK * tile : at + 1024 + BLOCK * tile, :].astype(F32)
            dn_ref[BLOCK * step : BLOCK * step + BLOCK, 128 * tile : 128 * tile + 128] = rows
    for base, q_ref, o_ref in ((DEP, dq_ref, do_ref), (TIM, tq_ref, to_ref)):
        for tile in range(12):
            rows = in_ref[base + 192 * tile : base + 192 * tile + 192, :].astype(F32)
            if tile < 9:
                q_ref[:, 128 * tile : 128 * tile + 128] = rows
            else:
                o_ref[:, 128 * (tile - 9) : 128 * (tile - 9) + 128] = rows
    if own:
        first_ref, second_ref, dscale_ref, tscale_ref = refs[7:11]
        two = in_ref[FFN : FFN + 32, :].astype(F32)
        dep = in_ref[DEP + ATT : DEP + ATT + 32, :].astype(F32)
        tim = in_ref[TIM + ATT : TIM + ATT + 32, :].astype(F32)
        one = dep + tim
        for tile in range(3):
            lanes = slice(128 * tile, 128 * tile + 128)
            second_ref[lanes] = two[8 * tile : 8 * tile + 1].reshape(128)
            first_ref[lanes] = one[8 * tile : 8 * tile + 1].reshape(128)
        for head in range(6):
            dscale_ref[head] = dep[24 + head // 2, 64 * (head % 2)]
            tscale_ref[head] = tim[24 + head // 2, 64 * (head % 2)]


def unpack(own, me, gathered, partial=()):
    half = (lambda m: m[2]) if own else (lambda m: 1 - m[2])
    out_shape = [
        shape((C, 3 * C), F32),
        shape((C, C), F32),
        shape((C, 3 * C), F32),
        shape((C, C), F32),
        shape((C, HID), F32),
        shape((3, 3, 3, HID), F32),
        shape((HID, C), F32),
    ]
    out_specs = [
        pl.BlockSpec((192, 3 * C), lambda i, m: (half(m), 0)),
        pl.BlockSpec((192, C), lambda i, m: (half(m), 0)),
        pl.BlockSpec((192, 3 * C), lambda i, m: (half(m), 0)),
        pl.BlockSpec((192, C), lambda i, m: (half(m), 0)),
        pl.BlockSpec((C, HID // 2), lambda i, m: (0, half(m))),
        pl.BlockSpec((3, 3, 3, HID // 2), lambda i, m: (0, 0, 0, half(m))),
        pl.BlockSpec((HID // 2, C), lambda i, m: (half(m), 0)),
    ]
    if own:
        out_shape += [shape((C,), F32), shape((C,), F32), shape((6,), F32), shape((6,), F32)]
        out_specs += [pl.BlockSpec((C,), lambda i, m: (0,))] * 2 + [pl.BlockSpec(memory_space=pltpu.SMEM)] * 2
    return pl.pallas_call(
        functools.partial(unpack_kernel, own),
        out_shape=tuple(out_shape),
        grid_spec=pltpu.PrefetchScalarGridSpec(
            num_scalar_prefetch=1,
            grid=(1,),
            in_specs=[pl.BlockSpec((STACK, 128), lambda i, m: (0, 0))]
            + [pl.BlockSpec(memory_space=pl.ANY)] * len(partial),
            out_specs=tuple(out_specs),
        ),
        input_output_aliases={2 + i: i for i in range(len(partial))},
        name="unpack_own" if own else "unpack_other",
    )(me, gathered, *partial)


def local(
    tokens, out_grad, first_gain, depth_qkv, depth_out, time_qkv, time_out, second_gain, up_weight,
    spatial_kernel, down_weight, depth_scale, time_scale,
):
    me = jnp.stack([lax.axis_index(TA), lax.axis_index(DEV), lax.axis_index("core")]).astype(jnp.int32)
    block_shape = tokens.shape
    flat = tokens.reshape(ROWS, C)
    og = out_grad.reshape(ROWS, C)
    count, frames = lax.axis_size(DEV), lax.axis_size(TA)
    ahead = [(i, i + 1) for i in range(count - 1)]
    behind = [(i + 1, i) for i in range(count - 1)]

    def turned(parts, axes, size):
        return [
            lax.ppermute(part, axes, [(i, (i + step) % size) for i in range(size)]) if step else part
            for step, part in enumerate(parts)
        ]

    queue = []

    def exchange(values, axes):
        if queue:
            values, _ = lax.optimization_barrier((values, queue[-1]))
        queue.append(lax.all_to_all(values, axes, split_axis=0, concat_axis=0, tiled=True))
        return queue[-1]

    dep, tim = first_norm(flat, first_gain)
    tim = exchange(tim, TA)
    dep = exchange(dep, DEV)
    tim_out, tim_fields, tim_mixed = attend(tim, time_qkv, time_out, time_scale)
    tim_back = exchange(tim_out, TA)
    dep_out, dep_fields, dep_mixed = attend(dep, depth_qkv, depth_out, depth_scale)
    dep_back = exchange(dep_out, DEV)
    og_low = lax.ppermute(og[CELLS:], DEV, ahead)
    og_high = lax.ppermute(og[:CELLS], DEV, behind)
    dep_back, og_low, og_high = lax.optimization_barrier((dep_back, og_low, og_high))
    mid = middle_of(flat, dep_back, tim_back)
    low = lax.ppermute(mid, DEV, ahead)
    high = lax.ppermute(mid, DEV, behind)
    block_out, mgrad, bdep, btim, *saved = feed_forward(
        low, mid, high, og_low, og, og_high, second_gain, up_weight, spatial_kernel, down_weight
    )
    ffn_g = feed_grads(og, *saved, up_weight, second_gain)
    btim = exchange(btim, TA)
    bdep = exchange(bdep, DEV)
    ffn_other = swapped(ffn_g)
    tim_first, tim_g = attend_back(me, btim, tim, tim_fields, tim_mixed, time_qkv, time_out, time_scale, first_gain)
    tim_other = swapped(tim_g)
    dep_first, dep_g = attend_back(me, bdep, dep, dep_fields, dep_mixed, depth_qkv, depth_out, depth_scale, first_gain)
    dep_other = swapped(dep_g)
    factor = 1.0 / math.sqrt(ROWS * count * frames)
    stack = pair_sum(me, [ffn_g, ffn_other, dep_g, dep_other, tim_g, tim_other])
    stack = exchange(stack.reshape(COPIES, CHUNK, 128), CHIPS)
    tim_first = turned(tim_first, TA, frames)
    spread, *tim_first = lax.optimization_barrier((chip_sum(stack, factor), *tim_first))
    dep_first = turned(dep_first, DEV, count)
    own = exchange(spread, CHIPS).reshape(STACK, 128)
    input_grad = last_norm(me, flat, dep_first, tim_first, first_gain, mgrad)
    other = swapped(own)
    *partial, first_gain_grad, second_gain_grad, depth_scale_grad, time_scale_grad = unpack(True, me, own)
    dq, do, tq, to, up_g, kern_g, down_g = unpack(False, me, other, partial)
    return (
        block_out.reshape(block_shape),
        input_grad.reshape(block_shape),
        dq,
        do,
        tq,
        to,
        up_g,
        kern_g,
        down_g,
        first_gain_grad,
        second_gain_grad,
        depth_scale_grad,
        time_scale_grad,
    )


def solution(mesh):
    fine = Mesh(mesh.devices.reshape(4, 2, 2, 2, 4), ("y", "xh", "core", "xl", "z"))
    split = P(TA, DEV, None, None)
    return jax.shard_map(
        local,
        mesh=fine,
        in_specs=(split, split) + (P(),) * 11,
        out_specs=(split, split) + (P(),) * 11,
        check_vma=False,
    )
```

time: 297 us -> 304 us (1.024)
  waiting for transfers between devices: 38.2 us -> 45.1 us
  blocking collectives: 61.2 us -> 66 us
  starting transfers between devices: 95.3 us -> 91.5 us
    ppermute x15 -> x22, waiting for transfers between devices: 6.43 us -> 30.5 us  [turned(): lax.ppermute(part, axes, [(i, (i + step) % size) for i in range(size)])]
    all_to_all x7 -> x5, waiting for transfers between devices: 26.8 us -> 6.86 us  [exchange(): lax.all_to_all(values, axes, split_axis=0, concat_axis=0, tiled=True)]
    all_to_all x7 -> x5, starting transfers between devices: 48.1 us -> 38.3 us  [exchange(): lax.all_to_all(values, axes, split_axis=0, concat_axis=0, tiled=True)]
    pallas_call x7, Pallas kernels: 39.2 us -> 47.5 us  [the longest x2 19.7 us: attend_back(): pl.pallas_call(attend_back_kernel, out_shape=(shape((part, C)),) * count...]
    ppermute x15 -> x22, starting transfers between devices: 28.1 us -> 35.2 us  [turned(): lax.ppermute(part, axes, [(i, (i + step) % size) for i in range(size)])]
    pallas_call x1, Pallas kernels: 31.6 us -> 25.1 us  [feed_forward(): pl.pallas_call(feed_kernel, grid=(STEPS,), out_shape=(shape((ROWS, C)), s...]
    all_to_all x3, blocking collectives: 61.2 us -> 66 us  [exchange(): lax.all_to_all(values, axes, split_axis=0, concat_axis=0, tiled=True)]
    pallas_call x2 -> x1, Pallas kernels: 7.28 us -> 4.99 us  [pair_sum(): pl.pallas_call(pair_kernel, out_shape=shape((STACK, 128)), grid_spec=pltp...]
  transfers between devices with their start and end apart: 30 -> 35, of which waited for: 13 -> 14; matrix products, arithmetic and copies ran while one was open for 0% -> 0% of each run, Pallas kernels for 16% -> 14%
where the time goes in v2:
time: 304 us; the launch traced here: 302 us
  Pallas kernels  92.3 us (30%)
  starting transfers between devices  91.5 us (30%)
  blocking collectives  66 us (22%)
  waiting for transfers between devices  45.1 us (15%)
  local copies, waits for them, and re-layouts  5.77 us (2%)
    all_to_all x3, blocking collectives, exchange(): lax.all_to_all(values, axes, split_axis=0, concat_axis=0, tiled=True)  66 us
    all_to_all x5, starting transfers between devices, exchange(): lax.all_to_all(values, axes, split_axis=0, concat_axis=0, tiled=True)  38.3 us
    ppermute x22, starting transfers between devices, turned(): lax.ppermute(part, axes, [(i, (i + step) % size) for i in range(size)])  35.2 us
    ppermute x22, waiting for transfers between devices, turned(): lax.ppermute(part, axes, [(i, (i + step) % size) for i in range(size)])  30.5 us
    pallas_call x1, Pallas kernels, feed_forward(): pl.pallas_call(feed_kernel, grid=(STEPS,), out_shape=(shape((ROWS, C)), s...  25.1 us
    pallas_call x2, Pallas kernels, attend_back(): pl.pallas_call(attend_back_kernel, out_shape=(shape((part, C)),) * count...  19.7 us
    pallas_call x1, Pallas kernels, feed_grads(): pl.pallas_call(grads_kernel, grid=(STEPS,), out_shape=shape((2, FFN + 32,...  11.2 us
    pallas_call x2, Pallas kernels, attend(): pl.pallas_call(attend_kernel, out_shape=(shape(inputs.shape), shape((rows...  10.4 us
  transfers between devices with their start and end apart: 35, of which 14 were waited for; matrix products, arithmetic and copies ran while one was open for 0% of the time, Pallas kernels for 14%

profile of v2, /device:TPU:1, one launch (start us, length us, event | category | flops | bytes accessed | tf_op | source)
XLA Modules:
  0.0 302.5 jit_solution(13552823052115229827)
XLA Ops:
  3.1 12.9 %all_to_all.40.in_ref = bf16[8,40,384]{2,1,0:T(8,128)(2,1)} all-to-all(bf16[8,40,384]{2,1,0:T(8,128)(2,1)} %get-tuple-element.94), channel_id=1, replica_groups=mesh['y'=4,'xh'=2,'core'=2,'xl'=2,'z'=4] {'xl','z'}, dimensions={0} | all-to-all | bytes 491520 | tf_op jit(solution)/shard_map/all_to_all | solution.py:754
  16.0 8.9 %all-to-all-start.1 = ((bf16[16,24,384]{2,1,0:T(8,128)(2,1)}), bf16[16,24,384]{2,1,0:T(8,128)(2,1)S(1)}, u32[]{:S(2)}, u32[]{:S(2)}) async-start(bf16[16,24,384]{2,1,0:T(8,128)(2,1)} %get-tuple-element.95), calls=%async_computation.1 | async-start | bytes 589824 | tf_op jit(solution)/shard_map/all_to_all | solution.py:754
  24.8 5.0 %shard_map.229 = (bf16[8,40,384]{2,1,0:T(8,128)(2,1)}, bf16[320,1152]{1,0:T(8,128)(2,1)}, bf16[320,384]{1,0:T(8,128)(2,1)}) custom-call(bf16[8,40,384]{2,1,0:T(8,128)(2,1)} %all_to_all.40.in_ref, bf16[384,1152]{1,0:T(8,128)(2,1)} %w_ref.7, bf16[384,384]{1,0:T(8,128)(2,1)} %wo_ref.7, f32[6]{0:T(128)} %scale_ref.7), custom_call_target="tpu_custom_call" | custom-call | tf_op jit(solution)/shard_map/pallas_call | solution.py:180
  29.8 4.0 %all-to-all-done.1.in_ref = bf16[16,24,384]{2,1,0:T(8,128)(2,1)S(1)} async-done(((bf16[16,24,384]{2,1,0:T(8,128)(2,1)}), bf16[16,24,384]{2,1,0:T(8,128)(2,1)S(1)}, u32[]{:S(2)}, u32[]{:S(2)}) %all-to-all-start.1) | async-done | bytes 294944 | tf_op jit(solution)/shard_map/all_to_all | solution.py:754
  33.8 3.4 %all-to-all-start.2 = ((bf16[8,40,384]{2,1,0:T(8,128)(2,1)}), bf16[8,40,384]{2,1,0:T(8,128)(2,1)S(1)}, u32[]{:S(2)}, u32[]{:S(2)}) async-start(bf16[8,40,384]{2,1,0:T(8,128)(2,1)} %get-tuple-element.98), calls=%async_computation.2 | async-start | bytes 491520 | tf_op jit(solution)/shard_map/all_to_all | solution.py:754
  37.2 5.4 %shard_map.228 = (bf16[16,24,384]{2,1,0:T(8,128)(2,1)}, bf16[384,1152]{1,0:T(8,128)(2,1)}, bf16[384,384]{1,0:T(8,128)(2,1)}) custom-call(bf16[16,24,384]{2,1,0:T(8,128)(2,1)} %copy-done.2, bf16[384,1152]{1,0:T(8,128)(2,1)} %w_ref.6, bf16[384,384]{1,0:T(8,128)(2,1)} %wo_ref.6, f32[6]{0:T(128)} %scale_ref.6), custom_call_target="tpu_custom_call" | custom-call | tf_op jit(solution)/shard_map/pallas_call | solution.py:180
  43.2 5.5 %all-to-all-start.3 = ((bf16[16,24,384]{2,1,0:T(8,128)(2,1)}), bf16[16,24,384]{2,1,0:T(8,128)(2,1)S(1)}, u32[]{:S(2)}, u32[]{:S(2)}) async-start(bf16[16,24,384]{2,1,0:T(8,128)(2,1)} %get-tuple-element.99), calls=%async_computation.3 | async-start | bytes 589824 | tf_op jit(solution)/shard_map/all_to_all | solution.py:754
  50.8 4.9 %collective-permute-start = (bf16[144,384]{1,0:T(8,128)(2,1)S(1)}, bf16[144,384]{1,0:T(8,128)(2,1)S(1)}, u32[]{:S(2)}, u32[]{:S(2)}) collective-permute-start(bf16[144,384]{1,0:T(8,128)(2,1)S(1)} %get-tuple-element.174), channel_id=1, source_target_pairs={{0,8},{8,16},{16,24},{24,32},{32,40},{40,48},{48,56},{56,64},{64,7... | collective-permute-start | bytes 331784 | tf_op jit(solution)/shard_map/ppermute | solution.py:764
  60.8 2.9 collective-permute-start.3
  63.7 4.7 %collective-permute-start.2 = (bf16[288,384]{1,0:T(8,128)(2,1)}, bf16[288,384]{1,0:T(8,128)(2,1)S(1)}, u32[]{:S(2)}, u32[]{:S(2)}) collective-permute-start(bf16[288,384]{1,0:T(8,128)(2,1)} %middle.1.mid_ref), channel_id=1, source_target_pairs={{0,8},{8,16},{16,24},{24,32},{32,40},{40,48},{48,56},{56,64},{64,7... | collective-permute-start | bytes 663560 | tf_op jit(solution)/shard_map/ppermute | solution.py:768
  72.2 25.1 %feed_forward.1 = (bf16[288,384]{1,0:T(8,128)(2,1)}, f32[288,384]{1,0:T(8,128)}, bf16[16,24,384]{2,1,0:T(8,128)(2,1)}, bf16[8,40,384]{2,1,0:T(8,128)(2,1)}, bf16...) custom-call(bf16[288,384]{1,0:T(8,128)(2,1)} %copy-done.10, ...), custom_call_target="tpu_custom_call" | custom-call | tf_op jit(solution)/shard_map/feed_forward/pallas_call | solution.py:526
  97.3 11.2 %feed_grads.1.refs_0_ = bf16[2,4832,128]{2,1,0:T(8,128)(2,1)} custom-call(bf16[288,384]{1,0:T(8,128)(2,1)} %bitcast.17, bf16[288,384]{1,0:T(8,128)(2,1)} %get-tuple-element.127.own_ref, bf16[576,1536]{1,0:T(8,128)(2,1)} %get-tuple-element.128.hid_in, bf16[288,1536]{1,0:T(8,128)(2,1)} %get-tuple-element.129.fgr_in, ...), custom_call_target="tpu_custom_call" | custom-call | tf_op jit(solution)/shard_map/feed_grads/pallas_call | solution.py:497
  108.5 9.6 %all_to_all.41.grad_ref = bf16[8,40,384]{2,1,0:T(8,128)(2,1)} all-to-all(bf16[8,40,384]{2,1,0:T(8,128)(2,1)S(1)} %copy-done.8), channel_id=1, replica_groups=mesh['y'=4,'xh'=2,'core'=2,'xl'=2,'z'=4] {'xl','z'}, dimensions={0} | all-to-all | bytes 491520 | tf_op jit(solution)/shard_map/all_to_all | solution.py:754
  118.1 12.0 %all-to-all-start.5 = ((bf16[16,24,384]{2,1,0:T(8,128)(2,1)}), bf16[16,24,384]{2,1,0:T(8,128)(2,1)S(1)}, u32[]{:S(2)}, u32[]{:S(2)}) async-start(bf16[16,24,384]{2,1,0:T(8,128)(2,1)} %get-tuple-element.108), calls=%async_computation.5 | async-start | bytes 589824 | tf_op jit(solution)/shard_map/all_to_all | solution.py:754
  130.7 9.6 %shard_map.231 = (bf16[40,384]{1,0:T(8,128)(2,1)}, bf16[40,384]{1,0:T(8,128)(2,1)}, bf16[40,384]{1,0:T(8,128)(2,1)}, bf16[40,384]{1,0:T(8,128)(2,1)}, bf16[40,38...) custom-call(bf16[8,40,384]{2,1,0:T(8,128)(2,1)} %all_to_all.41.grad_, ...), custom_call_target="tpu_custom_call" | custom-call | tf_op jit(solution)/shard_map/pallas_call | solution.py:274
  141.1 10.2 %shard_map.230 = (bf16[24,384]{1,0:T(8,128)(2,1)}, bf16[24,384]{1,0:T(8,128)(2,1)}, bf16[24,384]{1,0:T(8,128)(2,1)}, bf16[24,384]{1,0:T(8,128)(2,1)}, bf16[24,38...) custom-call(bf16[16,24,384]{2,1,0:T(8,128)(2,1)} %copy-done.5, ...), custom_call_target="tpu_custom_call" | custom-call | tf_op jit(solution)/shard_map/pallas_call | solution.py:274
  151.7 2.8 collective-permute-done.20.refs_3_
  156.1 5.0 %shard_map.232 = bf16[9728,128]{1,0:T(8,128)(2,1)} custom-call(s32[3]{0:T(128)} %pad_add_fusion.me_ref, bf16[2,4832,128]{2,1,0:T(8,128)(2,1)} %feed_grads.1.refs_0_, bf16[2,4832,128]{2,1,0:T(8,128)(2,1)} %copy-done.3, bf16[2,2336,128]{2,1,0:T(8,128)(2,1)} %get-tuple-element.132.refs_2_, bf16[2,2336,128]{2,1,0:T(8,128)(2,1)} %collective-permute-done.20.refs_3_, ...), custom_call_target="tpu_custom_call" | custom-call | tf_op jit(solution)/shard_map/pallas_call | solution.py:621
  161.1 8.5 %all-to-all-start.6 = ((bf16[64,152,128]{2,1,0:T(8,128)(2,1)}), bf16[64,152,128]{2,1,0:T(8,128)(2,1)S(1)}, u32[]{:S(2)}, u32[]{:S(2)}) async-start(bf16[64,152,128]{2,1,0:T(8,128)(2,1)} %bitcast.15), calls=%async_computation.6 | async-start | bytes 4980736 | tf_op jit(solution)/shard_map/all_to_all | solution.py:754
  176.7 23.9 %collective-permute-done.22.rest_17_ = bf16[40,384]{1,0:T(8,128)(2,1)S(1)} collective-permute-done((bf16[40,384]{1,0:T(8,128)(2,1)S(1)}, bf16[40,384]{1,0:T(8,128)(2,1)S(1)}, u32[]{:S(2)}, u32[]{:S(2)}) %collective-permute-start.22) | collective-permute-done | bytes 30752 | tf_op jit(solution)/shard_map/ppermute | solution.py:745
  204.6 3.8 %chip_sum.1 = bf16[64,152,128]{2,1,0:T(8,128)(2,1)} custom-call(bf16[64,152,128]{2,1,0:T(8,128)(2,1)} %copy-done.1), custom_call_target="tpu_custom_call" | custom-call | tf_op jit(solution)/shard_map/chip_sum/pallas_call | solution.py:648
  208.7 43.5 %all_to_all.42 = bf16[64,152,128]{2,1,0:T(8,128)(2,1)S(1)} all-to-all(bf16[64,152,128]{2,1,0:T(8,128)(2,1)} %chip_sum.1), channel_id=1, replica_groups=mesh['y'=4,'xh'=2,'core'=2,'xl'=2,'z'=4] {'y','xh','xl','z'}, dimensions={0} | all-to-all | bytes 4980736 | tf_op jit(solution)/shard_map/all_to_all | solution.py:754
  252.2 2.8 collective-permute-start.29
  259.4 4.9 %collective-permute-start.8 = (bf16[24,384]{1,0:T(8,128)(2,1)S(1)}, bf16[24,384]{1,0:T(8,128)(2,1)S(1)}, u32[]{:S(2)}, u32[]{:S(2)}) collective-permute-start(bf16[24,384]{1,0:T(8,128)(2,1)S(1)} %copy-done.52), channel_id=1, source_target_pairs={{0,40},{8,48},{16,56},{24,64},{32,72},{40,80},{48,88},{56,96},{64,... | collective-permute-start | bytes 55304 | tf_op jit(solution)/shard_map/ppermute | solution.py:745
  265.1 2.7 collective-permute-start.11
  267.8 4.9 %collective-permute-start.12 = (bf16[24,384]{1,0:T(8,128)(2,1)S(1)}, bf16[24,384]{1,0:T(8,128)(2,1)S(1)}, u32[]{:S(2)}, u32[]{:S(2)}) collective-permute-start(bf16[24,384]{1,0:T(8,128)(2,1)S(1)} %copy-done.48), channel_id=1, source_target_pairs={{0,72},{8,80},{16,88},{24,96},{32,104},{40,112},{48,120},{56,0},{6... | collective-permute-start | bytes 55304 | tf_op jit(solution)/shard_map/ppermute | solution.py:745
  277.6 3.7 %collective-permute-start.16 = (bf16[24,384]{1,0:T(8,128)(2,1)S(1)}, bf16[24,384]{1,0:T(8,128)(2,1)S(1)}, u32[]{:S(2)}, u32[]{:S(2)}) collective-permute-start(bf16[24,384]{1,0:T(8,128)(2,1)S(1)} %copy-done.44), channel_id=1, source_target_pairs={{0,104},{8,112},{16,120},{24,0},{32,8},{40,16},{48,24},{56,32},{64... | collective-permute-start | bytes 55304 | tf_op jit(solution)/shard_map/ppermute | solution.py:745
  281.3 3.5 %collective-permute-start.17 = (bf16[24,384]{1,0:T(8,128)(2,1)S(1)}, bf16[24,384]{1,0:T(8,128)(2,1)S(1)}, u32[]{:S(2)}, u32[]{:S(2)}) collective-permute-start(bf16[24,384]{1,0:T(8,128)(2,1)S(1)} %copy-done.43), channel_id=1, source_target_pairs={{0,112},{8,120},{16,0},{24,8},{32,16},{40,24},{48,32},{56,40},{64,... | collective-permute-start | bytes 55304 | tf_op jit(solution)/shard_map/ppermute | solution.py:745
  285.7 3.9 %collective-permute-done.18.rest_15_ = bf16[24,384]{1,0:T(8,128)(2,1)S(1)} collective-permute-done((bf16[24,384]{1,0:T(8,128)(2,1)S(1)}, bf16[24,384]{1,0:T(8,128)(2,1)S(1)}, u32[]{:S(2)}, u32[]{:S(2)}) %collective-permute-start.18) | collective-permute-done | bytes 18464 | tf_op jit(solution)/shard_map/ppermute | solution.py:745
  290.1 2.9 last_norm.1
  293.0 4.8 %unpack_own.1 = (f32[384,1152]{1,0:T(8,128)}, f32[384,384]{1,0:T(8,128)}, f32[384,1152]{1,0:T(8,128)}, f32[384,384]{1,0:T(8,128)}, f32[384,1536]{1,0:T(8,128)}, ...) custom-call(s32[3]{0:T(128)} %pad_add_fusion.me_ref, ...), custom_call_target="tpu_custom_call" | custom-call | tf_op jit(solution)/shard_map/unpack_own/pallas_call | solution.py:716
  297.9 4.6 %unpack_other.1 = (f32[384,1152]{1,0:T(8,128)}, f32[384,384]{1,0:T(8,128)}, f32[384,1152]{1,0:T(8,128)}, f32[384,384]{1,0:T(8,128)}, f32[384,1536]{1,0:T(8,128)}...) custom-call(s32[3]{0:T(128)} %pad_add_fusion.me_ref, ...), custom_call_target="tpu_custom_call", output_to_operand_aliasing={{0}: (2, {}), {1}: (3, {}), {2}: (4, {}), {3}: (5, {}), {4}... | custom-call | tf_op jit(solution)/shard_map/unpack_other/pallas_call | solution.py:716
  (170 shorter events, 39.8 us)
Async XLA Ops:
  16.0 17.8 %all-to-all-start.1 = ((bf16[16,24,384]{2,1,0:T(8,128)(2,1)}), bf16[16,24,384]{2,1,0:T(8,128)(2,1)S(1)}, u32[]{:S(2)}, u32[]{:S(2)}) async-start(bf16[16,24,384]{2,1,0:T(8,128)(2,1)} %get-tuple-element.95), calls=%async_computation.1 | async-start | bytes 589824 | tf_op jit(solution)/shard_map/all_to_all | solution.py:754
  33.8 9.4 %all-to-all-start.2 = ((bf16[8,40,384]{2,1,0:T(8,128)(2,1)}), bf16[8,40,384]{2,1,0:T(8,128)(2,1)S(1)}, u32[]{:S(2)}, u32[]{:S(2)}) async-start(bf16[8,40,384]{2,1,0:T(8,128)(2,1)} %get-tuple-element.98), calls=%async_computation.2 | async-start | bytes 491520 | tf_op jit(solution)/shard_map/all_to_all | solution.py:754
  43.2 14.5 %all-to-all-start.3 = ((bf16[16,24,384]{2,1,0:T(8,128)(2,1)}), bf16[16,24,384]{2,1,0:T(8,128)(2,1)S(1)}, u32[]{:S(2)}, u32[]{:S(2)}) async-start(bf16[16,24,384]{2,1,0:T(8,128)(2,1)} %get-tuple-element.99), calls=%async_computation.3 | async-start | bytes 589824 | tf_op jit(solution)/shard_map/all_to_all | solution.py:754
  48.7 8.6 %collective-permute-start.1 = (bf16[144,384]{1,0:T(8,128)(2,1)S(1)}, bf16[144,384]{1,0:T(8,128)(2,1)S(1)}, u32[]{:S(2)}, u32[]{:S(2)}) collective-permute-start(bf16[144,384]{1,0:T(8,128)(2,1)S(1)} %get-tuple-element.173), channel_id=1, source_target_pairs={{8,0},{16,8},{24,16},{32,24},{40,32},{48,40},{56,48},{64,56},{72,6... | collective-permute-start | bytes 331784 | tf_op jit(solution)/shard_map/ppermute | solution.py:765
  50.8 6.7 %collective-permute-start = (bf16[144,384]{1,0:T(8,128)(2,1)S(1)}, bf16[144,384]{1,0:T(8,128)(2,1)S(1)}, u32[]{:S(2)}, u32[]{:S(2)}) collective-permute-start(bf16[144,384]{1,0:T(8,128)(2,1)S(1)} %get-tuple-element.174), channel_id=1, source_target_pairs={{0,8},{8,16},{16,24},{24,32},{32,40},{40,48},{48,56},{56,64},{64,7... | collective-permute-start | bytes 331784 | tf_op jit(solution)/shard_map/ppermute | solution.py:764
  60.8 9.5 %collective-permute-start.3 = (bf16[288,384]{1,0:T(8,128)(2,1)}, bf16[288,384]{1,0:T(8,128)(2,1)S(1)}, u32[]{:S(2)}, u32[]{:S(2)}) collective-permute-start(bf16[288,384]{1,0:T(8,128)(2,1)} %middle.1.mid_ref), channel_id=1, source_target_pairs={{8,0},{16,8},{24,16},{32,24},{40,32},{48,40},{56,48},{64,56},{72,6... | collective-permute-start | bytes 663560 | tf_op jit(solution)/shard_map/ppermute | solution.py:769
  63.7 7.8 %collective-permute-start.2 = (bf16[288,384]{1,0:T(8,128)(2,1)}, bf16[288,384]{1,0:T(8,128)(2,1)S(1)}, u32[]{:S(2)}, u32[]{:S(2)}) collective-permute-start(bf16[288,384]{1,0:T(8,128)(2,1)} %middle.1.mid_ref), channel_id=1, source_target_pairs={{0,8},{8,16},{16,24},{24,32},{32,40},{40,48},{48,56},{56,64},{64,7... | collective-permute-start | bytes 663560 | tf_op jit(solution)/shard_map/ppermute | solution.py:768
  108.5 46.0 %collective-permute-start.19 = (bf16[2,4832,128]{2,1,0:T(8,128)(2,1)}, bf16[2,4832,128]{2,1,0:T(8,128)(2,1)S(1)}, u32[]{:S(2)}, u32[]{:S(2)}) collective-permute-start(bf16[2,4832,128]{2,1,0:T(8,128)(2,1)} %feed_grads.1.refs_0_), channel_id=1, source_target_pairs={{0,8},{8,0},{1,9},{9,1},{2,10},{10,2},{3,11},{11,3},{4,12},{12,4},... | collective-permute-start | bytes 7421960 | tf_op jit(solution)/shard_map/ppermute | solution.py:617
  118.1 22.3 %all-to-all-start.5 = ((bf16[16,24,384]{2,1,0:T(8,128)(2,1)}), bf16[16,24,384]{2,1,0:T(8,128)(2,1)S(1)}, u32[]{:S(2)}, u32[]{:S(2)}) async-start(bf16[16,24,384]{2,1,0:T(8,128)(2,1)} %get-tuple-element.108), calls=%async_computation.5 | async-start | bytes 589824 | tf_op jit(solution)/shard_map/all_to_all | solution.py:754
  140.3 11.4 %collective-permute-start.21 = (bf16[2,2336,128]{2,1,0:T(8,128)(2,1)}, bf16[2,2336,128]{2,1,0:T(8,128)(2,1)}, u32[]{:S(2)}, u32[]{:S(2)}) collective-permute-start(bf16[2,2336,128]{2,1,0:T(8,128)(2,1)} %get-tuple-element.135.refs_4_), channel_id=1, source_target_pairs={{0,8},{8,0},{1,9},{9,1},{2,10},{10,2},{3,11},{11,3},{4,12},{12,4},... | collective-permute-start | bytes 3588104 | tf_op jit(solution)/shard_map/ppermute | solution.py:617
  161.1 42.0 %all-to-all-start.6 = ((bf16[64,152,128]{2,1,0:T(8,128)(2,1)}), bf16[64,152,128]{2,1,0:T(8,128)(2,1)S(1)}, u32[]{:S(2)}, u32[]{:S(2)}) async-start(bf16[64,152,128]{2,1,0:T(8,128)(2,1)} %bitcast.15), calls=%async_computation.6 | async-start | bytes 4980736 | tf_op jit(solution)/shard_map/all_to_all | solution.py:754
  169.6 31.0 %collective-permute-start.22 = (bf16[40,384]{1,0:T(8,128)(2,1)S(1)}, bf16[40,384]{1,0:T(8,128)(2,1)S(1)}, u32[]{:S(2)}, u32[]{:S(2)}) collective-permute-start(bf16[40,384]{1,0:T(8,128)(2,1)S(1)} %copy-done.41), channel_id=1, source_target_pairs={{0,1},{1,2},{2,3},{3,4},{4,5},{5,6},{6,7},{7,0},{8,9},{9,10},{10,1... | collective-permute-start | bytes 92168 | tf_op jit(solution)/shard_map/ppermute | solution.py:745
  170.7 30.2 %collective-permute-start.23 = (bf16[40,384]{1,0:T(8,128)(2,1)S(1)}, bf16[40,384]{1,0:T(8,128)(2,1)S(1)}, u32[]{:S(2)}, u32[]{:S(2)}) collective-permute-start(bf16[40,384]{1,0:T(8,128)(2,1)S(1)} %copy-done.40), channel_id=1, source_target_pairs={{0,2},{1,3},{2,4},{3,5},{4,6},{5,7},{6,0},{7,1},{8,10},{9,11},{10,... | collective-permute-start | bytes 92168 | tf_op jit(solution)/shard_map/ppermute | solution.py:745
  173.1 35.3 %collective-permute-start.24 = (bf16[40,384]{1,0:T(8,128)(2,1)S(1)}, bf16[40,384]{1,0:T(8,128)(2,1)S(1)}, u32[]{:S(2)}, u32[]{:S(2)}) collective-permute-start(bf16[40,384]{1,0:T(8,128)(2,1)S(1)} %copy-done.39), channel_id=1, source_target_pairs={{0,3},{1,4},{2,5},{3,6},{4,7},{5,0},{6,1},{7,2},{8,11},{9,12},{10,... | collective-permute-start | bytes 92168 | tf_op jit(solution)/shard_map/ppermute | solution.py:745
  175.2 33.2 %collective-permute-start.25 = (bf16[40,384]{1,0:T(8,128)(2,1)S(1)}, bf16[40,384]{1,0:T(8,128)(2,1)S(1)}, u32[]{:S(2)}, u32[]{:S(2)}) collective-permute-start(bf16[40,384]{1,0:T(8,128)(2,1)S(1)} %copy-done.38), channel_id=1, source_target_pairs={{0,4},{1,5},{2,6},{3,7},{4,0},{5,1},{6,2},{7,3},{8,12},{9,13},{10,... | collective-permute-start | bytes 92168 | tf_op jit(solution)/shard_map/ppermute | solution.py:745
  175.5 33.0 %collective-permute-start.26 = (bf16[40,384]{1,0:T(8,128)(2,1)S(1)}, bf16[40,384]{1,0:T(8,128)(2,1)S(1)}, u32[]{:S(2)}, u32[]{:S(2)}) collective-permute-start(bf16[40,384]{1,0:T(8,128)(2,1)S(1)} %copy-done.37), channel_id=1, source_target_pairs={{0,5},{1,6},{2,7},{3,0},{4,1},{5,2},{6,3},{7,4},{8,13},{9,14},{10,... | collective-permute-start | bytes 92168 | tf_op jit(solution)/shard_map/ppermute | solution.py:745
  200.6 7.9 %collective-permute-start.27 = (bf16[40,384]{1,0:T(8,128)(2,1)S(1)}, bf16[40,384]{1,0:T(8,128)(2,1)S(1)}, u32[]{:S(2)}, u32[]{:S(2)}) collective-permute-start(bf16[40,384]{1,0:T(8,128)(2,1)S(1)} %copy-done.36), channel_id=1, source_target_pairs={{0,6},{1,7},{2,0},{3,1},{4,2},{5,3},{6,4},{7,5},{8,14},{9,15},{10,... | collective-permute-start | bytes 92168 | tf_op jit(solution)/shard_map/ppermute | solution.py:745
  200.9 7.5 %collective-permute-start.28 = (bf16[40,384]{1,0:T(8,128)(2,1)S(1)}, bf16[40,384]{1,0:T(8,128)(2,1)S(1)}, u32[]{:S(2)}, u32[]{:S(2)}) collective-permute-start(bf16[40,384]{1,0:T(8,128)(2,1)S(1)} %copy-done.35), channel_id=1, source_target_pairs={{0,7},{1,0},{2,1},{3,2},{4,3},{5,4},{6,5},{7,6},{8,15},{9,8},{10,9... | collective-permute-start | bytes 92168 | tf_op jit(solution)/shard_map/ppermute | solution.py:745
  252.2 45.6 %collective-permute-start.29 = (bf16[9728,128]{1,0:T(8,128)(2,1)S(1)}, bf16[9728,128]{1,0:T(8,128)(2,1)}, u32[]{:S(2)}, u32[]{:S(2)}) collective-permute-start(bf16[9728,128]{1,0:T(8,128)(2,1)S(1)} %bitcast.13), channel_id=1, source_target_pairs={{0,8},{8,0},{1,9},{9,1},{2,10},{10,2},{3,11},{11,3},{4,12},{12,4},... | collective-permute-start | bytes 7471112 | tf_op jit(solution)/shard_map/ppermute | solution.py:617
  255.5 8.8 %collective-permute-start.5 = (bf16[24,384]{1,0:T(8,128)(2,1)S(1)}, bf16[24,384]{1,0:T(8,128)(2,1)S(1)}, u32[]{:S(2)}, u32[]{:S(2)}) collective-permute-start(bf16[24,384]{1,0:T(8,128)(2,1)S(1)} %copy-done.55), channel_id=1, source_target_pairs={{0,16},{8,24},{16,32},{24,40},{32,48},{40,56},{48,64},{56,72},{64,... | collective-permute-start | bytes 55304 | tf_op jit(solution)/shard_map/ppermute | solution.py:745
  257.7 7.2 %collective-permute-start.6 = (bf16[24,384]{1,0:T(8,128)(2,1)S(1)}, bf16[24,384]{1,0:T(8,128)(2,1)S(1)}, u32[]{:S(2)}, u32[]{:S(2)}) collective-permute-start(bf16[24,384]{1,0:T(8,128)(2,1)S(1)} %copy-done.54), channel_id=1, source_target_pairs={{0,24},{8,32},{16,40},{24,48},{32,56},{40,64},{48,72},{56,80},{64,... | collective-permute-start | bytes 55304 | tf_op jit(solution)/shard_map/ppermute | solution.py:745
  257.7 7.5 %collective-permute-start.7 = (bf16[24,384]{1,0:T(8,128)(2,1)S(1)}, bf16[24,384]{1,0:T(8,128)(2,1)S(1)}, u32[]{:S(2)}, u32[]{:S(2)}) collective-permute-start(bf16[24,384]{1,0:T(8,128)(2,1)S(1)} %copy-done.53), channel_id=1, source_target_pairs={{0,32},{8,40},{16,48},{24,56},{32,64},{40,72},{48,80},{56,88},{64,... | collective-permute-start | bytes 55304 | tf_op jit(solution)/shard_map/ppermute | solution.py:745
  259.4 8.4 %collective-permute-start.8 = (bf16[24,384]{1,0:T(8,128)(2,1)S(1)}, bf16[24,384]{1,0:T(8,128)(2,1)S(1)}, u32[]{:S(2)}, u32[]{:S(2)}) collective-permute-start(bf16[24,384]{1,0:T(8,128)(2,1)S(1)} %copy-done.52), channel_id=1, source_target_pairs={{0,40},{8,48},{16,56},{24,64},{32,72},{40,80},{48,88},{56,96},{64,... | collective-permute-start | bytes 55304 | tf_op jit(solution)/shard_map/ppermute | solution.py:745
  264.3 8.5 %collective-permute-start.9 = (bf16[24,384]{1,0:T(8,128)(2,1)S(1)}, bf16[24,384]{1,0:T(8,128)(2,1)S(1)}, u32[]{:S(2)}, u32[]{:S(2)}) collective-permute-start(bf16[24,384]{1,0:T(8,128)(2,1)S(1)} %copy-done.51), channel_id=1, source_target_pairs={{0,48},{8,56},{16,64},{24,72},{32,80},{40,88},{48,96},{56,104},{64... | collective-permute-start | bytes 55304 | tf_op jit(solution)/shard_map/ppermute | solution.py:745
  264.8 10.6 %collective-permute-start.10 = (bf16[24,384]{1,0:T(8,128)(2,1)S(1)}, bf16[24,384]{1,0:T(8,128)(2,1)S(1)}, u32[]{:S(2)}, u32[]{:S(2)}) collective-permute-start(bf16[24,384]{1,0:T(8,128)(2,1)S(1)} %copy-done.50), channel_id=1, source_target_pairs={{0,56},{8,64},{16,72},{24,80},{32,88},{40,96},{48,104},{56,112},{6... | collective-permute-start | bytes 55304 | tf_op jit(solution)/shard_map/ppermute | solution.py:745
  265.1 10.9 %collective-permute-start.11 = (bf16[24,384]{1,0:T(8,128)(2,1)S(1)}, bf16[24,384]{1,0:T(8,128)(2,1)S(1)}, u32[]{:S(2)}, u32[]{:S(2)}) collective-permute-start(bf16[24,384]{1,0:T(8,128)(2,1)S(1)} %copy-done.49), channel_id=1, source_target_pairs={{0,64},{8,72},{16,80},{24,88},{32,96},{40,104},{48,112},{56,120},{... | collective-permute-start | bytes 55304 | tf_op jit(solution)/shard_map/ppermute | solution.py:745
  267.8 9.8 %collective-permute-start.12 = (bf16[24,384]{1,0:T(8,128)(2,1)S(1)}, bf16[24,384]{1,0:T(8,128)(2,1)S(1)}, u32[]{:S(2)}, u32[]{:S(2)}) collective-permute-start(bf16[24,384]{1,0:T(8,128)(2,1)S(1)} %copy-done.48), channel_id=1, source_target_pairs={{0,72},{8,80},{16,88},{24,96},{32,104},{40,112},{48,120},{56,0},{6... | collective-permute-start | bytes 55304 | tf_op jit(solution)/shard_map/ppermute | solution.py:745
  272.8 8.5 %collective-permute-start.13 = (bf16[24,384]{1,0:T(8,128)(2,1)S(1)}, bf16[24,384]{1,0:T(8,128)(2,1)S(1)}, u32[]{:S(2)}, u32[]{:S(2)}) collective-permute-start(bf16[24,384]{1,0:T(8,128)(2,1)S(1)} %copy-done.47), channel_id=1, source_target_pairs={{0,80},{8,88},{16,96},{24,104},{32,112},{40,120},{48,0},{56,8},{64... | collective-permute-start | bytes 55304 | tf_op jit(solution)/shard_map/ppermute | solution.py:745
  275.4 9.3 %collective-permute-start.14 = (bf16[24,384]{1,0:T(8,128)(2,1)S(1)}, bf16[24,384]{1,0:T(8,128)(2,1)S(1)}, u32[]{:S(2)}, u32[]{:S(2)}) collective-permute-start(bf16[24,384]{1,0:T(8,128)(2,1)S(1)} %copy-done.46), channel_id=1, source_target_pairs={{0,88},{8,96},{16,104},{24,112},{32,120},{40,0},{48,8},{56,16},{64... | collective-permute-start | bytes 55304 | tf_op jit(solution)/shard_map/ppermute | solution.py:745
  276.0 8.9 %collective-permute-start.15 = (bf16[24,384]{1,0:T(8,128)(2,1)S(1)}, bf16[24,384]{1,0:T(8,128)(2,1)S(1)}, u32[]{:S(2)}, u32[]{:S(2)}) collective-permute-start(bf16[24,384]{1,0:T(8,128)(2,1)S(1)} %copy-done.45), channel_id=1, source_target_pairs={{0,96},{8,104},{16,112},{24,120},{32,0},{40,8},{48,16},{56,24},{64... | collective-permute-start | bytes 55304 | tf_op jit(solution)/shard_map/ppermute | solution.py:745
  277.6 7.3 %collective-permute-start.16 = (bf16[24,384]{1,0:T(8,128)(2,1)S(1)}, bf16[24,384]{1,0:T(8,128)(2,1)S(1)}, u32[]{:S(2)}, u32[]{:S(2)}) collective-permute-start(bf16[24,384]{1,0:T(8,128)(2,1)S(1)} %copy-done.44), channel_id=1, source_target_pairs={{0,104},{8,112},{16,120},{24,0},{32,8},{40,16},{48,24},{56,32},{64... | collective-permute-start | bytes 55304 | tf_op jit(solution)/shard_map/ppermute | solution.py:745
  284.8 4.8 %collective-permute-start.18 = (bf16[24,384]{1,0:T(8,128)(2,1)S(1)}, bf16[24,384]{1,0:T(8,128)(2,1)S(1)}, u32[]{:S(2)}, u32[]{:S(2)}) collective-permute-start(bf16[24,384]{1,0:T(8,128)(2,1)S(1)} %copy-done.42), channel_id=1, source_target_pairs={{0,120},{8,0},{16,8},{24,16},{32,24},{40,32},{48,40},{56,48},{64,5... | collective-permute-start | bytes 55304 | tf_op jit(solution)/shard_map/ppermute | solution.py:745
  (60 other events, 1780.8 us)

commit v3 on v2

--- a/solution.py
+++ b/solution.py
@@ -26,6 +26,7 @@
 F32 = jnp.float32
 BF16 = jnp.bfloat16
 EPS = 1e-5
+LIMIT = 24 << 20
 
 
 def piece_of(row, size):
@@ -595,6 +596,7 @@
         in_specs=SMEM + vmem(27),
         out_specs=vmem(1)[0],
         scratch_shapes=[pltpu.VMEM((16, 24, C), F32), pltpu.VMEM((8, 40, C), F32)],
+        compiler_params=pltpu.CompilerParams(vmem_limit_bytes=LIMIT),
         name="last_norm",
     )(me, tokens, gain, mgrad, *depth, *time)
 
@@ -627,6 +629,7 @@
             in_specs=[pl.BlockSpec((1,) + a.shape[1:], lambda i, m: (m[2], 0, 0)) for a in args],
             out_specs=pl.BlockSpec((STACK, 128), lambda i, m: (0, 0)),
         ),
+        compiler_params=pltpu.CompilerParams(vmem_limit_bytes=LIMIT),
     )(me, *args)
 
 
@@ -650,6 +653,7 @@
         out_shape=shape(received.shape),
         in_specs=vmem(1),
         out_specs=vmem(1)[0],
+        compiler_params=pltpu.CompilerParams(vmem_limit_bytes=LIMIT),
         name="chip_sum",
     )(received)
 
@@ -724,6 +728,7 @@
             out_specs=tuple(out_specs),
         ),
         input_output_aliases={2 + i: i for i in range(len(partial))},
+        compiler_params=pltpu.CompilerParams(vmem_limit_bytes=LIMIT),
         name="unpack_own" if own else "unpack_other",
     )(me, gathered, *partial)
 

time: 304 us -> 294 us (0.967)
  Pallas kernels: 92.3 us -> 83.9 us
    pallas_call x2, Pallas kernels: 9.45 us -> 6.02 us  [unpack(): pl.pallas_call(functools.partial(unpack_kernel, own), out_shape=tuple(out...]
    pallas_call x1, Pallas kernels: 3.84 us -> 0.7 us  [chip_sum(): pl.pallas_call(functools.partial(chip_kernel, factor), out_shape=shape(re...]
  transfers between devices with their start and end apart: 35 -> 35, of which waited for: 14 -> 15; matrix products, arithmetic and copies ran while one was open for 0% -> 0% of each run, Pallas kernels for 14% -> 12%
where the time goes in v3:
time: 294 us; the launch traced here: 293 us
  starting transfers between devices  91.3 us (31%)
  Pallas kernels  83.9 us (29%)
  blocking collectives  65.3 us (22%)
  waiting for transfers between devices  46 us (16%)
  local copies, waits for them, and re-layouts  4.83 us (2%)
    all_to_all x3, blocking collectives, exchange(): lax.all_to_all(values, axes, split_axis=0, concat_axis=0, tiled=True)  65.3 us
    all_to_all x5, starting transfers between devices, exchange(): lax.all_to_all(values, axes, split_axis=0, concat_axis=0, tiled=True)  38.3 us
    ppermute x22, starting transfers between devices, turned(): lax.ppermute(part, axes, [(i, (i + step) % size) for i in range(size)])  34.5 us
    ppermute x22, waiting for transfers between devices, turned(): lax.ppermute(part, axes, [(i, (i + step) % size) for i in range(size)])  31.6 us
    pallas_call x1, Pallas kernels, feed_forward(): pl.pallas_call(feed_kernel, grid=(STEPS,), out_shape=(shape((ROWS, C)), s...  24.8 us
    pallas_call x2, Pallas kernels, attend_back(): pl.pallas_call(attend_back_kernel, out_shape=(shape((part, C)),) * count...  19.9 us
    pallas_call x1, Pallas kernels, feed_grads(): pl.pallas_call(grads_kernel, grid=(STEPS,), out_shape=shape((2, FFN + 32,...  11.2 us
    pallas_call x2, Pallas kernels, attend(): pl.pallas_call(attend_kernel, out_shape=(shape(inputs.shape), shape((rows...  10.4 us
  transfers between devices with their start and end apart: 35, of which 15 were waited for; matrix products, arithmetic and copies ran while one was open for 0% of the time, Pallas kernels for 12%

profile of v3, /device:TPU:1, one launch (start us, length us, event | category | flops | bytes accessed | tf_op | source)
XLA Modules:
  0.0 292.9 jit_solution(7265953511443346778)
XLA Ops:
  0.6 2.4 first_norm.1
  3.1 12.9 %all_to_all.40.in_ref = bf16[8,40,384]{2,1,0:T(8,128)(2,1)} all-to-all(bf16[8,40,384]{2,1,0:T(8,128)(2,1)} %get-tuple-element.94), channel_id=1, replica_groups=mesh['y'=4,'xh'=2,'core'=2,'xl'=2,'z'=4] {'xl','z'}, dimensions={0} | all-to-all | bytes 491520 | tf_op jit(solution)/shard_map/all_to_all | solution.py:759
  16.0 8.9 %all-to-all-start.1 = ((bf16[16,24,384]{2,1,0:T(8,128)(2,1)}), bf16[16,24,384]{2,1,0:T(8,128)(2,1)S(1)}, u32[]{:S(2)}, u32[]{:S(2)}) async-start(bf16[16,24,384]{2,1,0:T(8,128)(2,1)} %get-tuple-element.95), calls=%async_computation.1 | async-start | bytes 589824 | tf_op jit(solution)/shard_map/all_to_all | solution.py:759
  24.8 5.0 %shard_map.229 = (bf16[8,40,384]{2,1,0:T(8,128)(2,1)}, bf16[320,1152]{1,0:T(8,128)(2,1)}, bf16[320,384]{1,0:T(8,128)(2,1)}) custom-call(bf16[8,40,384]{2,1,0:T(8,128)(2,1)} %all_to_all.40.in_ref, bf16[384,1152]{1,0:T(8,128)(2,1)} %w_ref.7, bf16[384,384]{1,0:T(8,128)(2,1)} %wo_ref.7, f32[6]{0:T(128)} %scale_ref.7), custom_call_target="tpu_custom_call" | custom-call | tf_op jit(solution)/shard_map/pallas_call | solution.py:181
  29.8 4.0 %all-to-all-done.1.in_ref = bf16[16,24,384]{2,1,0:T(8,128)(2,1)S(1)} async-done(((bf16[16,24,384]{2,1,0:T(8,128)(2,1)}), bf16[16,24,384]{2,1,0:T(8,128)(2,1)S(1)}, u32[]{:S(2)}, u32[]{:S(2)}) %all-to-all-start.1) | async-done | bytes 294944 | tf_op jit(solution)/shard_map/all_to_all | solution.py:759
  33.8 3.4 %all-to-all-start.2 = ((bf16[8,40,384]{2,1,0:T(8,128)(2,1)}), bf16[8,40,384]{2,1,0:T(8,128)(2,1)S(1)}, u32[]{:S(2)}, u32[]{:S(2)}) async-start(bf16[8,40,384]{2,1,0:T(8,128)(2,1)} %get-tuple-element.98), calls=%async_computation.2 | async-start | bytes 491520 | tf_op jit(solution)/shard_map/all_to_all | solution.py:759
  37.2 5.4 %shard_map.228 = (bf16[16,24,384]{2,1,0:T(8,128)(2,1)}, bf16[384,1152]{1,0:T(8,128)(2,1)}, bf16[384,384]{1,0:T(8,128)(2,1)}) custom-call(bf16[16,24,384]{2,1,0:T(8,128)(2,1)} %copy-done.9, bf16[384,1152]{1,0:T(8,128)(2,1)} %w_ref.6, bf16[384,384]{1,0:T(8,128)(2,1)} %wo_ref.6, f32[6]{0:T(128)} %scale_ref.6), custom_call_target="tpu_custom_call" | custom-call | tf_op jit(solution)/shard_map/pallas_call | solution.py:181
  43.2 5.5 %all-to-all-start.3 = ((bf16[16,24,384]{2,1,0:T(8,128)(2,1)}), bf16[16,24,384]{2,1,0:T(8,128)(2,1)S(1)}, u32[]{:S(2)}, u32[]{:S(2)}) async-start(bf16[16,24,384]{2,1,0:T(8,128)(2,1)} %get-tuple-element.99), calls=%async_computation.3 | async-start | bytes 589824 | tf_op jit(solution)/shard_map/all_to_all | solution.py:759
  50.8 4.9 %collective-permute-start = (bf16[144,384]{1,0:T(8,128)(2,1)S(1)}, bf16[144,384]{1,0:T(8,128)(2,1)S(1)}, u32[]{:S(2)}, u32[]{:S(2)}) collective-permute-start(bf16[144,384]{1,0:T(8,128)(2,1)S(1)} %get-tuple-element.174), channel_id=1, source_target_pairs={{0,8},{8,16},{16,24},{24,32},{32,40},{40,48},{48,56},{56,64},{64,7... | collective-permute-start | bytes 331784 | tf_op jit(solution)/shard_map/ppermute | solution.py:769
  60.8 2.9 %collective-permute-start.3 = (bf16[288,384]{1,0:T(8,128)(2,1)}, bf16[288,384]{1,0:T(8,128)(2,1)S(1)}, u32[]{:S(2)}, u32[]{:S(2)}) collective-permute-start(bf16[288,384]{1,0:T(8,128)(2,1)} %middle.1.mid_ref), channel_id=1, source_target_pairs={{8,0},{16,8},{24,16},{32,24},{40,32},{48,40},{56,48},{64,56},{72,6... | collective-permute-start | bytes 663560 | tf_op jit(solution)/shard_map/ppermute | solution.py:774
  63.7 4.7 %collective-permute-start.2 = (bf16[288,384]{1,0:T(8,128)(2,1)}, bf16[288,384]{1,0:T(8,128)(2,1)S(1)}, u32[]{:S(2)}, u32[]{:S(2)}) collective-permute-start(bf16[288,384]{1,0:T(8,128)(2,1)} %middle.1.mid_ref), channel_id=1, source_target_pairs={{0,8},{8,16},{16,24},{24,32},{32,40},{40,48},{48,56},{56,64},{64,7... | collective-permute-start | bytes 663560 | tf_op jit(solution)/shard_map/ppermute | solution.py:773
  72.2 24.8 %feed_forward.1 = (bf16[288,384]{1,0:T(8,128)(2,1)}, f32[288,384]{1,0:T(8,128)}, bf16[16,24,384]{2,1,0:T(8,128)(2,1)}, bf16[8,40,384]{2,1,0:T(8,128)(2,1)}, bf16...) custom-call(bf16[288,384]{1,0:T(8,128)(2,1)} %copy-done.16, ...), custom_call_target="tpu_custom_call" | custom-call | tf_op jit(solution)/shard_map/feed_forward/pallas_call | solution.py:527
  97.1 11.2 %feed_grads.1.refs_0_ = bf16[2,4832,128]{2,1,0:T(8,128)(2,1)} custom-call(bf16[288,384]{1,0:T(8,128)(2,1)} %bitcast.19, bf16[288,384]{1,0:T(8,128)(2,1)} %get-tuple-element.127.own_ref, bf16[576,1536]{1,0:T(8,128)(2,1)} %get-tuple-element.128.hid_in, bf16[288,1536]{1,0:T(8,128)(2,1)} %get-tuple-element.129.fgr_in, ...), custom_call_target="tpu_custom_call" | custom-call | tf_op jit(solution)/shard_map/feed_grads/pallas_call | solution.py:498
  108.2 9.6 %all_to_all.41.grad_ref = bf16[8,40,384]{2,1,0:T(8,128)(2,1)} all-to-all(bf16[8,40,384]{2,1,0:T(8,128)(2,1)S(1)} %copy-done.14), channel_id=1, replica_groups=mesh['y'=4,'xh'=2,'core'=2,'xl'=2,'z'=4] {'xl','z'}, dimensions={0} | all-to-all | bytes 491520 | tf_op jit(solution)/shard_map/all_to_all | solution.py:759
  117.8 12.0 %all-to-all-start.5 = ((bf16[16,24,384]{2,1,0:T(8,128)(2,1)}), bf16[16,24,384]{2,1,0:T(8,128)(2,1)S(1)}, u32[]{:S(2)}, u32[]{:S(2)}) async-start(bf16[16,24,384]{2,1,0:T(8,128)(2,1)} %get-tuple-element.108), calls=%async_computation.5 | async-start | bytes 589824 | tf_op jit(solution)/shard_map/all_to_all | solution.py:759
  130.4 9.7 %shard_map.231 = (bf16[40,384]{1,0:T(8,128)(2,1)}, bf16[40,384]{1,0:T(8,128)(2,1)}, bf16[40,384]{1,0:T(8,128)(2,1)}, bf16[40,384]{1,0:T(8,128)(2,1)}, bf16[40,38...) custom-call(bf16[8,40,384]{2,1,0:T(8,128)(2,1)} %all_to_all.41.grad_, ...), custom_call_target="tpu_custom_call" | custom-call | tf_op jit(solution)/shard_map/pallas_call | solution.py:275
  141.0 10.2 %shard_map.230 = (bf16[24,384]{1,0:T(8,128)(2,1)}, bf16[24,384]{1,0:T(8,128)(2,1)}, bf16[24,384]{1,0:T(8,128)(2,1)}, bf16[24,384]{1,0:T(8,128)(2,1)}, bf16[24,38...) custom-call(bf16[16,24,384]{2,1,0:T(8,128)(2,1)} %copy-done.11, ...), custom_call_target="tpu_custom_call" | custom-call | tf_op jit(solution)/shard_map/pallas_call | solution.py:275
  151.6 2.7 collective-permute-done.20.refs_3_
  156.8 4.0 %shard_map.232 = bf16[9728,128]{1,0:T(8,128)(2,1)} custom-call(s32[3]{0:T(128)S(1)} %copy-done.7, bf16[2,4832,128]{2,1,0:T(8,128)(2,1)S(1)} %copy-done, bf16[2,4832,128]{2,1,0:T(8,128)(2,1)} %collective-permute-done.19.refs_1_, bf16[2,2336,128]{2,1,0:T(8,128)(2,1)S(1)} %copy-done.3, bf16[2,2336,128]{2,1,0:T(8,128)(2,1)S(1)} %collective-permute-done.20.refs_3_, ...), custom_call_target="tpu_custom_call" | custom-call | tf_op jit(solution)/shard_map/pallas_call | solution.py:623
  160.9 8.5 %all-to-all-start.6 = ((bf16[64,152,128]{2,1,0:T(8,128)(2,1)}), bf16[64,152,128]{2,1,0:T(8,128)(2,1)S(1)}, u32[]{:S(2)}, u32[]{:S(2)}) async-start(bf16[64,152,128]{2,1,0:T(8,128)(2,1)} %bitcast.8), calls=%async_computation.6 | async-start | bytes 4980736 | tf_op jit(solution)/shard_map/all_to_all | solution.py:759
  176.5 23.9 %collective-permute-done.22.rest_17_ = bf16[40,384]{1,0:T(8,128)(2,1)S(1)} collective-permute-done((bf16[40,384]{1,0:T(8,128)(2,1)S(1)}, bf16[40,384]{1,0:T(8,128)(2,1)S(1)}, u32[]{:S(2)}, u32[]{:S(2)}) %collective-permute-start.22) | collective-permute-done | bytes 30752 | tf_op jit(solution)/shard_map/ppermute | solution.py:750
  204.8 42.9 %all_to_all.42 = bf16[64,152,128]{2,1,0:T(8,128)(2,1)S(1)} all-to-all(bf16[64,152,128]{2,1,0:T(8,128)(2,1)S(1)} %chip_sum.1), channel_id=1, replica_groups=mesh['y'=4,'xh'=2,'core'=2,'xl'=2,'z'=4] {'y','xh','xl','z'}, dimensions={0} | all-to-all | bytes 4980736 | tf_op jit(solution)/shard_map/all_to_all | solution.py:759
  247.7 3.4 %collective-permute-start.29 = (bf16[9728,128]{1,0:T(8,128)(2,1)S(1)}, bf16[9728,128]{1,0:T(8,128)(2,1)S(1)}, u32[]{:S(2)}, u32[]{:S(2)}) collective-permute-start(bf16[9728,128]{1,0:T(8,128)(2,1)S(1)} %bitcast.13), channel_id=1, source_target_pairs={{0,8},{8,0},{1,9},{9,1},{2,10},{10,2},{3,11},{11,3},{4,12},{12,4},... | collective-permute-start | bytes 7471112 | tf_op jit(solution)/shard_map/ppermute | solution.py:619
  255.3 4.9 %collective-permute-start.8 = (bf16[24,384]{1,0:T(8,128)(2,1)S(1)}, bf16[24,384]{1,0:T(8,128)(2,1)S(1)}, u32[]{:S(2)}, u32[]{:S(2)}) collective-permute-start(bf16[24,384]{1,0:T(8,128)(2,1)S(1)} %copy-done.36), channel_id=1, source_target_pairs={{0,40},{8,48},{16,56},{24,64},{32,72},{40,80},{48,88},{56,96},{64,... | collective-permute-start | bytes 55304 | tf_op jit(solution)/shard_map/ppermute | solution.py:750
  260.9 2.6 collective-permute-start.11
  263.5 4.9 %collective-permute-start.12 = (bf16[24,384]{1,0:T(8,128)(2,1)S(1)}, bf16[24,384]{1,0:T(8,128)(2,1)S(1)}, u32[]{:S(2)}, u32[]{:S(2)}) collective-permute-start(bf16[24,384]{1,0:T(8,128)(2,1)S(1)} %copy-done.32), channel_id=1, source_target_pairs={{0,72},{8,80},{16,88},{24,96},{32,104},{40,112},{48,120},{56,0},{6... | collective-permute-start | bytes 55304 | tf_op jit(solution)/shard_map/ppermute | solution.py:750
  268.4 2.5 collective-permute-start.13
  273.0 3.7 %collective-permute-start.16 = (bf16[24,384]{1,0:T(8,128)(2,1)S(1)}, bf16[24,384]{1,0:T(8,128)(2,1)S(1)}, u32[]{:S(2)}, u32[]{:S(2)}) collective-permute-start(bf16[24,384]{1,0:T(8,128)(2,1)S(1)} %copy-done.28), channel_id=1, source_target_pairs={{0,104},{8,112},{16,120},{24,0},{32,8},{40,16},{48,24},{56,32},{64... | collective-permute-start | bytes 55304 | tf_op jit(solution)/shard_map/ppermute | solution.py:750
  276.7 3.4 %collective-permute-start.17 = (bf16[24,384]{1,0:T(8,128)(2,1)S(1)}, bf16[24,384]{1,0:T(8,128)(2,1)S(1)}, u32[]{:S(2)}, u32[]{:S(2)}) collective-permute-start(bf16[24,384]{1,0:T(8,128)(2,1)S(1)} %copy-done.27), channel_id=1, source_target_pairs={{0,112},{8,120},{16,0},{24,8},{32,16},{40,24},{48,32},{56,40},{64,... | collective-permute-start | bytes 55304 | tf_op jit(solution)/shard_map/ppermute | solution.py:750
  281.0 3.8 %collective-permute-done.18.rest_15_ = bf16[24,384]{1,0:T(8,128)(2,1)S(1)} collective-permute-done((bf16[24,384]{1,0:T(8,128)(2,1)S(1)}, bf16[24,384]{1,0:T(8,128)(2,1)S(1)}, u32[]{:S(2)}, u32[]{:S(2)}) %collective-permute-start.18) | collective-permute-done | bytes 18464 | tf_op jit(solution)/shard_map/ppermute | solution.py:750
  286.9 3.0 %unpack_own.1 = (f32[384,1152]{1,0:T(8,128)}, f32[384,384]{1,0:T(8,128)}, f32[384,1152]{1,0:T(8,128)}, f32[384,384]{1,0:T(8,128)}, f32[384,1536]{1,0:T(8,128)}, ...) custom-call(s32[3]{0:T(128)S(1)} %copy-done.7, ...), custom_call_target="tpu_custom_call" | custom-call | tf_op jit(solution)/shard_map/unpack_own/pallas_call | solution.py:720
  290.0 3.0 %unpack_other.1 = (f32[384,1152]{1,0:T(8,128)}, f32[384,384]{1,0:T(8,128)}, f32[384,1152]{1,0:T(8,128)}, f32[384,384]{1,0:T(8,128)}, f32[384,1536]{1,0:T(8,128)}...) custom-call(s32[3]{0:T(128)S(1)} %copy-done.7, ...), custom_call_target="tpu_custom_call", output_to_operand_aliasing={{0}: (2, {}), {1}: (3, {}), {2}: (4, {}), {3}: (5, {}), {4}... | custom-call | tf_op jit(solution)/shard_map/unpack_other/pallas_call | solution.py:720
  (138 shorter events, 37.3 us)
Async XLA Ops:
  16.0 17.8 %all-to-all-start.1 = ((bf16[16,24,384]{2,1,0:T(8,128)(2,1)}), bf16[16,24,384]{2,1,0:T(8,128)(2,1)S(1)}, u32[]{:S(2)}, u32[]{:S(2)}) async-start(bf16[16,24,384]{2,1,0:T(8,128)(2,1)} %get-tuple-element.95), calls=%async_computation.1 | async-start | bytes 589824 | tf_op jit(solution)/shard_map/all_to_all | solution.py:759
  33.8 9.4 %all-to-all-start.2 = ((bf16[8,40,384]{2,1,0:T(8,128)(2,1)}), bf16[8,40,384]{2,1,0:T(8,128)(2,1)S(1)}, u32[]{:S(2)}, u32[]{:S(2)}) async-start(bf16[8,40,384]{2,1,0:T(8,128)(2,1)} %get-tuple-element.98), calls=%async_computation.2 | async-start | bytes 491520 | tf_op jit(solution)/shard_map/all_to_all | solution.py:759
  43.2 14.5 %all-to-all-start.3 = ((bf16[16,24,384]{2,1,0:T(8,128)(2,1)}), bf16[16,24,384]{2,1,0:T(8,128)(2,1)S(1)}, u32[]{:S(2)}, u32[]{:S(2)}) async-start(bf16[16,24,384]{2,1,0:T(8,128)(2,1)} %get-tuple-element.99), calls=%async_computation.3 | async-start | bytes 589824 | tf_op jit(solution)/shard_map/all_to_all | solution.py:759
  48.7 8.6 %collective-permute-start.1 = (bf16[144,384]{1,0:T(8,128)(2,1)S(1)}, bf16[144,384]{1,0:T(8,128)(2,1)S(1)}, u32[]{:S(2)}, u32[]{:S(2)}) collective-permute-start(bf16[144,384]{1,0:T(8,128)(2,1)S(1)} %get-tuple-element.173), channel_id=1, source_target_pairs={{8,0},{16,8},{24,16},{32,24},{40,32},{48,40},{56,48},{64,56},{72,6... | collective-permute-start | bytes 331784 | tf_op jit(solution)/shard_map/ppermute | solution.py:770
  50.8 6.7 %collective-permute-start = (bf16[144,384]{1,0:T(8,128)(2,1)S(1)}, bf16[144,384]{1,0:T(8,128)(2,1)S(1)}, u32[]{:S(2)}, u32[]{:S(2)}) collective-permute-start(bf16[144,384]{1,0:T(8,128)(2,1)S(1)} %get-tuple-element.174), channel_id=1, source_target_pairs={{0,8},{8,16},{16,24},{24,32},{32,40},{40,48},{48,56},{56,64},{64,7... | collective-permute-start | bytes 331784 | tf_op jit(solution)/shard_map/ppermute | solution.py:769
  60.8 9.5 %collective-permute-start.3 = (bf16[288,384]{1,0:T(8,128)(2,1)}, bf16[288,384]{1,0:T(8,128)(2,1)S(1)}, u32[]{:S(2)}, u32[]{:S(2)}) collective-permute-start(bf16[288,384]{1,0:T(8,128)(2,1)} %middle.1.mid_ref), channel_id=1, source_target_pairs={{8,0},{16,8},{24,16},{32,24},{40,32},{48,40},{56,48},{64,56},{72,6... | collective-permute-start | bytes 663560 | tf_op jit(solution)/shard_map/ppermute | solution.py:774
  63.7 7.8 %collective-permute-start.2 = (bf16[288,384]{1,0:T(8,128)(2,1)}, bf16[288,384]{1,0:T(8,128)(2,1)S(1)}, u32[]{:S(2)}, u32[]{:S(2)}) collective-permute-start(bf16[288,384]{1,0:T(8,128)(2,1)} %middle.1.mid_ref), channel_id=1, source_target_pairs={{0,8},{8,16},{16,24},{24,32},{32,40},{40,48},{48,56},{56,64},{64,7... | collective-permute-start | bytes 663560 | tf_op jit(solution)/shard_map/ppermute | solution.py:773
  108.2 46.0 %collective-permute-start.19 = (bf16[2,4832,128]{2,1,0:T(8,128)(2,1)}, bf16[2,4832,128]{2,1,0:T(8,128)(2,1)}, u32[]{:S(2)}, u32[]{:S(2)}) collective-permute-start(bf16[2,4832,128]{2,1,0:T(8,128)(2,1)} %feed_grads.1.refs_0_), channel_id=1, source_target_pairs={{0,8},{8,0},{1,9},{9,1},{2,10},{10,2},{3,11},{11,3},{4,12},{12,4},... | collective-permute-start | bytes 7421960 | tf_op jit(solution)/shard_map/ppermute | solution.py:619
  117.8 22.5 %all-to-all-start.5 = ((bf16[16,24,384]{2,1,0:T(8,128)(2,1)}), bf16[16,24,384]{2,1,0:T(8,128)(2,1)S(1)}, u32[]{:S(2)}, u32[]{:S(2)}) async-start(bf16[16,24,384]{2,1,0:T(8,128)(2,1)} %get-tuple-element.108), calls=%async_computation.5 | async-start | bytes 589824 | tf_op jit(solution)/shard_map/all_to_all | solution.py:759
  140.2 11.4 %collective-permute-start.21 = (bf16[2,2336,128]{2,1,0:T(8,128)(2,1)}, bf16[2,2336,128]{2,1,0:T(8,128)(2,1)}, u32[]{:S(2)}, u32[]{:S(2)}) collective-permute-start(bf16[2,2336,128]{2,1,0:T(8,128)(2,1)} %get-tuple-element.135.refs_4_), channel_id=1, source_target_pairs={{0,8},{8,0},{1,9},{9,1},{2,10},{10,2},{3,11},{11,3},{4,12},{12,4},... | collective-permute-start | bytes 3588104 | tf_op jit(solution)/shard_map/ppermute | solution.py:619
  160.9 41.9 %all-to-all-start.6 = ((bf16[64,152,128]{2,1,0:T(8,128)(2,1)}), bf16[64,152,128]{2,1,0:T(8,128)(2,1)S(1)}, u32[]{:S(2)}, u32[]{:S(2)}) async-start(bf16[64,152,128]{2,1,0:T(8,128)(2,1)} %bitcast.8), calls=%async_computation.6 | async-start | bytes 4980736 | tf_op jit(solution)/shard_map/all_to_all | solution.py:759
  169.4 30.9 %collective-permute-start.22 = (bf16[40,384]{1,0:T(8,128)(2,1)S(1)}, bf16[40,384]{1,0:T(8,128)(2,1)S(1)}, u32[]{:S(2)}, u32[]{:S(2)}) collective-permute-start(bf16[40,384]{1,0:T(8,128)(2,1)S(1)} %copy-done.25), channel_id=1, source_target_pairs={{0,1},{1,2},{2,3},{3,4},{4,5},{5,6},{6,7},{7,0},{8,9},{9,10},{10,1... | collective-permute-start | bytes 92168 | tf_op jit(solution)/shard_map/ppermute | solution.py:750
  170.5 30.2 %collective-permute-start.23 = (bf16[40,384]{1,0:T(8,128)(2,1)S(1)}, bf16[40,384]{1,0:T(8,128)(2,1)S(1)}, u32[]{:S(2)}, u32[]{:S(2)}) collective-permute-start(bf16[40,384]{1,0:T(8,128)(2,1)S(1)} %copy-done.24), channel_id=1, source_target_pairs={{0,2},{1,3},{2,4},{3,5},{4,6},{5,7},{6,0},{7,1},{8,10},{9,11},{10,... | collective-permute-start | bytes 92168 | tf_op jit(solution)/shard_map/ppermute | solution.py:750
  172.9 30.6 %collective-permute-start.24 = (bf16[40,384]{1,0:T(8,128)(2,1)S(1)}, bf16[40,384]{1,0:T(8,128)(2,1)S(1)}, u32[]{:S(2)}, u32[]{:S(2)}) collective-permute-start(bf16[40,384]{1,0:T(8,128)(2,1)S(1)} %copy-done.23), channel_id=1, source_target_pairs={{0,3},{1,4},{2,5},{3,6},{4,7},{5,0},{6,1},{7,2},{8,11},{9,12},{10,... | collective-permute-start | bytes 92168 | tf_op jit(solution)/shard_map/ppermute | solution.py:750
  175.0 28.5 %collective-permute-start.25 = (bf16[40,384]{1,0:T(8,128)(2,1)S(1)}, bf16[40,384]{1,0:T(8,128)(2,1)S(1)}, u32[]{:S(2)}, u32[]{:S(2)}) collective-permute-start(bf16[40,384]{1,0:T(8,128)(2,1)S(1)} %copy-done.22), channel_id=1, source_target_pairs={{0,4},{1,5},{2,6},{3,7},{4,0},{5,1},{6,2},{7,3},{8,12},{9,13},{10,... | collective-permute-start | bytes 92168 | tf_op jit(solution)/shard_map/ppermute | solution.py:750
  175.3 28.3 %collective-permute-start.26 = (bf16[40,384]{1,0:T(8,128)(2,1)S(1)}, bf16[40,384]{1,0:T(8,128)(2,1)S(1)}, u32[]{:S(2)}, u32[]{:S(2)}) collective-permute-start(bf16[40,384]{1,0:T(8,128)(2,1)S(1)} %copy-done.21), channel_id=1, source_target_pairs={{0,5},{1,6},{2,7},{3,0},{4,1},{5,2},{6,3},{7,4},{8,13},{9,14},{10,... | collective-permute-start | bytes 92168 | tf_op jit(solution)/shard_map/ppermute | solution.py:750
  200.4 4.2 %collective-permute-start.27 = (bf16[40,384]{1,0:T(8,128)(2,1)S(1)}, bf16[40,384]{1,0:T(8,128)(2,1)S(1)}, u32[]{:S(2)}, u32[]{:S(2)}) collective-permute-start(bf16[40,384]{1,0:T(8,128)(2,1)S(1)} %copy-done.20), channel_id=1, source_target_pairs={{0,6},{1,7},{2,0},{3,1},{4,2},{5,3},{6,4},{7,5},{8,14},{9,15},{10,... | collective-permute-start | bytes 92168 | tf_op jit(solution)/shard_map/ppermute | solution.py:750
  247.7 42.3 %collective-permute-start.29 = (bf16[9728,128]{1,0:T(8,128)(2,1)S(1)}, bf16[9728,128]{1,0:T(8,128)(2,1)S(1)}, u32[]{:S(2)}, u32[]{:S(2)}) collective-permute-start(bf16[9728,128]{1,0:T(8,128)(2,1)S(1)} %bitcast.13), channel_id=1, source_target_pairs={{0,8},{8,0},{1,9},{9,1},{2,10},{10,2},{3,11},{11,3},{4,12},{12,4},... | collective-permute-start | bytes 7471112 | tf_op jit(solution)/shard_map/ppermute | solution.py:619
  251.3 8.8 %collective-permute-start.5 = (bf16[24,384]{1,0:T(8,128)(2,1)S(1)}, bf16[24,384]{1,0:T(8,128)(2,1)S(1)}, u32[]{:S(2)}, u32[]{:S(2)}) collective-permute-start(bf16[24,384]{1,0:T(8,128)(2,1)S(1)} %copy-done.39), channel_id=1, source_target_pairs={{0,16},{8,24},{16,32},{24,40},{32,48},{40,56},{48,64},{56,72},{64,... | collective-permute-start | bytes 55304 | tf_op jit(solution)/shard_map/ppermute | solution.py:750
  253.6 7.0 %collective-permute-start.6 = (bf16[24,384]{1,0:T(8,128)(2,1)S(1)}, bf16[24,384]{1,0:T(8,128)(2,1)S(1)}, u32[]{:S(2)}, u32[]{:S(2)}) collective-permute-start(bf16[24,384]{1,0:T(8,128)(2,1)S(1)} %copy-done.38), channel_id=1, source_target_pairs={{0,24},{8,32},{16,40},{24,48},{32,56},{40,64},{48,72},{56,80},{64,... | collective-permute-start | bytes 55304 | tf_op jit(solution)/shard_map/ppermute | solution.py:750
  253.6 7.3 %collective-permute-start.7 = (bf16[24,384]{1,0:T(8,128)(2,1)S(1)}, bf16[24,384]{1,0:T(8,128)(2,1)S(1)}, u32[]{:S(2)}, u32[]{:S(2)}) collective-permute-start(bf16[24,384]{1,0:T(8,128)(2,1)S(1)} %copy-done.37), channel_id=1, source_target_pairs={{0,32},{8,40},{16,48},{24,56},{32,64},{40,72},{48,80},{56,88},{64,... | collective-permute-start | bytes 55304 | tf_op jit(solution)/shard_map/ppermute | solution.py:750
  255.3 8.2 %collective-permute-start.8 = (bf16[24,384]{1,0:T(8,128)(2,1)S(1)}, bf16[24,384]{1,0:T(8,128)(2,1)S(1)}, u32[]{:S(2)}, u32[]{:S(2)}) collective-permute-start(bf16[24,384]{1,0:T(8,128)(2,1)S(1)} %copy-done.36), channel_id=1, source_target_pairs={{0,40},{8,48},{16,56},{24,64},{32,72},{40,80},{48,88},{56,96},{64,... | collective-permute-start | bytes 55304 | tf_op jit(solution)/shard_map/ppermute | solution.py:750
  260.1 8.3 %collective-permute-start.9 = (bf16[24,384]{1,0:T(8,128)(2,1)S(1)}, bf16[24,384]{1,0:T(8,128)(2,1)S(1)}, u32[]{:S(2)}, u32[]{:S(2)}) collective-permute-start(bf16[24,384]{1,0:T(8,128)(2,1)S(1)} %copy-done.35), channel_id=1, source_target_pairs={{0,48},{8,56},{16,64},{24,72},{32,80},{40,88},{48,96},{56,104},{64... | collective-permute-start | bytes 55304 | tf_op jit(solution)/shard_map/ppermute | solution.py:750
  260.6 10.3 %collective-permute-start.10 = (bf16[24,384]{1,0:T(8,128)(2,1)S(1)}, bf16[24,384]{1,0:T(8,128)(2,1)S(1)}, u32[]{:S(2)}, u32[]{:S(2)}) collective-permute-start(bf16[24,384]{1,0:T(8,128)(2,1)S(1)} %copy-done.34), channel_id=1, source_target_pairs={{0,56},{8,64},{16,72},{24,80},{32,88},{40,96},{48,104},{56,112},{6... | collective-permute-start | bytes 55304 | tf_op jit(solution)/shard_map/ppermute | solution.py:750
  260.9 10.6 %collective-permute-start.11 = (bf16[24,384]{1,0:T(8,128)(2,1)S(1)}, bf16[24,384]{1,0:T(8,128)(2,1)S(1)}, u32[]{:S(2)}, u32[]{:S(2)}) collective-permute-start(bf16[24,384]{1,0:T(8,128)(2,1)S(1)} %copy-done.33), channel_id=1, source_target_pairs={{0,64},{8,72},{16,80},{24,88},{32,96},{40,104},{48,112},{56,120},{... | collective-permute-start | bytes 55304 | tf_op jit(solution)/shard_map/ppermute | solution.py:750
  263.5 9.5 %collective-permute-start.12 = (bf16[24,384]{1,0:T(8,128)(2,1)S(1)}, bf16[24,384]{1,0:T(8,128)(2,1)S(1)}, u32[]{:S(2)}, u32[]{:S(2)}) collective-permute-start(bf16[24,384]{1,0:T(8,128)(2,1)S(1)} %copy-done.32), channel_id=1, source_target_pairs={{0,72},{8,80},{16,88},{24,96},{32,104},{40,112},{48,120},{56,0},{6... | collective-permute-start | bytes 55304 | tf_op jit(solution)/shard_map/ppermute | solution.py:750
  268.4 8.3 %collective-permute-start.13 = (bf16[24,384]{1,0:T(8,128)(2,1)S(1)}, bf16[24,384]{1,0:T(8,128)(2,1)S(1)}, u32[]{:S(2)}, u32[]{:S(2)}) collective-permute-start(bf16[24,384]{1,0:T(8,128)(2,1)S(1)} %copy-done.31), channel_id=1, source_target_pairs={{0,80},{8,88},{16,96},{24,104},{32,112},{40,120},{48,0},{56,8},{64... | collective-permute-start | bytes 55304 | tf_op jit(solution)/shard_map/ppermute | solution.py:750
  270.9 9.1 %collective-permute-start.14 = (bf16[24,384]{1,0:T(8,128)(2,1)S(1)}, bf16[24,384]{1,0:T(8,128)(2,1)S(1)}, u32[]{:S(2)}, u32[]{:S(2)}) collective-permute-start(bf16[24,384]{1,0:T(8,128)(2,1)S(1)} %copy-done.30), channel_id=1, source_target_pairs={{0,88},{8,96},{16,104},{24,112},{32,120},{40,0},{48,8},{56,16},{64... | collective-permute-start | bytes 55304 | tf_op jit(solution)/shard_map/ppermute | solution.py:750
  271.5 8.6 %collective-permute-start.15 = (bf16[24,384]{1,0:T(8,128)(2,1)S(1)}, bf16[24,384]{1,0:T(8,128)(2,1)S(1)}, u32[]{:S(2)}, u32[]{:S(2)}) collective-permute-start(bf16[24,384]{1,0:T(8,128)(2,1)S(1)} %copy-done.29), channel_id=1, source_target_pairs={{0,96},{8,104},{16,112},{24,120},{32,0},{40,8},{48,16},{56,24},{64... | collective-permute-start | bytes 55304 | tf_op jit(solution)/shard_map/ppermute | solution.py:750
  273.0 7.1 %collective-permute-start.16 = (bf16[24,384]{1,0:T(8,128)(2,1)S(1)}, bf16[24,384]{1,0:T(8,128)(2,1)S(1)}, u32[]{:S(2)}, u32[]{:S(2)}) collective-permute-start(bf16[24,384]{1,0:T(8,128)(2,1)S(1)} %copy-done.28), channel_id=1, source_target_pairs={{0,104},{8,112},{16,120},{24,0},{32,8},{40,16},{48,24},{56,32},{64... | collective-permute-start | bytes 55304 | tf_op jit(solution)/shard_map/ppermute | solution.py:750
  276.7 4.3 %collective-permute-start.17 = (bf16[24,384]{1,0:T(8,128)(2,1)S(1)}, bf16[24,384]{1,0:T(8,128)(2,1)S(1)}, u32[]{:S(2)}, u32[]{:S(2)}) collective-permute-start(bf16[24,384]{1,0:T(8,128)(2,1)S(1)} %copy-done.27), channel_id=1, source_target_pairs={{0,112},{8,120},{16,0},{24,8},{32,16},{40,24},{48,32},{56,40},{64,... | collective-permute-start | bytes 55304 | tf_op jit(solution)/shard_map/ppermute | solution.py:750
  280.1 4.7 %collective-permute-start.18 = (bf16[24,384]{1,0:T(8,128)(2,1)S(1)}, bf16[24,384]{1,0:T(8,128)(2,1)S(1)}, u32[]{:S(2)}, u32[]{:S(2)}) collective-permute-start(bf16[24,384]{1,0:T(8,128)(2,1)S(1)} %copy-done.26), channel_id=1, source_target_pairs={{0,120},{8,0},{16,8},{24,16},{32,24},{40,32},{48,40},{56,48},{64,5... | collective-permute-start | bytes 55304 | tf_op jit(solution)/shard_map/ppermute | solution.py:750
  (44 other events, 1573.6 us)
